TPU v7x, 256 devices: a whole 4x4x8 slice. The times are simulated.
256 devices in a mesh: blk: 128 (over z, y, x_hi, core), help: 2 (over x_lo).
Axes of the slice: x: 4 (x_hi: 2, x_lo: 2; x = x_hi * 2 + x_lo), y: 4, z: 8, core: 2. Of those that a mesh axis runs over, the one named last changes fastest.
Arguments:
- heads: float32 [32768, 400], P(('blk', 'help')), may hold values from -6 to 6
- tails: float32 [32768, 400], P(('blk', 'help')), may hold values from -6 to 6
- head_acc: float32 [32768], P(('blk', 'help')), may hold values from 0.01 to 0.1
- tail_acc: float32 [32768], P(('blk', 'help')), may hold values from 0.01 to 0.1
- relations: bfloat16 [7424, 400], replicated, may hold values from -0.59765625 to 0.59765625
- counts: int32 [4, 256], P(None, ('blk', 'help')), may hold values from 1 to 5, as said below
- rel_ids: int32 [4, 256, 5], P(None, ('blk', 'help')), may hold values from 0 to 7423
- head_edges: int32 [4, 256, 5, 1024], P(None, ('blk', 'help')), may hold values from 0 to 127
- tail_edges: int32 [4, 256, 5, 1024], P(None, ('blk', 'help')), may hold values from 0 to 127
Outputs:
- new_heads: float32 [32768, 400], P(('blk', 'help'))
- new_tails: float32 [32768, 400], P(('blk', 'help'))
- new_head_acc: float32 [32768], P(('blk', 'help'))
- new_tail_acc: float32 [32768], P(('blk', 'help'))
Inputs may be any that keep to these rules, and one draw needn't show every extreme that they name: `counts`: in every round the two partitions 2 q and 2 q + 1 have one count from 3 to 5 and the other 1 or 2; in every round partitions 0 and 1 hold 5 and 1.
All inputs are finite; a program needn't handle non-finite values.
Results may differ from a plain program's by a relative error of at most 0.0003.
Values sent between devices are 32-bit elements; how exact they have to be, the bound alone decides.
No kernel may reach another device: no remote copies, remote signals or barrier semaphores. Data moves between devices by JAX's collectives and lax.ppermute only.
A program may use at most 64 MiB of HBM per device.

v0:
```python
import jax
import jax.numpy as jnp
from jax import lax
from jax.sharding import PartitionSpec as P

NEG_WEIGHT = 0.0625
LEARN_RATE = 0.1
HIGH = lax.Precision.HIGHEST


def shifted(block, axis, distance):
    devices = range(lax.axis_size(axis))
    route = [((i - distance) % len(devices), i) for i in devices]
    return lax.ppermute(block, axis, route)


def one_hot_rows(index, row_count):
    columns = lax.broadcasted_iota(jnp.int32, (index.shape[0], row_count), 1)
    return (index[:, None] == columns).astype(jnp.bfloat16)


def task_grads(head_block, tail_block, rel_vec, head_index, tail_index):
    row_count = head_block.shape[0]
    scaled = head_block * rel_vec[None, :]
    scores = lax.dot_general(
        scaled,
        tail_block,
        (((1,), (1,)), ((), ())),
        precision=HIGH,
        preferred_element_type=jnp.float32,
    )
    head_hot = one_hot_rows(head_index, row_count)
    tail_hot = one_hot_rows(tail_index, row_count)
    labels = lax.dot_general(
        head_hot, tail_hot, (((0,), (0,)), ((), ())), preferred_element_type=jnp.float32
    )
    coefficient = NEG_WEIGHT * jax.nn.sigmoid(scores) - labels
    head_grad = (
        jnp.dot(coefficient, tail_block, precision=HIGH, preferred_element_type=jnp.float32)
        * rel_vec[None, :]
    )
    tail_grad = lax.dot_general(
        coefficient,
        scaled,
        (((0,), (0,)), ((), ())),
        precision=HIGH,
        preferred_element_type=jnp.float32,
    )
    return (head_grad, tail_grad)


def adagrad(block, state, grad):
    new_state = state + jnp.mean(grad * grad, axis=1)
    return (block - LEARN_RATE * grad / jnp.sqrt(new_state)[:, None], new_state)


def own_grads(head_block, tail_block, relations, counts, rel_ids, head_edges, tail_edges, round_ix):
    rel_row = rel_ids[round_ix, 0]
    head_rows = head_edges[round_ix, 0]
    tail_rows = tail_edges[round_ix, 0]

    def add_task(slot_id, totals):
        rel_vec = relations[rel_row[slot_id]].astype(jnp.float32)
        head_grad, tail_grad = task_grads(
            head_block, tail_block, rel_vec, head_rows[slot_id], tail_rows[slot_id]
        )
        return (totals[0] + head_grad, totals[1] + tail_grad)

    empty = jnp.zeros(head_block.shape, jnp.float32)
    return lax.fori_loop(jnp.int32(0), counts[round_ix, 0], add_task, (empty, empty))


def on_device(heads, tails, head_acc, tail_acc, relations, counts, rel_ids, head_edges, tail_edges):
    rounds_total = counts.shape[0]
    head_block, tail_block, head_state, tail_state = (heads, tails, head_acc, tail_acc)
    for round_ix in range(rounds_total):
        if round_ix > 0:
            tail_block, tail_state = shifted((tail_block, tail_state), "blk", 1)
        head_grad, tail_grad = own_grads(
            head_block, tail_block, relations, counts, rel_ids, head_edges, tail_edges, round_ix
        )
        head_block, head_state = adagrad(head_block, head_state, head_grad)
        tail_block, tail_state = adagrad(tail_block, tail_state, tail_grad)
    tail_block, tail_state = shifted((tail_block, tail_state), "blk", 1 - rounds_total)
    return (head_block, tail_block, head_state, tail_state)


def solution(mesh):
    in_specs = (
        P(("blk", "help"), None),
        P(("blk", "help"), None),
        P(("blk", "help")),
        P(("blk", "help")),
        P(),
        P(None, ("blk", "help")),
        P(None, ("blk", "help"), None),
        P(None, ("blk", "help"), None, None),
        P(None, ("blk", "help"), None, None),
    )
    out_specs = (
        P(("blk", "help"), None),
        P(("blk", "help"), None),
        P(("blk", "help")),
        P(("blk", "help")),
    )
    return jax.shard_map(
        on_device, mesh=mesh, in_specs=in_specs, out_specs=out_specs, check_vma=False
    )
```

profile of v0, /device:TPU:0, one launch (start us, length us, event | category | flops | bytes accessed | tf_op | source)
XLA Modules:
  0.0 181.2 jit_solution(17453812366036144639)
XLA Ops:
  0.7 0.8 fusion.52
  1.5 0.8 fusion.53
  2.3 9.6 %copy.26 = bf16[7424,400]{1,0:T(8,128)(2,1)} copy(bf16[7424,400]{0,1:T(8,128)(2,1)} %param.21) | data formatting | bytes 11878400 | tf_op jit(solution)/shard_map/while | solution.py:70
  12.6 30.3 %while.48 = (s32[]{:T(128)}, f32[128,400]{0,1:T(8,128)S(1)}, f32[128,400]{0,1:T(8,128)S(1)}, s32[]{:T(128)}, s32[5]{0:T(128)S(1)}, /*index=5*/bf16[7424,400]{1,0...) while((s32[]{:T(128)}, f32[128,400]{0,1:T(8,128)S(1)}, ...), condition=%wide.region_1.0_spmd, body=%wide.region_0.0_spmd.sunk | while | flops 270084512 | bytes 1998077 | solution.py:70
  16.3 0.7 fusion.109
  22.2 0.7 fusion.109
  28.2 0.7 fusion.109
  34.1 0.7 fusion.109
  40.0 0.7 fusion.109
  43.4 10.6 %collective-permute-done = f32[128,400]{0,1:T(8,128)S(1)} collective-permute-done((f32[128,400]{0,1:T(8,128)S(1)}, f32[128,400]{0,1:T(8,128)S(1)}, u32[]{:S(2)}, u32[]{:S(2)}) %collective-permute-start) | collective-permute-done | bytes 204832 | tf_op jit(solution)/shard_map/ppermute | solution.py:14
  54.2 31.7 %while.49 = (s32[]{:T(128)}, f32[128,400]{0,1:T(8,128)S(1)}, f32[128,400]{0,1:T(8,128)S(1)}, s32[]{:T(128)}, s32[5]{0:T(128)S(1)}, /*index=5*/bf16[7424,400]{1,0...) while((s32[]{:T(128)}, f32[128,400]{0,1:T(8,128)S(1)}, ...), condition=%wide.region_5.0_spmd, body=%wide.region_4.0_spmd.sunk | while | flops 270084512 | bytes 1998077 | solution.py:70
  58.0 0.7 fusion.117
  64.2 0.7 fusion.117
  70.5 0.7 fusion.117
  76.7 0.7 fusion.117
  82.9 0.7 fusion.117
  86.4 10.7 %collective-permute-done.2 = f32[128,400]{0,1:T(8,128)S(1)} collective-permute-done((f32[128,400]{0,1:T(8,128)S(1)}, f32[128,400]{0,1:T(8,128)S(1)}, u32[]{:S(2)}, u32[]{:S(2)}) %collective-permute-start.2) | collective-permute-done | bytes 204832 | tf_op jit(solution)/shard_map/ppermute | solution.py:14
  97.3 32.2 %while.50 = (s32[]{:T(128)}, f32[128,400]{0,1:T(8,128)S(1)}, f32[128,400]{0,1:T(8,128)S(1)}, s32[]{:T(128)}, s32[5]{0:T(128)S(1)}, /*index=5*/bf16[7424,400]{1,0...) while((s32[]{:T(128)}, f32[128,400]{0,1:T(8,128)S(1)}, ...), condition=%wide.region_9.0_spmd, body=%wide.region_8.0_spmd.sunk | while | flops 270084512 | bytes 1998077 | solution.py:70
  101.2 0.7 fusion.125
  107.5 0.7 fusion.125
  120.1 0.7 fusion.125
  130.1 10.5 %collective-permute-done.4 = f32[128,400]{0,1:T(8,128)S(1)} collective-permute-done((f32[128,400]{0,1:T(8,128)S(1)}, f32[128,400]{0,1:T(8,128)S(1)}, u32[]{:S(2)}, u32[]{:S(2)}) %collective-permute-start.4) | collective-permute-done | bytes 204832 | tf_op jit(solution)/shard_map/ppermute | solution.py:14
  140.8 32.2 %while.51 = (s32[]{:T(128)}, f32[128,400]{0,1:T(8,128)S(1)}, f32[128,400]{0,1:T(8,128)S(1)}, s32[]{:T(128)}, s32[5]{0:T(128)S(1)}, /*index=5*/bf16[7424,400]{1,0...) while((s32[]{:T(128)}, f32[128,400]{0,1:T(8,128)S(1)}, ...), condition=%wide.region_13.0_spmd, body=%wide.region_12.0_spmd.sunk | while | flops 270084512 | bytes 1998077 | solution.py:70
  174.6 5.4 %collective-permute-done.7 = f32[128]{0:T(128)S(1)} collective-permute-done((f32[128]{0:T(128)S(1)}, f32[128]{0:T(128)S(1)}, u32[]{:S(2)}, u32[]{:S(2)}) %collective-permute-start.7) | collective-permute-done | bytes 544 | tf_op jit(solution)/shard_map/ppermute | solution.py:14
  (194 shorter events, 68.6 us)
Async XLA Ops:
  0.6 11.2 %copy-start.2 = (s32[4,1]{0,1:T(1,128)S(1)}, s32[4,1]{0,1:T(1,128)}, u32[]{:S(2)}) copy-start(s32[4,1]{0,1:T(1,128)} %param.22) | copy-start | bytes 52
  0.6 11.8 %copy-start.3 = (s32[4,1,5]{2,1,0:T(1,128)S(1)}, s32[4,1,5]{2,1,0:T(1,128)}, u32[]{:S(2)}) copy-start(s32[4,1,5]{2,1,0:T(1,128)} %param.23) | copy-start | bytes 244
  0.7 11.9 %copy-start.1 = (f32[128,400]{0,1:T(8,128)S(1)}, f32[128,400]{0,1:T(8,128)}, u32[]{:S(2)}) copy-start(f32[128,400]{0,1:T(8,128)} %param.17) | copy-start | bytes 614404
  0.7 11.9 %copy-start = (f32[128,400]{0,1:T(8,128)S(1)}, f32[128,400]{0,1:T(8,128)}, u32[]{:S(2)}) copy-start(f32[128,400]{0,1:T(8,128)} %param.18) | copy-start | bytes 614404
  11.9 31.1 %copy-start.5 = (f32[128]{0:T(128)S(1)}, f32[128]{0:T(128)}, u32[]{:S(2)}) copy-start(f32[128]{0:T(128)} %param.20) | copy-start | bytes 1540
  11.9 31.4 %copy-start.4 = (f32[128]{0:T(128)S(1)}, f32[128]{0:T(128)}, u32[]{:S(2)}) copy-start(f32[128]{0:T(128)} %param.19) | copy-start | bytes 1540
  43.0 11.0 %collective-permute-start = (f32[128,400]{0,1:T(8,128)S(1)}, f32[128,400]{0,1:T(8,128)S(1)}, u32[]{:S(2)}, u32[]{:S(2)}) collective-permute-start(f32[128,400]{0,1:T(8,128)S(1)} %divide_subtract_fusion.6), channel_id=1, source_target_pairs={{254,0},{0,2},{2,4},{4,6},{6,8},{8,10},{10,12},{12,14},{14,16},{16... | collective-permute-start | bytes 614408 | tf_op jit(solution)/shard_map/ppermute | solution.py:14
  43.1 42.9 %collective-permute-start.1 = (f32[128]{0:T(128)S(1)}, f32[128]{0:T(128)S(1)}, u32[]{:S(2)}, u32[]{:S(2)}) collective-permute-start(f32[128]{0:T(128)S(1)} %get-tuple-element.389), channel_id=1, source_target_pairs={{254,0},{0,2},{2,4},{4,6},{6,8},{8,10},{10,12},{12,14},{14,16},{16... | collective-permute-start | bytes 1544 | tf_op jit(solution)/shard_map/ppermute | solution.py:14
  86.1 11.0 %collective-permute-start.2 = (f32[128,400]{0,1:T(8,128)S(1)}, f32[128,400]{0,1:T(8,128)S(1)}, u32[]{:S(2)}, u32[]{:S(2)}) collective-permute-start(f32[128,400]{0,1:T(8,128)S(1)} %divide_subtract_fusion.4), channel_id=1, source_target_pairs={{254,0},{0,2},{2,4},{4,6},{6,8},{8,10},{10,12},{12,14},{14,16},{16... | collective-permute-start | bytes 614408 | tf_op jit(solution)/shard_map/ppermute | solution.py:14
  86.3 43.3 %collective-permute-start.3 = (f32[128]{0:T(128)S(1)}, f32[128]{0:T(128)S(1)}, u32[]{:S(2)}, u32[]{:S(2)}) collective-permute-start(f32[128]{0:T(128)S(1)} %get-tuple-element.385), channel_id=1, source_target_pairs={{254,0},{0,2},{2,4},{4,6},{6,8},{8,10},{10,12},{12,14},{14,16},{16... | collective-permute-start | bytes 1544 | tf_op jit(solution)/shard_map/ppermute | solution.py:14
  129.6 11.0 %collective-permute-start.4 = (f32[128,400]{0,1:T(8,128)S(1)}, f32[128,400]{0,1:T(8,128)S(1)}, u32[]{:S(2)}, u32[]{:S(2)}) collective-permute-start(f32[128,400]{0,1:T(8,128)S(1)} %divide_subtract_fusion.2), channel_id=1, source_target_pairs={{254,0},{0,2},{2,4},{4,6},{6,8},{8,10},{10,12},{12,14},{14,16},{16... | collective-permute-start | bytes 614408 | tf_op jit(solution)/shard_map/ppermute | solution.py:14
  129.8 43.3 %collective-permute-start.5 = (f32[128]{0:T(128)S(1)}, f32[128]{0:T(128)S(1)}, u32[]{:S(2)}, u32[]{:S(2)}) collective-permute-start(f32[128]{0:T(128)S(1)} %get-tuple-element.383), channel_id=1, source_target_pairs={{254,0},{0,2},{2,4},{4,6},{6,8},{8,10},{10,12},{12,14},{14,16},{16... | collective-permute-start | bytes 1544 | tf_op jit(solution)/shard_map/ppermute | solution.py:14
  173.1 6.9 %collective-permute-start.6 = (f32[128,400]{0,1:T(8,128)S(1)}, f32[128,400]{0,1:T(8,128)S(1)}, u32[]{:S(2)}, u32[]{:S(2)}) collective-permute-start(f32[128,400]{0,1:T(8,128)S(1)} %divide_subtract_fusion), channel_id=1, source_target_pairs={{6,0},{8,2},{10,4},{12,6},{14,8},{16,10},{18,12},{20,14},{22,16},{... | collective-permute-start | bytes 614408 | tf_op jit(solution)/shard_map/ppermute | solution.py:14
  173.2 6.8 %collective-permute-start.7 = (f32[128]{0:T(128)S(1)}, f32[128]{0:T(128)S(1)}, u32[]{:S(2)}, u32[]{:S(2)}) collective-permute-start(f32[128]{0:T(128)S(1)} %get-tuple-element.379), channel_id=1, source_target_pairs={{6,0},{8,2},{10,4},{12,6},{14,8},{16,10},{18,12},{20,14},{22,16},{... | collective-permute-start | bytes 1544 | tf_op jit(solution)/shard_map/ppermute | solution.py:14
where the time goes:
time: 183 us; the launch traced here: 181 us
  loops' own time  53.8 us (29%)
  matrix products  46.4 us (25%)
  waiting for transfers between devices  37.2 us (20%)
  local copies, waits for them, and re-layouts  25.8 us (14%)
  other arithmetic  16.2 us (9%)
    another operation x4, loops' own time, own_grads(): lax.fori_loop(jnp.int32(0), counts[round_ix, 0], add_task, (empty, empty))  53.8 us
    ppermute x8, waiting for transfers between devices, shifted(): return lax.ppermute(block, axis, route)  37.2 us
    dot_general x20, matrix products, task_grads(): lax.dot_general(scaled, tail_block, (((1,), (1,)), ((), ())), precision=H...  14.4 us
    mul x20, other arithmetic, task_grads(): scaled = head_block * rel_vec[None, :]  14.1 us
    dot_general x20, matrix products, task_grads(): lax.dot_general(head_hot, tail_hot, (((0,), (0,)), ((), ())), preferred_e...  12.2 us
    dynamic_slice x20, local copies, waits for them, and re-layouts, add_task(): rel_vec = relations[rel_row[slot_id]].astype(jnp.float32)  11.9 us
    dot_general x20, matrix products, task_grads(): jnp.dot(coefficient, tail_block, precision=HIGH, preferred_element_type=j...  11 us
    while x4, local copies, waits for them, and re-layouts, own_grads(): lax.fori_loop(jnp.int32(0), counts[round_ix, 0], add_task, (empty, empty))  9.96 us
  transfers between devices with their start and end apart: 8, of which 4 were waited for; matrix products, arithmetic and copies ran while one was open for 32% of the time, Pallas kernels for 0%

commit v1 on v0

v1 whole, which is shorter than its diff:
```python
import jax
import jax.numpy as jnp
from jax import lax
from jax.experimental import pallas as pl
from jax.experimental.pallas import tpu as pltpu
from jax.sharding import PartitionSpec as P

NEG_WEIGHT = 0.0625
LEARN_RATE = 0.1
F32, BF16 = jnp.float32, jnp.bfloat16
LANES = 128
VMEM = pl.BlockSpec(memory_space=pltpu.VMEM)
SMEM = pl.BlockSpec(memory_space=pltpu.SMEM)
ANY = pl.BlockSpec(memory_space=pl.ANY)


def dot(a, b, dims):
    return lax.dot_general(a, b, (dims, ((), ())), preferred_element_type=F32)


NN, NT, TN = ((1,), (0,)), ((1,), (1,)), ((0,), (0,))


def hi_lo(x):
    hi = x.astype(BF16)
    return hi, (x - hi.astype(F32)).astype(BF16)


def one_hot(rows):
    which = lax.broadcasted_iota(jnp.int32, (LANES, LANES), 0)
    parts = [jnp.where(rows[r : r + 1, :] == which, 1.0, 0.0).astype(BF16) for r in range(8)]
    return jnp.concatenate(parts, axis=1)


def labels(labels_ref, he_ref, te_ref, first, tasks):
    for s in range(tasks):
        labels_ref[s] = dot(one_hot(te_ref[first + s]), one_hot(he_ref[first + s]), NT)


def fetch(rel_ids, rel_ref, rel_buf, sem, first, s):
    start = pl.multiple_of((rel_ids[first + s] // LANES) * LANES, LANES)
    return pltpu.make_async_copy(rel_ref.at[:, pl.ds(start, LANES)], rel_buf.at[s], sem.at[s])


def rel_columns(rel_ids, rel_buf, first, s):
    lane = lax.rem(rel_ids[first + s], LANES)
    pick = (lax.broadcasted_iota(jnp.int32, (LANES, LANES), 0) == lane).astype(F32).astype(BF16)
    return dot(rel_buf[s], pick, NN)


def scale_heads(heads, rel_ids, rel_buf, rel_out, shi, slo, first, tasks):
    for s in range(tasks):
        cols = pl.ds(s * LANES, LANES)
        rel = rel_columns(rel_ids, rel_buf, first, s)
        rel_out[:, cols] = rel.astype(BF16)
        hi, lo = hi_lo(heads * rel)
        shi[:, cols] = hi
        slo[:, cols] = lo


def adagrad(block, state, grad):
    width = block.shape[0]
    state = state + jnp.sum(grad * grad, axis=0, keepdims=True) * (1.0 / width)
    return block - grad * (LEARN_RATE / jnp.sqrt(state)), state


def tail_step(count, tail, state, shi_ref, slo_ref, labels_ref, chi_ref, clo_ref, tasks):
    thi, tlo = hi_lo(tail)
    shi, slo = shi_ref[...], slo_ref[...]
    scores = dot(thi, shi, TN) + dot(tlo, shi, TN) + dot(thi, slo, TN)
    for s in range(tasks):
        cols = pl.ds(s * LANES, LANES)
        score = scores[:, s * LANES : (s + 1) * LANES]
        coefficient = NEG_WEIGHT * (0.5 * jnp.tanh(0.5 * score) + 0.5) - labels_ref[s]
        chi, clo = hi_lo(jnp.where(s < count, coefficient, 0.0))
        chi_ref[:, cols] = chi
        clo_ref[:, cols] = clo
    chi, clo = chi_ref[...], clo_ref[...]
    grad = dot(shi, chi, NT) + dot(slo, chi, NT) + dot(shi, clo, NT)
    return adagrad(tail, state, grad)


def head_step(head, state, tail, rel_ref, chi_ref, clo_ref, tasks):
    thi, tlo = hi_lo(tail)
    grad = None
    for s in range(tasks):
        cols = pl.ds(s * LANES, LANES)
        chi, clo = chi_ref[:, cols], clo_ref[:, cols]
        term = dot(thi, chi, NN) + dot(tlo, chi, NN) + dot(thi, clo, NN)
        term = term * rel_ref[:, cols].astype(F32)
        grad = term if grad is None else grad + term
    return adagrad(head, state, grad)


def put_tail(out_ref, tail, state, width):
    out_ref[pl.ds(0, width), :] = tail
    out_ref[pl.ds(width, 8), :] = jnp.broadcast_to(state, (8, LANES))


def first_kernel(tasks, width):
    def body(counts, rel_ids, head_hbm, tail_hbm, tacc, rel_ref, he_hbm, te_hbm,
             tail_out, chi_ref, clo_ref, rel_out,
             head, tail, he, te, shi, slo, labels_ref, rel_buf, rel_sem, sem):
        edges = [pltpu.make_async_copy(src.at[pl.ds(0, tasks)], dst, sem.at[i])
                 for i, (src, dst) in enumerate(((he_hbm, he), (te_hbm, te)))]
        blocks = [pltpu.make_async_copy(src, dst, sem.at[2 + i])
                  for i, (src, dst) in enumerate(((head_hbm, head), (tail_hbm, tail)))]
        rels = [fetch(rel_ids, rel_ref, rel_buf, rel_sem, 0, s) for s in range(tasks)]
        for copy in edges + rels + blocks:
            copy.start()
        for copy in edges:
            copy.wait()
        labels(labels_ref, he, te, 0, tasks)
        for copy in rels + blocks:
            copy.wait()
        scale_heads(head[...], rel_ids, rel_buf, rel_out, shi, slo, 0, tasks)
        new, state = tail_step(counts[0], tail[...], tacc[...], shi, slo, labels_ref, chi_ref, clo_ref, tasks)
        put_tail(tail_out, new, state, width)

    return body


def tail_kernel(k, tasks, width, last):
    def body(counts, tail_in, shi, slo, labels_ref, *outs):
        tail, state = tail_in[pl.ds(0, width), :], tail_in[pl.ds(width, 1), :]
        chi_ref, clo_ref = outs[-2:]
        new, state = tail_step(counts[k], tail, state, shi, slo, labels_ref, chi_ref, clo_ref, tasks)
        if last:
            outs[0][...] = new
            outs[1][...] = state
        else:
            put_tail(outs[0], new, state, width)

    return body


def head_kernel(k, tasks, width):
    first = (k + 1) * tasks

    def body(rel_ids, head, hacc, tail_in, rel_in, chi_ref, clo_ref, rel_ref, he, te,
             head_out, hacc_out, shi, slo, labels_ref, rel_out, rel_buf, rel_sem):
        rels = [fetch(rel_ids, rel_ref, rel_buf, rel_sem, first, s) for s in range(tasks)]
        for copy in rels:
            copy.start()
        new, state = head_step(head[...], hacc[...], tail_in[pl.ds(0, width), :], rel_in, chi_ref, clo_ref, tasks)
        head_out[...] = new
        hacc_out[...] = state
        labels(labels_ref, he, te, first, tasks)
        for copy in rels:
            copy.wait()
        scale_heads(new, rel_ids, rel_buf, rel_out, shi, slo, first, tasks)

    return body


def last_kernel(tasks, width):
    def body(head, hacc, tail_in, rel_in, chi_ref, clo_ref, head_out, hacc_out):
        new, state = head_step(head[...], hacc[...], tail_in[pl.ds(0, width), :], rel_in, chi_ref, clo_ref, tasks)
        head_out[...] = new
        hacc_out[...] = state

    return body


def call(body, ins, outs, scratch, args, name, flops):
    return pl.pallas_call(
        body,
        in_specs=ins,
        out_specs=[VMEM] * len(outs),
        out_shape=[jax.ShapeDtypeStruct(*o) for o in outs],
        scratch_shapes=scratch,
        compiler_params=pltpu.CompilerParams(vmem_limit_bytes=16 << 20),
        cost_estimate=pl.CostEstimate(flops=flops, bytes_accessed=1 << 20, transcendentals=0),
        name=name,
    )(*args)


def shifted(block, distance):
    n = lax.axis_size("blk")
    return lax.ppermute(block, "blk", [((i - distance) % n, i) for i in range(n)])


def on_device(heads, tails, head_acc, tail_acc, relations, counts, rel_ids, head_edges, tail_edges):
    rounds, _, tasks, edges = head_edges.shape
    rows, width = heads.shape
    head, tail, rels = heads.T, tails.T, relations.T
    hacc, tacc = head_acc.reshape(1, rows), tail_acc.reshape(1, rows)
    counts, rel_ids = counts.reshape(-1), rel_ids.reshape(-1)
    he = head_edges.reshape(rounds * tasks, edges // LANES, LANES)
    te = tail_edges.reshape(rounds * tasks, edges // LANES, LANES)
    wide = tasks * rows
    block, packed, row = ((width, rows), F32), ((width + 8, rows), F32), ((1, rows), F32)
    coeff, scaled, table = ((rows, wide), BF16), ((width, wide), BF16), ((tasks, rows, rows), F32)
    rel_scratch = [pltpu.VMEM((tasks, width, LANES), BF16), pltpu.SemaphoreType.DMA((tasks,))]
    big = 10**9

    sent, chi, clo, rel = call(
        first_kernel(tasks, width),
        [SMEM, SMEM, ANY, ANY, VMEM, ANY, ANY, ANY],
        [packed, coeff, coeff, scaled],
        [pltpu.VMEM(*block), pltpu.VMEM(*block),
         pltpu.VMEM((tasks, edges // LANES, LANES), jnp.int32), pltpu.VMEM((tasks, edges // LANES, LANES), jnp.int32),
         pltpu.VMEM(*scaled), pltpu.VMEM(*scaled), pltpu.VMEM(*table)] + rel_scratch + [pltpu.SemaphoreType.DMA((4,))],
        (counts, rel_ids, head, tail, tacc, rels, he, te), "first", big)
    held = tail
    for k in range(rounds - 1):
        arrived = shifted(sent, 1)
        head, hacc, shi, slo, lab, rel = call(
            head_kernel(k, tasks, width),
            [SMEM, VMEM, VMEM, VMEM, VMEM, VMEM, VMEM, ANY, VMEM, VMEM],
            [block, row, scaled, scaled, table, scaled], rel_scratch,
            (rel_ids, head, hacc, held, rel, chi, clo, rels, he, te), f"heads_{k}", big)
        held = arrived
        last = k == rounds - 2
        *sent, chi, clo = call(
            tail_kernel(k + 1, tasks, width, last),
            [SMEM, VMEM, VMEM, VMEM, VMEM],
            ([block, row] if last else [packed]) + [coeff, coeff], [],
            (counts, held, shi, slo, lab), f"tails_{k + 1}", big)
        sent = tuple(sent) if last else sent[0]
    tail, tacc = shifted(sent, 1 - rounds)
    head, hacc = call(
        last_kernel(tasks, width), [VMEM] * 6, [block, row], [],
        (head, hacc, held, rel, chi, clo), "heads_last", big)
    return head.T, tail.T, hacc.reshape(rows), tacc.reshape(rows)


def solution(mesh):
    split, edge = P(("blk", "help"), None), P(None, ("blk", "help"), None, None)
    flat = P(("blk", "help"))
    return jax.shard_map(
        on_device,
        mesh=mesh,
        in_specs=(split, split, flat, flat, P(), P(None, ("blk", "help")), P(None, ("blk", "help"), None), edge, edge),
        out_specs=(split, split, flat, flat),
        check_vma=False,
    )
```

time: 183 us -> 63.2 us (0.35)
  loops' own time: 53.8 us -> 0 us
  matrix products: 46.4 us -> 0 us
  Pallas kernels: 0 us -> 19 us
  local copies, waits for them, and re-layouts: 25.8 us -> 9.44 us
  other arithmetic: 16.2 us -> 1.34 us
  waiting for transfers between devices: 37.2 us -> 31 us
    another operation x4 -> x0, loops' own time: 53.8 us -> none  [own_grads(): lax.fori_loop(jnp.int32(0), counts[round_ix, 0], add_task, (empty, empty))]
    dot_general x80 -> x0, matrix products: 46.4 us -> none  [the longest x20 14.4 us: task_grads(): lax.dot_general(scaled, tail_block, (((1,), (1,)), ((), ())), precision=H...]
    pallas_call x0 -> x8, Pallas kernels: none -> 19 us  [call(): pl.pallas_call(body, in_specs=ins, out_specs=[VMEM] * len(outs), out_shap...]
    mul x20 -> x0, other arithmetic: 14.1 us -> none  [task_grads(): scaled = head_block * rel_vec[None, :]]
    dynamic_slice x40 -> x0, local copies, waits for them, and re-layouts: 12.2 us -> none  [the longest x20 11.9 us: add_task(): rel_vec = relations[rel_row[slot_id]].astype(jnp.float32)]
    while x4 -> x0, local copies, waits for them, and re-layouts: 9.96 us -> none  [own_grads(): lax.fori_loop(jnp.int32(0), counts[round_ix, 0], add_task, (empty, empty))]
    unnamed x14 -> x27, local copies, waits for them, and re-layouts: 1.22 us -> 9.35 us
    ppermute x8 -> x5, waiting for transfers between devices: 37.2 us -> 31 us  [shifted(): lax.ppermute(block, 'blk', [((i - distance) % n, i) for i in range(n)])]
  transfers between devices with their start and end apart: 8 -> 5, of which waited for: 4 -> 4; matrix products, arithmetic and copies ran while one was open for 32% -> 0% of each run, Pallas kernels for 0% -> 15%
where the time goes in v1:
time: 63.2 us; the launch traced here: 62.1 us
  waiting for transfers between devices  31 us (49%)
  Pallas kernels  19 us (30%)
  local copies, waits for them, and re-layouts  9.44 us (15%)
  other arithmetic  1.34 us (2%)
  between operations  0.79 us (1%)
    ppermute x5, waiting for transfers between devices, shifted(): lax.ppermute(block, 'blk', [((i - distance) % n, i) for i in range(n)])  31 us
    pallas_call x8, Pallas kernels, call(): pl.pallas_call(body, in_specs=ins, out_specs=[VMEM] * len(outs), out_shap...  19 us
    unnamed x27, local copies, waits for them, and re-layouts  9.35 us
    unnamed x1, other arithmetic  1.34 us
  transfers between devices with their start and end apart: 5, of which 4 were waited for; matrix products, arithmetic and copies ran while one was open for 0% of the time, Pallas kernels for 15%

profile of v1, /device:TPU:0, one launch (start us, length us, event | category | flops | bytes accessed | tf_op | source)
XLA Modules:
  0.0 62.1 jit_solution(6622609822592678537)
XLA Ops:
  0.6 0.5 broadcast.3
  1.2 1.3 %reduce.3 = s32[4,5]{1,0:T(4,128)S(1)} reduce(s32[4,1,5]{2,1,0:T(1,128)} %param.15, s32[]{:T(128)} %broadcast.3), dimensions={1}, to_apply=%param.15.reduce_sub_computation.3 | reduce | bytes 164 | tf_op args[6]
  2.6 2.7 %copy-done = bf16[7424,400]{0,1:T(8,128)(2,1)S(1)} copy-done((bf16[7424,400]{0,1:T(8,128)(2,1)S(1)}, bf16[7424,400]{0,1:T(8,128)(2,1)}, u32[]{:S(2)}) %copy-start) | copy-done | bytes 5939224
  5.3 0.9 %copy-done.2 = s32[4,1,5,1024]{3,1,2,0:T(1,128)S(1)} copy-done((s32[4,1,5,1024]{3,1,2,0:T(1,128)S(1)}, s32[4,1,5,1024]{3,1,2,0:T(1,128)}, u32[]{:S(2)}) %copy-start.2) | copy-done | bytes 81944
  6.2 0.9 %copy-done.4 = s32[4,1,5,1024]{3,1,2,0:T(1,128)S(1)} copy-done((s32[4,1,5,1024]{3,1,2,0:T(1,128)S(1)}, s32[4,1,5,1024]{3,1,2,0:T(1,128)}, u32[]{:S(2)}) %copy-start.4) | copy-done | bytes 81944
  7.0 0.9 %copy-done.6 = f32[128,400]{0,1:T(8,128)S(1)} copy-done((f32[128,400]{0,1:T(8,128)S(1)}, f32[128,400]{0,1:T(8,128)}, u32[]{:S(2)}) %copy-start.6) | copy-done | bytes 204824
  8.0 0.9 %copy-done.8 = f32[128,400]{0,1:T(8,128)S(1)} copy-done((f32[128,400]{0,1:T(8,128)S(1)}, f32[128,400]{0,1:T(8,128)}, u32[]{:S(2)}) %copy-start.8) | copy-done | bytes 204824
  8.9 0.7 %copy-done.9 = f32[128]{0:T(128)S(1)} copy-done((f32[128]{0:T(128)S(1)}, f32[128]{0:T(128)}, u32[]{:S(2)}) %copy-start.9) | copy-done | bytes 536
  9.6 0.7 %copy-done.11 = s32[4,1]{0,1:T(1,128)S(1)} copy-done((s32[4,1]{0,1:T(1,128)S(1)}, s32[4,1]{0,1:T(1,128)}, u32[]{:S(2)}) %copy-start.11) | copy-done | bytes 40
  10.2 4.1 %first.1 = (f32[408,128]{1,0:T(8,128)S(1)}, bf16[128,640]{1,0:T(8,128)(2,1)S(1)}, bf16[128,640]{1,0:T(8,128)(2,1)S(1)}, bf16[400,640]{1,0:T(8,128)(2,1)S(1)}) custom-call(s32[4]{0:T(128)S(1)} %bitcast.30, s32[20]{0:T(128)S(1)} %reshape.32.rel_ids, f32[400,128]{1,0:T(8,128)S(1)} %bitcast.24, f32[400,128]{1,0:T(8,128)S(1)} %bitcast.26, f32[1,128]{1,0:T(1,128)S(1)} %bitcast.28, ...), custom_call_target="tpu_custom_call" | custom-call | flops 1000000000 | bytes 1048576 | tf_op jit(solution)/shard_map/first/pallas_call | solution.py:166
  14.5 2.6 %heads_0.1 = (f32[400,128]{1,0:T(8,128)S(1)}, f32[1,128]{1,0:T(1,128)S(1)}, bf16[400,640]{1,0:T(8,128)(2,1)S(1)}, bf16[400,640]{1,0:T(8,128)(2,1)S(1)}, f32[5,12...) custom-call(s32[20]{0:T(128)S(1)} %reshape.32.rel_ids, f32[400,128]{1,0:T(8,128)S(1)} %bitcast.25, ...), custom_call_target="tpu_custom_call" | custom-call | flops 1000000000 | bytes 1048576 | tf_op jit(solution)/shard_map/heads_0/pallas_call | solution.py:166
  17.1 9.3 %collective-permute-done.tail_in = f32[408,128]{1,0:T(8,128)S(1)} collective-permute-done((f32[408,128]{1,0:T(8,128)S(1)}, f32[408,128]{1,0:T(8,128)S(1)}, u32[]{:S(2)}, u32[]{:S(2)}) %collective-permute-start) | collective-permute-done | bytes 208928 | tf_op jit(solution)/shard_map/ppermute | solution.py:180
  26.4 1.8 %tails_1.1 = (f32[408,128]{1,0:T(8,128)S(1)}, bf16[128,640]{1,0:T(8,128)(2,1)S(1)}, bf16[128,640]{1,0:T(8,128)(2,1)S(1)}) custom-call(s32[4]{0:T(128)S(1)} %bitcast.31, f32[408,128]{1,0:T(8,128)S(1)} %collective-permute-done.tail_in, bf16[400,640]{1,0:T(8,128)(2,1)S(1)} %get-tuple-element.45.shi, bf16[400,640]{1,0:T(8,128)(2,1)S(1)} %get-tuple-element.46.slo, ...), custom_call_target="tpu_custom_call" | custom-call | flops 1000000000 | bytes 1048576 | tf_op jit(solution)/shard_map/tails_1/pallas_call | solution.py:166
  28.2 2.6 %heads_1.1 = (f32[400,128]{1,0:T(8,128)S(1)}, f32[1,128]{1,0:T(1,128)S(1)}, bf16[400,640]{1,0:T(8,128)(2,1)S(1)}, bf16[400,640]{1,0:T(8,128)(2,1)S(1)}, f32[5,12...) custom-call(s32[20]{0:T(128)S(1)} %reshape.32.rel_ids, f32[400,128]{1,0:T(8,128)S(1)} %get-tuple-element.41.head, ...), custom_call_target="tpu_custom_call" | custom-call | flops 1000000000 | bytes 1048576 | tf_op jit(solution)/shard_map/heads_1/pallas_call | solution.py:166
  30.9 8.3 %collective-permute-done.1.tail_in = f32[408,128]{1,0:T(8,128)S(1)} collective-permute-done((f32[408,128]{1,0:T(8,128)S(1)}, f32[408,128]{1,0:T(8,128)S(1)}, u32[]{:S(2)}, u32[]{:S(2)}) %collective-permute-start.1) | collective-permute-done | bytes 208928 | tf_op jit(solution)/shard_map/ppermute | solution.py:180
  39.2 1.8 %tails_2.1 = (f32[408,128]{1,0:T(8,128)S(1)}, bf16[128,640]{1,0:T(8,128)(2,1)S(1)}, bf16[128,640]{1,0:T(8,128)(2,1)S(1)}) custom-call(s32[4]{0:T(128)S(1)} %bitcast.32, f32[408,128]{1,0:T(8,128)S(1)} %collective-permute-done.1.tail_in, bf16[400,640]{1,0:T(8,128)(2,1)S(1)} %get-tuple-element.54.shi, bf16[400,640]{1,0:T(8,128)(2,1)S(1)} %get-tuple-element.55.slo, ...), custom_call_target="tpu_custom_call" | custom-call | flops 1000000000 | bytes 1048576 | tf_op jit(solution)/shard_map/tails_2/pallas_call | solution.py:166
  41.0 0.3 collective-permute-start.2
  41.3 2.6 %heads_2.1 = (f32[400,128]{1,0:T(8,128)S(1)}, f32[1,128]{1,0:T(1,128)S(1)}, bf16[400,640]{1,0:T(8,128)(2,1)S(1)}, bf16[400,640]{1,0:T(8,128)(2,1)S(1)}, f32[5,12...) custom-call(s32[20]{0:T(128)S(1)} %reshape.32.rel_ids, f32[400,128]{1,0:T(8,128)S(1)} %get-tuple-element.50.head, ...), custom_call_target="tpu_custom_call" | custom-call | flops 1000000000 | bytes 1048576 | tf_op jit(solution)/shard_map/heads_2/pallas_call | solution.py:166
  43.9 8.4 %collective-permute-done.2.tail_in = f32[408,128]{1,0:T(8,128)S(1)} collective-permute-done((f32[408,128]{1,0:T(8,128)S(1)}, f32[408,128]{1,0:T(8,128)S(1)}, u32[]{:S(2)}, u32[]{:S(2)}) %collective-permute-start.2) | collective-permute-done | bytes 208928 | tf_op jit(solution)/shard_map/ppermute | solution.py:180
  52.3 1.8 %tails_3.1 = (f32[400,128]{1,0:T(8,128)S(1)}, f32[1,128]{1,0:T(1,128)S(1)}, bf16[128,640]{1,0:T(8,128)(2,1)S(1)}, bf16[128,640]{1,0:T(8,128)(2,1)S(1)}) custom-call(s32[4]{0:T(128)S(1)} %bitcast.33, f32[408,128]{1,0:T(8,128)S(1)} %collective-permute-done.2.tail_in, bf16[400,640]{1,0:T(8,128)(2,1)S(1)} %get-tuple-element.63.shi, ...), custom_call_target="tpu_custom_call" | custom-call | flops 1000000000 | bytes 1048576 | tf_op jit(solution)/shard_map/tails_3/pallas_call | solution.py:166
  54.3 1.7 %heads_last.1 = (f32[400,128]{1,0:T(8,128)}, f32[1,128]{1,0:T(1,128)}) custom-call(f32[400,128]{1,0:T(8,128)S(1)} %get-tuple-element.59.head, f32[1,128]{1,0:T(1,128)S(1)} %get-tuple-element.60.hacc, f32[408,128]{1,0:T(8,128)S(1)} %collective-permute-done.2.tail_in, bf16[400,640]{1,0:T(8,128)(2,1)S(1)} %get-tuple-element.62.rel_in, ...), custom_call_target="tpu_custom_call" | custom-call | flops 1000000000 | bytes 1048576 | tf_op jit(solution)/shard_map/heads_last/pallas_call | solution.py:166
  56.0 5.0 %collective-permute-done.4 = f32[1,128]{1,0:T(1,128)S(1)} collective-permute-done((f32[1,128]{1,0:T(1,128)S(1)}, f32[1,128]{1,0:T(1,128)S(1)}, u32[]{:S(2)}, u32[]{:S(2)}) %collective-permute-start.4) | collective-permute-done | bytes 544 | tf_op jit(solution)/shard_map/ppermute | solution.py:180
  60.9 0.7 %copy.15 = f32[128,400]{0,1:T(8,128)} copy(f32[128,400]{0,1:T(8,128)S(1)} %bitcast.34) | data formatting | bytes 409600
  61.6 0.5 copy.16
  (23 shorter events, 0.5 us)
Async XLA Ops:
  0.6 13.8 %copy-start.10 = (f32[128]{0:T(128)S(1)}, f32[128]{0:T(128)}, u32[]{:S(2)}) copy-start(f32[128]{0:T(128)} %param.11) | copy-start | bytes 1540
  2.6 2.7 %copy-start = (bf16[7424,400]{0,1:T(8,128)(2,1)S(1)}, bf16[7424,400]{0,1:T(8,128)(2,1)}, u32[]{:S(2)}) copy-start(bf16[7424,400]{0,1:T(8,128)(2,1)} %param.13) | copy-start | bytes 17817604
  5.3 0.9 %copy-start.2 = (s32[4,1,5,1024]{3,1,2,0:T(1,128)S(1)}, s32[4,1,5,1024]{3,1,2,0:T(1,128)}, u32[]{:S(2)}) copy-start(s32[4,1,5,1024]{3,1,2,0:T(1,128)} %param.16) | copy-start | bytes 245764
  6.2 0.9 %copy-start.4 = (s32[4,1,5,1024]{3,1,2,0:T(1,128)S(1)}, s32[4,1,5,1024]{3,1,2,0:T(1,128)}, u32[]{:S(2)}) copy-start(s32[4,1,5,1024]{3,1,2,0:T(1,128)} %param.17) | copy-start | bytes 245764
  7.0 0.9 %copy-start.6 = (f32[128,400]{0,1:T(8,128)S(1)}, f32[128,400]{0,1:T(8,128)}, u32[]{:S(2)}) copy-start(f32[128,400]{0,1:T(8,128)} %param.9) | copy-start | bytes 614404
  8.0 0.9 %copy-start.8 = (f32[128,400]{0,1:T(8,128)S(1)}, f32[128,400]{0,1:T(8,128)}, u32[]{:S(2)}) copy-start(f32[128,400]{0,1:T(8,128)} %param.10) | copy-start | bytes 614404
  8.9 0.7 %copy-start.9 = (f32[128]{0:T(128)S(1)}, f32[128]{0:T(128)}, u32[]{:S(2)}) copy-start(f32[128]{0:T(128)} %param.12) | copy-start | bytes 1540
  9.6 0.7 %copy-start.11 = (s32[4,1]{0,1:T(1,128)S(1)}, s32[4,1]{0,1:T(1,128)}, u32[]{:S(2)}) copy-start(s32[4,1]{0,1:T(1,128)} %param.14) | copy-start | bytes 52
  10.2 4.2 %copy-start.1 = (bf16[7424,400]{0,1:T(8,128)(2,1)S(1)}, bf16[7424,400]{0,1:T(8,128)(2,1)}, u32[]{:S(2)}) copy-start(bf16[7424,400]{0,1:T(8,128)(2,1)} %param.13) | copy-start | bytes 17817604
  10.2 4.2 %copy-start.3 = (s32[4,1,5,1024]{3,1,2,0:T(1,128)S(1)}, s32[4,1,5,1024]{3,1,2,0:T(1,128)}, u32[]{:S(2)}) copy-start(s32[4,1,5,1024]{3,1,2,0:T(1,128)} %param.16) | copy-start | bytes 245764
  10.2 4.2 %copy-start.5 = (s32[4,1,5,1024]{3,1,2,0:T(1,128)S(1)}, s32[4,1,5,1024]{3,1,2,0:T(1,128)}, u32[]{:S(2)}) copy-start(s32[4,1,5,1024]{3,1,2,0:T(1,128)} %param.17) | copy-start | bytes 245764
  10.2 4.2 %copy-start.7 = (f32[128,400]{0,1:T(8,128)S(1)}, f32[128,400]{0,1:T(8,128)}, u32[]{:S(2)}) copy-start(f32[128,400]{0,1:T(8,128)} %param.9) | copy-start | bytes 614404
  14.3 12.1 %collective-permute-start = (f32[408,128]{1,0:T(8,128)S(1)}, f32[408,128]{1,0:T(8,128)S(1)}, u32[]{:S(2)}, u32[]{:S(2)}) collective-permute-start(f32[408,128]{1,0:T(8,128)S(1)} %get-tuple-element.43), channel_id=1, source_target_pairs={{254,0},{0,2},{2,4},{4,6},{6,8},{8,10},{10,12},{12,14},{14,16},{16... | collective-permute-start | bytes 626696 | tf_op jit(solution)/shard_map/ppermute | solution.py:180
  28.2 11.0 %collective-permute-start.1 = (f32[408,128]{1,0:T(8,128)S(1)}, f32[408,128]{1,0:T(8,128)S(1)}, u32[]{:S(2)}, u32[]{:S(2)}) collective-permute-start(f32[408,128]{1,0:T(8,128)S(1)} %get-tuple-element.52), channel_id=1, source_target_pairs={{254,0},{0,2},{2,4},{4,6},{6,8},{8,10},{10,12},{12,14},{14,16},{16... | collective-permute-start | bytes 626696 | tf_op jit(solution)/shard_map/ppermute | solution.py:180
  41.0 11.3 %collective-permute-start.2 = (f32[408,128]{1,0:T(8,128)S(1)}, f32[408,128]{1,0:T(8,128)S(1)}, u32[]{:S(2)}, u32[]{:S(2)}) collective-permute-start(f32[408,128]{1,0:T(8,128)S(1)} %get-tuple-element.61), channel_id=1, source_target_pairs={{254,0},{0,2},{2,4},{4,6},{6,8},{8,10},{10,12},{12,14},{14,16},{16... | collective-permute-start | bytes 626696 | tf_op jit(solution)/shard_map/ppermute | solution.py:180
  54.1 6.9 %collective-permute-start.3 = (f32[400,128]{1,0:T(8,128)S(1)}, f32[400,128]{1,0:T(8,128)S(1)}, u32[]{:S(2)}, u32[]{:S(2)}) collective-permute-start(f32[400,128]{1,0:T(8,128)S(1)} %get-tuple-element.69), channel_id=1, source_target_pairs={{6,0},{8,2},{10,4},{12,6},{14,8},{16,10},{18,12},{20,14},{22,16},{... | collective-permute-start | bytes 614408 | tf_op jit(solution)/shard_map/ppermute | solution.py:180
  54.2 6.8 %collective-permute-start.4 = (f32[1,128]{1,0:T(1,128)S(1)}, f32[1,128]{1,0:T(1,128)S(1)}, u32[]{:S(2)}, u32[]{:S(2)}) collective-permute-start(f32[1,128]{1,0:T(1,128)S(1)} %get-tuple-element.71), channel_id=1, source_target_pairs={{6,0},{8,2},{10,4},{12,6},{14,8},{16,10},{18,12},{20,14},{22,16},{... | collective-permute-start | bytes 1544 | tf_op jit(solution)/shard_map/ppermute | solution.py:180

commit v2 on v1

v2 whole, which is shorter than its diff:
```python
import jax
import jax.numpy as jnp
from jax import lax
from jax.experimental import pallas as pl
from jax.experimental.pallas import tpu as pltpu
from jax.sharding import PartitionSpec as P

NEG_WEIGHT = 0.0625
LEARN_RATE = 0.1
F32, BF16, I32 = jnp.float32, jnp.bfloat16, jnp.int32
LANES = 128
ODD, EVEN = 1, 0
VMEM = pl.BlockSpec(memory_space=pltpu.VMEM)
SMEM = pl.BlockSpec(memory_space=pltpu.SMEM)
HBM = pl.BlockSpec(memory_space=pltpu.HBM)
NN, NT, TN = ((1,), (0,)), ((1,), (1,)), ((0,), (0,))


def role():
    return lax.rem(lax.axis_index("blk"), 2)


def dot(a, b, dims):
    return lax.dot_general(a, b, (dims, ((), ())), preferred_element_type=F32)


def hi_lo(x):
    hi = x.astype(BF16)
    return hi, (x - hi.astype(F32)).astype(BF16)


def cols(s):
    return pl.ds(s * LANES, LANES)


def one_hot(rows):
    which = lax.broadcasted_iota(I32, (LANES, LANES), 0)
    parts = [jnp.where(rows[r : r + 1, :] == which, 1.0, 0.0).astype(BF16) for r in range(rows.shape[0])]
    return jnp.concatenate(parts, axis=1)


def make_labels(labels_ref, he, te, tasks):
    for s in range(tasks):
        labels_ref[s] = dot(one_hot(te[s]), one_hot(he[s]), NT)


def rel_copies(rel_ids, rel_ref, rel_buf, sem, step, tasks):
    copies = []
    for s in range(tasks):
        start = pl.multiple_of((rel_ids[step, 0, s] // LANES) * LANES, LANES)
        copies.append(pltpu.make_async_copy(rel_ref.at[:, pl.ds(start, LANES)], rel_buf.at[s], sem.at[s]))
    return copies


def edge_copies(he_hbm, te_hbm, he, te, sem, step, tasks):
    rows = pl.ds(step * tasks, tasks)
    return [pltpu.make_async_copy(he_hbm.at[rows], he, sem.at[0]), pltpu.make_async_copy(te_hbm.at[rows], te, sem.at[1])]


def scale_heads(head, rel_ids, count, rel_buf, step, shi, slo, rel_out, live, tasks):
    for s in range(tasks):
        lane = lax.rem(rel_ids[step, 0, s], LANES)
        pick = (lax.broadcasted_iota(I32, (LANES, LANES), 0) == lane).astype(F32).astype(BF16)
        rel = dot(rel_buf[s], pick, NN)
        rel_out[:, cols(s)] = rel.astype(BF16)
        shi[:, cols(s)], slo[:, cols(s)] = hi_lo(head * rel)
        live[s] = jnp.full(live.shape[1:], jnp.where(s < count, 1.0, 0.0), F32)


def adagrad(block, state, grad):
    state = state + jnp.sum(grad * grad, axis=0, keepdims=True) * (1.0 / block.shape[0])
    return block - grad * (LEARN_RATE / jnp.sqrt(state)), state


def tail_step(tail, state, shi_ref, slo_ref, labels_ref, live_ref, kept, tail_out, tasks):
    thi_ref, tlo_ref, chi_ref, clo_ref = kept
    width = tail.shape[0]
    thi, tlo = hi_lo(tail)
    thi_ref[...], tlo_ref[...] = thi, tlo
    shi, slo = shi_ref[...], slo_ref[...]
    scores = dot(thi, shi, TN) + dot(tlo, shi, TN) + dot(thi, slo, TN)
    for s in range(tasks):
        score = scores[:, s * LANES : (s + 1) * LANES]
        coefficient = NEG_WEIGHT * (0.5 * jnp.tanh(0.5 * score) + 0.5) - labels_ref[s]
        chi_ref[:, cols(s)], clo_ref[:, cols(s)] = hi_lo(coefficient * live_ref[s, 0:1, :])
    chi, clo = chi_ref[...], clo_ref[...]
    grad = dot(shi, chi, NT) + dot(slo, chi, NT) + dot(shi, clo, NT)
    tail, state = adagrad(tail, state, grad)
    tail_out[pl.ds(0, width), :] = tail
    tail_out[pl.ds(width, 8), :] = jnp.broadcast_to(state, (8, LANES))


def head_step(head, state, kept, rel_ref, tasks):
    thi_ref, tlo_ref, chi_ref, clo_ref = kept
    thi, tlo = thi_ref[...], tlo_ref[...]
    grad = None
    for s in range(tasks):
        chi, clo = chi_ref[:, cols(s)], clo_ref[:, cols(s)]
        term = dot(thi, chi, NN) + dot(tlo, chi, NN) + dot(thi, clo, NN)
        term = term * rel_ref[:, cols(s)].astype(F32)
        grad = term if grad is None else grad + term
    return adagrad(head, state, grad)


def first_kernel(mine, tasks):
    n = 11

    def body(counts_hbm, ids_hbm, head_hbm, tail_hbm, hacc_hbm, tacc_hbm, rel_ref, he_hbm, te_hbm, *refs):
        outs, scratch = refs[-9 - n - 1 : -9], refs[-9:]
        tail_out, kept, (head, hacc, shi, slo, labels_ref, rel_out, live) = outs[0], outs[1:5], outs[5:]
        counts, rel_ids, tail, tacc, he, te, rel_buf, rel_sem, sem = scratch

        @pl.when(role() == mine)
        def _():
            small = [pltpu.make_async_copy(counts_hbm, counts, sem.at[2]), pltpu.make_async_copy(ids_hbm, rel_ids, sem.at[3])]
            edges = edge_copies(he_hbm, te_hbm, he, te, sem, 0, tasks)
            blocks = [pltpu.make_async_copy(src, dst, sem.at[4 + i]) for i, (src, dst) in enumerate(
                ((head_hbm, head), (tail_hbm, tail), (hacc_hbm, hacc), (tacc_hbm, tacc)))]
            for copy in small + edges + blocks:
                copy.start()
            for copy in small:
                copy.wait()
            rels = rel_copies(rel_ids, rel_ref, rel_buf, rel_sem, 0, tasks)
            for copy in rels:
                copy.start()
            for copy in edges:
                copy.wait()
            make_labels(labels_ref, he, te, tasks)
            for copy in rels + blocks:
                copy.wait()
            scale_heads(head[...], rel_ids, counts[0, 0], rel_buf, 0, shi, slo, rel_out, live, tasks)
            tail_step(tail[...], tacc[...], shi, slo, labels_ref, live, kept, tail_out, tasks)

    return body


def tail_kernel(mine, tasks, width):
    def body(tail_in, shi, slo, labels_ref, live, *refs):
        outs = refs[4:]

        @pl.when(role() == mine)
        def _():
            tail, state = tail_in[pl.ds(0, width), :], tail_in[pl.ds(width, 1), :]
            tail_step(tail, state, shi, slo, labels_ref, live, outs[1:5], outs[0], tasks)

    return body


def head_kernel(m, tasks, rounds):
    def body(counts, rel_ids, rel_ref, he_hbm, te_hbm, thi, tlo, chi, clo, *refs):
        ins, outs, (he, te, rel_buf, rel_sem, sem) = refs[:7], refs[7:14], refs[14:]
        head, hacc, rel_in = ins[0], ins[1], ins[5]
        head_out, hacc_out, shi, slo, labels_ref, rel_out, live = outs
        done = m - 1 + role()

        @pl.when((done >= 0) & (done < rounds - 1))
        def _():
            step = done + 1
            rels = rel_copies(rel_ids, rel_ref, rel_buf, rel_sem, step, tasks)
            edges = edge_copies(he_hbm, te_hbm, he, te, sem, step, tasks)
            for copy in edges + rels:
                copy.start()
            new, state = head_step(head[...], hacc[...], (thi, tlo, chi, clo), rel_in, tasks)
            head_out[...] = new
            hacc_out[...] = state
            for copy in edges:
                copy.wait()
            make_labels(labels_ref, he, te, tasks)
            for copy in rels:
                copy.wait()
            scale_heads(new, rel_ids, counts[0, step], rel_buf, step, shi, slo, rel_out, live, tasks)

    return body


def last_heads(tasks):
    def body(head, hacc, rel_in, thi, tlo, chi, clo, head_out, hacc_out):
        head_out[...], hacc_out[...] = head_step(head[...], hacc[...], (thi, tlo, chi, clo), rel_in, tasks)

    return body


def pick_tails(width):
    def body(from_odd, from_even, tail_out, tacc_out):
        for mine, ref in ((EVEN, from_odd), (ODD, from_even)):
            @pl.when(role() == mine)
            def _():
                tail_out[...] = ref[pl.ds(0, width), :]
                tacc_out[...] = ref[pl.ds(width, 1), :]

    return body


def call(body, ins, outs, scratch, args, name, alias=None):
    args = [pltpu.with_memory_space_constraint(a, pltpu.HBM) if spec is HBM else a for spec, a in zip(ins, args)]
    return pl.pallas_call(
        body,
        in_specs=ins,
        out_specs=[VMEM] * len(outs),
        out_shape=[jax.ShapeDtypeStruct(*o) for o in outs],
        scratch_shapes=scratch,
        input_output_aliases=alias or {},
        compiler_params=pltpu.CompilerParams(vmem_limit_bytes=16 << 20),
        cost_estimate=pl.CostEstimate(flops=10**9, bytes_accessed=1 << 20, transcendentals=0),
        name=name,
    )(*args)


def send(block, distance, mine):
    n = lax.axis_size("blk")
    return lax.ppermute(block, "blk", [(i, (i + distance) % n) for i in range(mine, n, 2)])


def swap(block):
    return lax.ppermute(block, "blk", [(i, i ^ 1) for i in range(lax.axis_size("blk"))])


def on_device(heads, tails, head_acc, tail_acc, relations, counts, rel_ids, head_edges, tail_edges):
    rounds, _, tasks, edges = head_edges.shape
    rows, width = heads.shape
    head, tail, rels = heads.T, tails.T, relations.T
    hacc, tacc, counts = head_acc.reshape(1, rows), tail_acc.reshape(1, rows), counts.T
    he = head_edges.reshape(rounds * tasks, edges // LANES, LANES)
    te = tail_edges.reshape(rounds * tasks, edges // LANES, LANES)
    wide = tasks * rows
    block, packed, row = ((width, rows), F32), ((width + 8, rows), F32), ((1, rows), F32)
    coeff, scaled, table = ((rows, wide), BF16), ((width, wide), BF16), ((tasks, rows, rows), F32)
    half, mask = ((width, rows), BF16), ((tasks, 8, rows), F32)
    kept_shapes = [half, half, coeff, coeff]
    state_shapes = [block, row, scaled, scaled, table, scaled, mask]
    edge_buf = pltpu.VMEM((tasks, edges // LANES, LANES), I32)
    rel_scratch = [pltpu.VMEM((tasks, width, LANES), BF16), pltpu.SemaphoreType.DMA((tasks,))]

    def first(mine, carried):
        return call(
            first_kernel(mine, tasks), [HBM] * 9 + [VMEM] * len(carried), [packed] + kept_shapes + state_shapes,
            [pltpu.SMEM(counts.shape, I32), pltpu.SMEM(rel_ids.shape, I32), pltpu.VMEM(*block), pltpu.VMEM(*row),
             edge_buf, edge_buf] + rel_scratch + [pltpu.SemaphoreType.DMA((8,))],
            [counts, rel_ids, head, tail, hacc, tacc, rels, he, te] + carried, f"first_{mine}",
            {9 + i: 1 + i for i in range(len(carried))})

    def tails_step(mine, k, tail_in, kept, state):
        out = call(
            tail_kernel(mine, tasks, width), [VMEM] * 9, [packed] + kept_shapes, [],
            [tail_in, state[2], state[3], state[4], state[6]] + kept, f"tails_{k}_{mine}",
            {5 + i: 1 + i for i in range(4)})
        return out[0], list(out[1:])

    def heads_step(m, kept, state):
        return list(call(
            head_kernel(m, tasks, rounds), [SMEM, SMEM, HBM, HBM, HBM] + [VMEM] * 11, state_shapes,
            [edge_buf, edge_buf] + rel_scratch + [pltpu.SemaphoreType.DMA((2,))],
            [counts, rel_ids, rels, he, te] + kept + state, f"heads_{m}", {9 + i: i for i in range(7)}))

    out = first(ODD, [])
    to_even = send(out[0], 1, ODD)
    out = first(EVEN, list(out[1:]))
    own, kept, state = out[0], list(out[1:5]), list(out[5:])
    state = heads_step(0, kept, state)
    for k in range(1, rounds):
        to_odd = swap(own)
        own, kept = tails_step(ODD, k, to_odd, kept, state)
        arrived = to_even
        to_even = send(own, 1 if k < rounds - 1 else 1 - rounds, ODD)
        state = heads_step(k, kept, state)
        own, kept = tails_step(EVEN, k, arrived, kept, state)
    to_odd = send(own, 1 - rounds, EVEN)
    head, hacc = call(last_heads(tasks), [VMEM] * 7, [block, row], [], [state[0], state[1], state[5]] + kept, "heads_last")
    tail, tacc = call(pick_tails(width), [VMEM] * 2, [block, row], [], [to_even, to_odd], "pick_tails")
    return head.T, tail.T, hacc.reshape(rows), tacc.reshape(rows)


def solution(mesh):
    split, edge = P(("blk", "help"), None), P(None, ("blk", "help"), None, None)
    flat = P(("blk", "help"))
    return jax.shard_map(
        on_device,
        mesh=mesh,
        in_specs=(split, split, flat, flat, P(), P(None, ("blk", "help")), P(None, ("blk", "help"), None), edge, edge),
        out_specs=(split, split, flat, flat),
        check_vma=False,
    )
```

time: 63.2 us -> 60.3 us (0.954)
  local copies, waits for them, and re-layouts: 9.44 us -> 0.01 us
  starting transfers between devices: 0.6 us -> 6.75 us
  Pallas kernels: 19 us -> 21.8 us
  other arithmetic: 1.34 us -> 0 us
  waiting for transfers between devices: 31 us -> 29.8 us
    unnamed x27 -> x4, local copies, waits for them, and re-layouts: 9.35 us -> 0.01 us
    ppermute x5 -> x8, starting transfers between devices: 0.6 us -> 6.75 us  [the longest x5 6.47 us: send(): lax.ppermute(block, 'blk', [(i, (i + distance) % n) for i in range(mine,...]
    pallas_call x8 -> x14, Pallas kernels: 19 us -> 21.8 us  [call(): pl.pallas_call(body, in_specs=ins, out_specs=[VMEM] * len(outs), out_shap...]
    unnamed x1 -> x0, other arithmetic: 1.34 us -> none
    ppermute x5 -> x8, waiting for transfers between devices: 31 us -> 29.8 us  [the longest x5 29.5 us: send(): lax.ppermute(block, 'blk', [(i, (i + distance) % n) for i in range(mine,...]
  transfers between devices with their start and end apart: 5 -> 8, of which waited for: 4 -> 7; matrix products, arithmetic and copies ran while one was open for 0% -> 0% of each run, Pallas kernels for 15% -> 22%
where the time goes in v2:
time: 60.3 us; the launch traced here: 59.2 us
  waiting for transfers between devices  29.8 us (49%)
  Pallas kernels  21.8 us (36%)
  starting transfers between devices  6.75 us (11%)
  between operations  0.82 us (1%)
    ppermute x5, waiting for transfers between devices, send(): lax.ppermute(block, 'blk', [(i, (i + distance) % n) for i in range(mine,...  29.5 us
    pallas_call x14, Pallas kernels, call(): pl.pallas_call(body, in_specs=ins, out_specs=[VMEM] * len(outs), out_shap...  21.8 us
    ppermute x5, starting transfers between devices, send(): lax.ppermute(block, 'blk', [(i, (i + distance) % n) for i in range(mine,...  6.47 us
  transfers between devices with their start and end apart: 8, of which 7 were waited for; matrix products, arithmetic and copies ran while one was open for 0% of the time, Pallas kernels for 22%

profile of v2, /device:TPU:0, one launch (start us, length us, event | category | flops | bytes accessed | tf_op | source)
XLA Modules:
  0.0 59.2 jit_solution(8667774464431491276)
XLA Ops:
  0.6 0.1 first_1.1
  0.8 4.1 %first_0.1 = (f32[408,128]{1,0:T(8,128)S(1)}, bf16[400,128]{1,0:T(8,128)(2,1)S(1)}, bf16[400,128]{1,0:T(8,128)(2,1)S(1)}, bf16[128,640]{1,0:T(8,128)(2,1)S(1)}, ...) custom-call(s32[1,4]{1,0:T(1,128)} %bitcast.13, ...), custom_call_target="tpu_custom_call", output_to_operand_aliasing={{1}: (9, {}), {2}: (10, {}), {3}: (11, {}), {4}: (12, {}), ... | custom-call | flops 1000000000 | bytes 1048576 | tf_op jit(solution)/shard_map/first_0/pallas_call | solution.py:196
  5.0 0.1 collective-permute-start
  5.1 1.3 %collective-permute-start.2 = (f32[408,128]{1,0:T(8,128)S(1)}, f32[408,128]{1,0:T(8,128)S(1)}, u32[]{:S(2)}, u32[]{:S(2)}) collective-permute-start(f32[408,128]{1,0:T(8,128)S(1)} %get-tuple-element.118), channel_id=1, source_target_pairs={{2,4},{6,8},{10,12},{14,16},{18,20},{22,24},{26,28},{30,32},{34,36... | collective-permute-start | bytes 626696 | tf_op jit(solution)/shard_map/ppermute | solution.py:211
  6.4 0.7 %heads_0.1 = (f32[400,128]{1,0:T(8,128)S(1)}, f32[1,128]{1,0:T(1,128)S(1)}, bf16[400,640]{1,0:T(8,128)(2,1)S(1)}, bf16[400,640]{1,0:T(8,128)(2,1)S(1)}, f32[5,12...) custom-call(s32[1,4]{1,0:T(1,128)S(1)} %bitcast.14, ...), custom_call_target="tpu_custom_call", output_to_operand_aliasing={{0}: (9, {}), {1}: (10, {}), {2}: (11, {}), {3}: (12, {}), ... | custom-call | flops 1000000000 | bytes 1048576 | tf_op jit(solution)/shard_map/heads_0/pallas_call | solution.py:196
  7.1 3.6 %heads_1.1 = (f32[400,128]{1,0:T(8,128)S(1)}, f32[1,128]{1,0:T(1,128)S(1)}, bf16[400,640]{1,0:T(8,128)(2,1)S(1)}, bf16[400,640]{1,0:T(8,128)(2,1)S(1)}, f32[5,12...) custom-call(s32[1,4]{1,0:T(1,128)S(1)} %bitcast.15, ...), custom_call_target="tpu_custom_call", output_to_operand_aliasing={{0}: (9, {}), {1}: (10, {}), {2}: (11, {}), {3}: (12, {}), ... | custom-call | flops 1000000000 | bytes 1048576 | tf_op jit(solution)/shard_map/heads_1/pallas_call | solution.py:196
  10.7 8.3 %collective-permute-done.2.tail_in = f32[408,128]{1,0:T(8,128)S(1)} collective-permute-done((f32[408,128]{1,0:T(8,128)S(1)}, f32[408,128]{1,0:T(8,128)S(1)}, u32[]{:S(2)}, u32[]{:S(2)}) %collective-permute-start.2) | collective-permute-done | bytes 208928 | tf_op jit(solution)/shard_map/ppermute | solution.py:211
  19.0 1.2 %tails_1_0.1 = (f32[408,128]{1,0:T(8,128)S(1)}, bf16[400,128]{1,0:T(8,128)(2,1)S(1)}, bf16[400,128]{1,0:T(8,128)(2,1)S(1)}, bf16[128,640]{1,0:T(8,128)(2,1)S(1)}, bf16[128,640]{1,0:T(8,128)(2,1)S(1)}) custom-call(f32[408,128]{1,0:T(8,128)S(1)} %collective-permute-done.2.tail_in, ...), custom_call_target="tpu_custom_call", output_to_operand_aliasing={{1}: (5, {}), {2}: (6, {}), {3}: (7, {}), {4}: (8, {})} | custom-call | flops 1000000000 | bytes 1048576 | tf_op jit(solution)/shard_map/tails_1_0/pallas_call | solution.py:196
  20.3 1.3 %collective-permute-start.1 = (f32[408,128]{1,0:T(8,128)S(1)}, f32[408,128]{1,0:T(8,128)S(1)}, u32[]{:S(2)}, u32[]{:S(2)}) collective-permute-start(f32[408,128]{1,0:T(8,128)S(1)} %get-tuple-element.117), channel_id=1, source_target_pairs={{2,4},{6,8},{10,12},{14,16},{18,20},{22,24},{26,28},{30,32},{34,36... | collective-permute-start | bytes 626696 | tf_op jit(solution)/shard_map/ppermute | solution.py:211
  21.6 0.1 collective-permute-done.3.tail_in
  21.8 3.6 %heads_2.1 = (f32[400,128]{1,0:T(8,128)S(1)}, f32[1,128]{1,0:T(1,128)S(1)}, bf16[400,640]{1,0:T(8,128)(2,1)S(1)}, bf16[400,640]{1,0:T(8,128)(2,1)S(1)}, f32[5,12...) custom-call(s32[1,4]{1,0:T(1,128)S(1)} %bitcast.16, ...), custom_call_target="tpu_custom_call", output_to_operand_aliasing={{0}: (9, {}), {1}: (10, {}), {2}: (11, {}), {3}: (12, {}), ... | custom-call | flops 1000000000 | bytes 1048576 | tf_op jit(solution)/shard_map/heads_2/pallas_call | solution.py:196
  25.4 7.7 %collective-permute-done.1.tail_in = f32[408,128]{1,0:T(8,128)S(1)} collective-permute-done((f32[408,128]{1,0:T(8,128)S(1)}, f32[408,128]{1,0:T(8,128)S(1)}, u32[]{:S(2)}, u32[]{:S(2)}) %collective-permute-start.1) | collective-permute-done | bytes 208928 | tf_op jit(solution)/shard_map/ppermute | solution.py:211
  33.1 1.2 %tails_2_0.1 = (f32[408,128]{1,0:T(8,128)S(1)}, bf16[400,128]{1,0:T(8,128)(2,1)S(1)}, bf16[400,128]{1,0:T(8,128)(2,1)S(1)}, bf16[128,640]{1,0:T(8,128)(2,1)S(1)}, bf16[128,640]{1,0:T(8,128)(2,1)S(1)}) custom-call(f32[408,128]{1,0:T(8,128)S(1)} %collective-permute-done.1.tail_in, ...), custom_call_target="tpu_custom_call", output_to_operand_aliasing={{1}: (5, {}), {2}: (6, {}), {3}: (7, {}), {4}: (8, {})} | custom-call | flops 1000000000 | bytes 1048576 | tf_op jit(solution)/shard_map/tails_2_0/pallas_call | solution.py:196
  34.5 1.3 %collective-permute-start.5 = (f32[408,128]{1,0:T(8,128)S(1)}, f32[408,128]{1,0:T(8,128)S(1)}, u32[]{:S(2)}, u32[]{:S(2)}) collective-permute-start(f32[408,128]{1,0:T(8,128)S(1)} %get-tuple-element.161), channel_id=1, source_target_pairs={{2,4},{6,8},{10,12},{14,16},{18,20},{22,24},{26,28},{30,32},{34,36... | collective-permute-start | bytes 626696 | tf_op jit(solution)/shard_map/ppermute | solution.py:211
  35.8 0.1 collective-permute-done.4.tail_in
  35.9 3.6 %heads_3.1 = (f32[400,128]{1,0:T(8,128)S(1)}, f32[1,128]{1,0:T(1,128)S(1)}, bf16[400,640]{1,0:T(8,128)(2,1)S(1)}, bf16[400,640]{1,0:T(8,128)(2,1)S(1)}, f32[5,12...) custom-call(s32[1,4]{1,0:T(1,128)S(1)} %bitcast.17, ...), custom_call_target="tpu_custom_call", output_to_operand_aliasing={{0}: (9, {}), {1}: (10, {}), {2}: (11, {}), {3}: (12, {}), ... | custom-call | flops 1000000000 | bytes 1048576 | tf_op jit(solution)/shard_map/heads_3/pallas_call | solution.py:196
  39.5 7.8 %collective-permute-done.5.tail_in = f32[408,128]{1,0:T(8,128)S(1)} collective-permute-done((f32[408,128]{1,0:T(8,128)S(1)}, f32[408,128]{1,0:T(8,128)S(1)}, u32[]{:S(2)}, u32[]{:S(2)}) %collective-permute-start.5) | collective-permute-done | bytes 208928 | tf_op jit(solution)/shard_map/ppermute | solution.py:211
  47.3 1.2 %tails_3_0.1 = (f32[408,128]{1,0:T(8,128)S(1)}, bf16[400,128]{1,0:T(8,128)(2,1)S(1)}, bf16[400,128]{1,0:T(8,128)(2,1)S(1)}, bf16[128,640]{1,0:T(8,128)(2,1)S(1)}, bf16[128,640]{1,0:T(8,128)(2,1)S(1)}) custom-call(f32[408,128]{1,0:T(8,128)S(1)} %collective-permute-done.5.tail_in, ...), custom_call_target="tpu_custom_call", output_to_operand_aliasing={{1}: (5, {}), {2}: (6, {}), {3}: (7, {}), {4}: (8, {})} | custom-call | flops 1000000000 | bytes 1048576 | tf_op jit(solution)/shard_map/tails_3_0/pallas_call | solution.py:196
  48.6 1.3 %collective-permute-start.7 = (f32[408,128]{1,0:T(8,128)S(1)}, f32[408,128]{1,0:T(8,128)S(1)}, u32[]{:S(2)}, u32[]{:S(2)}) collective-permute-start(f32[408,128]{1,0:T(8,128)S(1)} %get-tuple-element.172), channel_id=1, source_target_pairs={{0,250},{4,254},{8,2},{12,6},{16,10},{20,14},{24,18},{28,22},{32,2... | collective-permute-start | bytes 626696 | tf_op jit(solution)/shard_map/ppermute | solution.py:211
  49.9 1.3 %collective-permute-start.6 = (f32[408,128]{1,0:T(8,128)S(1)}, f32[408,128]{1,0:T(8,128)S(1)}, u32[]{:S(2)}, u32[]{:S(2)}) collective-permute-start(f32[408,128]{1,0:T(8,128)S(1)} %get-tuple-element.171), channel_id=1, source_target_pairs={{2,252},{6,0},{10,4},{14,8},{18,12},{22,16},{26,20},{30,24},{34,28... | collective-permute-start | bytes 626696 | tf_op jit(solution)/shard_map/ppermute | solution.py:211
  51.2 1.7 %heads_last.1 = (f32[400,128]{1,0:T(8,128)}, f32[1,128]{1,0:T(1,128)}) custom-call(f32[400,128]{1,0:T(8,128)S(1)} %get-tuple-element.158.head, f32[1,128]{1,0:T(1,128)S(1)} %get-tuple-element.159.hacc, bf16[400,640]{1,0:T(8,128)(2,1)S(1)} %get-tuple-element.160.rel_in, bf16[400,128]{1,0:T(8,128)(2,1)S(1)} %get-tuple-element.166.thi, ...), custom_call_target="tpu_custom_call" | custom-call | flops 1000000000 | bytes 1048576 | tf_op jit(solution)/shard_map/heads_last/pallas_call | solution.py:196
  52.9 0.9 %collective-permute-done.7.from_even = f32[408,128]{1,0:T(8,128)S(1)} collective-permute-done((f32[408,128]{1,0:T(8,128)S(1)}, f32[408,128]{1,0:T(8,128)S(1)}, u32[]{:S(2)}, u32[]{:S(2)}) %collective-permute-start.7) | collective-permute-done | bytes 208928 | tf_op jit(solution)/shard_map/ppermute | solution.py:211
  53.7 4.8 %collective-permute-done.6.from_odd = f32[408,128]{1,0:T(8,128)S(1)} collective-permute-done((f32[408,128]{1,0:T(8,128)S(1)}, f32[408,128]{1,0:T(8,128)S(1)}, u32[]{:S(2)}, u32[]{:S(2)}) %collective-permute-start.6) | collective-permute-done | bytes 208928 | tf_op jit(solution)/shard_map/ppermute | solution.py:211
  58.5 0.7 %pick_tails.1 = (f32[400,128]{1,0:T(8,128)}, f32[1,128]{1,0:T(1,128)}) custom-call(f32[408,128]{1,0:T(8,128)S(1)} %collective-permute-done.6.from_odd, f32[408,128]{1,0:T(8,128)S(1)} %collective-permute-done.7.from_even), custom_call_target="tpu_custom_call" | custom-call | flops 1000000000 | bytes 1048576 | tf_op jit(solution)/shard_map/pick_tails/pallas_call | solution.py:196
  (10 shorter events, 0.3 us)
Async XLA Ops:
  0.8 5.6 %copy-start = (s32[4,1,5]{2,1,0:T(1,128)S(1)}, s32[4,1,5]{2,1,0:T(1,128)}, u32[]{:S(2)}) copy-start(s32[4,1,5]{2,1,0:T(1,128)} %rel_ids.7) | copy-start | bytes 244
  0.8 5.6 %copy-start.1 = (s32[4,1]{0,1:T(1,128)S(1)}, s32[4,1]{0,1:T(1,128)}, u32[]{:S(2)}) copy-start(s32[4,1]{0,1:T(1,128)} %param.14) | copy-start | bytes 52
  5.0 2.1 %collective-permute-start = (f32[408,128]{1,0:T(8,128)S(1)}, f32[408,128]{1,0:T(8,128)S(1)}, u32[]{:S(2)}, u32[]{:S(2)}) collective-permute-start(f32[408,128]{1,0:T(8,128)S(1)} %get-tuple-element.101), channel_id=1, source_target_pairs={{0,2},{2,0},{4,6},{6,4},{8,10},{10,8},{12,14},{14,12},{16,18},{18,... | collective-permute-start | bytes 626696 | tf_op jit(solution)/shard_map/ppermute | solution.py:215
  5.1 13.9 %collective-permute-start.2 = (f32[408,128]{1,0:T(8,128)S(1)}, f32[408,128]{1,0:T(8,128)S(1)}, u32[]{:S(2)}, u32[]{:S(2)}) collective-permute-start(f32[408,128]{1,0:T(8,128)S(1)} %get-tuple-element.118), channel_id=1, source_target_pairs={{2,4},{6,8},{10,12},{14,16},{18,20},{22,24},{26,28},{30,32},{34,36... | collective-permute-start | bytes 626696 | tf_op jit(solution)/shard_map/ppermute | solution.py:211
  20.2 1.5 %collective-permute-start.3 = (f32[408,128]{1,0:T(8,128)S(1)}, f32[408,128]{1,0:T(8,128)S(1)}, u32[]{:S(2)}, u32[]{:S(2)}) collective-permute-start(f32[408,128]{1,0:T(8,128)S(1)} %get-tuple-element.130), channel_id=1, source_target_pairs={{0,2},{2,0},{4,6},{6,4},{8,10},{10,8},{12,14},{14,12},{16,18},{18,... | collective-permute-start | bytes 626696 | tf_op jit(solution)/shard_map/ppermute | solution.py:215
  20.3 12.8 %collective-permute-start.1 = (f32[408,128]{1,0:T(8,128)S(1)}, f32[408,128]{1,0:T(8,128)S(1)}, u32[]{:S(2)}, u32[]{:S(2)}) collective-permute-start(f32[408,128]{1,0:T(8,128)S(1)} %get-tuple-element.117), channel_id=1, source_target_pairs={{2,4},{6,8},{10,12},{14,16},{18,20},{22,24},{26,28},{30,32},{34,36... | collective-permute-start | bytes 626696 | tf_op jit(solution)/shard_map/ppermute | solution.py:211
  34.4 1.5 %collective-permute-start.4 = (f32[408,128]{1,0:T(8,128)S(1)}, f32[408,128]{1,0:T(8,128)S(1)}, u32[]{:S(2)}, u32[]{:S(2)}) collective-permute-start(f32[408,128]{1,0:T(8,128)S(1)} %get-tuple-element.146), channel_id=1, source_target_pairs={{0,2},{2,0},{4,6},{6,4},{8,10},{10,8},{12,14},{14,12},{16,18},{18,... | collective-permute-start | bytes 626696 | tf_op jit(solution)/shard_map/ppermute | solution.py:215
  34.5 12.8 %collective-permute-start.5 = (f32[408,128]{1,0:T(8,128)S(1)}, f32[408,128]{1,0:T(8,128)S(1)}, u32[]{:S(2)}, u32[]{:S(2)}) collective-permute-start(f32[408,128]{1,0:T(8,128)S(1)} %get-tuple-element.161), channel_id=1, source_target_pairs={{2,4},{6,8},{10,12},{14,16},{18,20},{22,24},{26,28},{30,32},{34,36... | collective-permute-start | bytes 626696 | tf_op jit(solution)/shard_map/ppermute | solution.py:211
  48.6 5.2 %collective-permute-start.7 = (f32[408,128]{1,0:T(8,128)S(1)}, f32[408,128]{1,0:T(8,128)S(1)}, u32[]{:S(2)}, u32[]{:S(2)}) collective-permute-start(f32[408,128]{1,0:T(8,128)S(1)} %get-tuple-element.172), channel_id=1, source_target_pairs={{0,250},{4,254},{8,2},{12,6},{16,10},{20,14},{24,18},{28,22},{32,2... | collective-permute-start | bytes 626696 | tf_op jit(solution)/shard_map/ppermute | solution.py:211
  49.9 8.6 %collective-permute-start.6 = (f32[408,128]{1,0:T(8,128)S(1)}, f32[408,128]{1,0:T(8,128)S(1)}, u32[]{:S(2)}, u32[]{:S(2)}) collective-permute-start(f32[408,128]{1,0:T(8,128)S(1)} %get-tuple-element.171), channel_id=1, source_target_pairs={{2,252},{6,0},{10,4},{14,8},{18,12},{22,16},{26,20},{30,24},{34,28... | collective-permute-start | bytes 626696 | tf_op jit(solution)/shard_map/ppermute | solution.py:211

commit v3 on v2

--- a/solution.py
+++ b/solution.py
@@ -4,6 +4,7 @@
 from jax.experimental import pallas as pl
 from jax.experimental.pallas import tpu as pltpu
 from jax.sharding import PartitionSpec as P
+
 
 NEG_WEIGHT = 0.0625
 LEARN_RATE = 0.1
@@ -191,7 +192,7 @@
     return body
 
 
-def call(body, ins, outs, scratch, args, name, alias=None):
+def call(body, ins, outs, scratch, args, alias=None):
     args = [pltpu.with_memory_space_constraint(a, pltpu.HBM) if spec is HBM else a for spec, a in zip(ins, args)]
     return pl.pallas_call(
         body,
@@ -202,7 +203,6 @@
         input_output_aliases=alias or {},
         compiler_params=pltpu.CompilerParams(vmem_limit_bytes=16 << 20),
         cost_estimate=pl.CostEstimate(flops=10**9, bytes_accessed=1 << 20, transcendentals=0),
-        name=name,
     )(*args)
 
 
@@ -236,13 +236,13 @@
             first_kernel(mine, tasks), [HBM] * 9 + [VMEM] * len(carried), [packed] + kept_shapes + state_shapes,
             [pltpu.SMEM(counts.shape, I32), pltpu.SMEM(rel_ids.shape, I32), pltpu.VMEM(*block), pltpu.VMEM(*row),
              edge_buf, edge_buf] + rel_scratch + [pltpu.SemaphoreType.DMA((8,))],
-            [counts, rel_ids, head, tail, hacc, tacc, rels, he, te] + carried, f"first_{mine}",
+            [counts, rel_ids, head, tail, hacc, tacc, rels, he, te] + carried,
             {9 + i: 1 + i for i in range(len(carried))})
 
-    def tails_step(mine, k, tail_in, kept, state):
+    def tails_step(mine, tail_in, kept, state):
         out = call(
             tail_kernel(mine, tasks, width), [VMEM] * 9, [packed] + kept_shapes, [],
-            [tail_in, state[2], state[3], state[4], state[6]] + kept, f"tails_{k}_{mine}",
+            [tail_in, state[2], state[3], state[4], state[6]] + kept,
             {5 + i: 1 + i for i in range(4)})
         return out[0], list(out[1:])
 
@@ -250,29 +250,31 @@
         return list(call(
             head_kernel(m, tasks, rounds), [SMEM, SMEM, HBM, HBM, HBM] + [VMEM] * 11, state_shapes,
             [edge_buf, edge_buf] + rel_scratch + [pltpu.SemaphoreType.DMA((2,))],
-            [counts, rel_ids, rels, he, te] + kept + state, f"heads_{m}", {9 + i: i for i in range(7)}))
+            [counts, rel_ids, rels, he, te] + kept + state, {9 + i: i for i in range(7)}))
 
     out = first(ODD, [])
     to_even = send(out[0], 1, ODD)
     out = first(EVEN, list(out[1:]))
     own, kept, state = out[0], list(out[1:5]), list(out[5:])
+    to_odd = swap(own)
     state = heads_step(0, kept, state)
     for k in range(1, rounds):
-        to_odd = swap(own)
-        own, kept = tails_step(ODD, k, to_odd, kept, state)
+        last = k == rounds - 1
+        own, kept = tails_step(ODD, to_odd, kept, state)
         arrived = to_even
-        to_even = send(own, 1 if k < rounds - 1 else 1 - rounds, ODD)
+        to_even = send(own, 1 - rounds if last else 1, ODD)
         state = heads_step(k, kept, state)
-        own, kept = tails_step(EVEN, k, arrived, kept, state)
-    to_odd = send(own, 1 - rounds, EVEN)
-    head, hacc = call(last_heads(tasks), [VMEM] * 7, [block, row], [], [state[0], state[1], state[5]] + kept, "heads_last")
-    tail, tacc = call(pick_tails(width), [VMEM] * 2, [block, row], [], [to_even, to_odd], "pick_tails")
+        own, kept = tails_step(EVEN, arrived, kept, state)
+        to_odd = send(own, 1 - rounds, EVEN) if last else swap(own)
+    head, hacc = call(last_heads(tasks), [VMEM] * 7, [block, row], [], [state[0], state[1], state[5]] + kept)
+    tail, tacc = call(pick_tails(width), [VMEM] * 2, [block, row], [], [to_even, to_odd])
     return head.T, tail.T, hacc.reshape(rows), tacc.reshape(rows)
 
 
 def solution(mesh):
     split, edge = P(("blk", "help"), None), P(None, ("blk", "help"), None, None)
     flat = P(("blk", "help"))
+
     return jax.shard_map(
         on_device,
         mesh=mesh,

time: 60.3 us -> 60.3 us (level)
  no operation moved by 1% of the time
where the time goes in v3:
time: 60.3 us; the launch traced here: 59.2 us
  waiting for transfers between devices  29.8 us (49%)
  Pallas kernels  21.8 us (36%)
  starting transfers between devices  6.75 us (11%)
  between operations  0.82 us (1%)
    ppermute x5, waiting for transfers between devices, send(): lax.ppermute(block, 'blk', [(i, (i + distance) % n) for i in range(mine,...  29.5 us
    pallas_call x14, Pallas kernels, call(): pl.pallas_call(body, in_specs=ins, out_specs=[VMEM] * len(outs), out_shap...  21.8 us
    ppermute x5, starting transfers between devices, send(): lax.ppermute(block, 'blk', [(i, (i + distance) % n) for i in range(mine,...  6.47 us
  transfers between devices with their start and end apart: 8, of which 7 were waited for; matrix products, arithmetic and copies ran while one was open for 0% of the time, Pallas kernels for 22%

profile of v3, /device:TPU:0, one launch (start us, length us, event | category | flops | bytes accessed | tf_op | source)
XLA Modules:
  0.0 59.2 jit_solution(8667774464431491276)
XLA Ops:
  0.6 0.1 shard_map.120
  0.8 4.1 %shard_map.121 = (f32[408,128]{1,0:T(8,128)S(1)}, bf16[400,128]{1,0:T(8,128)(2,1)S(1)}, bf16[400,128]{1,0:T(8,128)(2,1)S(1)}, bf16[128,640]{1,0:T(8,128)(2,1)S(1...) custom-call(s32[1,4]{1,0:T(1,128)} %bitcast.13, ...), custom_call_target="tpu_custom_call", output_to_operand_aliasing={{1}: (9, {}), {2}: (10, {}), {3}: (11, {}), {4}: (12, {}), ... | custom-call | flops 1000000000 | bytes 1048576 | tf_op jit(solution)/shard_map/pallas_call | solution.py:197
  5.0 0.1 collective-permute-start
  5.1 1.3 %collective-permute-start.2 = (f32[408,128]{1,0:T(8,128)S(1)}, f32[408,128]{1,0:T(8,128)S(1)}, u32[]{:S(2)}, u32[]{:S(2)}) collective-permute-start(f32[408,128]{1,0:T(8,128)S(1)} %get-tuple-element.118), channel_id=1, source_target_pairs={{2,4},{6,8},{10,12},{14,16},{18,20},{22,24},{26,28},{30,32},{34,36... | collective-permute-start | bytes 626696 | tf_op jit(solution)/shard_map/ppermute | solution.py:211
  6.4 0.7 %shard_map.122 = (f32[400,128]{1,0:T(8,128)S(1)}, f32[1,128]{1,0:T(1,128)S(1)}, bf16[400,640]{1,0:T(8,128)(2,1)S(1)}, bf16[400,640]{1,0:T(8,128)(2,1)S(1)}, f32[...) custom-call(s32[1,4]{1,0:T(1,128)S(1)} %bitcast.14, ...), custom_call_target="tpu_custom_call", output_to_operand_aliasing={{0}: (9, {}), {1}: (10, {}), {2}: (11, {}), {3}: (12, {}), ... | custom-call | flops 1000000000 | bytes 1048576 | tf_op jit(solution)/shard_map/pallas_call | solution.py:197
  7.1 3.6 %shard_map.124 = (f32[400,128]{1,0:T(8,128)S(1)}, f32[1,128]{1,0:T(1,128)S(1)}, bf16[400,640]{1,0:T(8,128)(2,1)S(1)}, bf16[400,640]{1,0:T(8,128)(2,1)S(1)}, f32[...) custom-call(s32[1,4]{1,0:T(1,128)S(1)} %bitcast.15, ...), custom_call_target="tpu_custom_call", output_to_operand_aliasing={{0}: (9, {}), {1}: (10, {}), {2}: (11, {}), {3}: (12, {}), ... | custom-call | flops 1000000000 | bytes 1048576 | tf_op jit(solution)/shard_map/pallas_call | solution.py:197
  10.7 8.3 %collective-permute-done.2.tail_in = f32[408,128]{1,0:T(8,128)S(1)} collective-permute-done((f32[408,128]{1,0:T(8,128)S(1)}, f32[408,128]{1,0:T(8,128)S(1)}, u32[]{:S(2)}, u32[]{:S(2)}) %collective-permute-start.2) | collective-permute-done | bytes 208928 | tf_op jit(solution)/shard_map/ppermute | solution.py:211
  19.0 1.2 %shard_map.125 = (f32[408,128]{1,0:T(8,128)S(1)}, bf16[400,128]{1,0:T(8,128)(2,1)S(1)}, bf16[400,128]{1,0:T(8,128)(2,1)S(1)}, bf16[128,640]{1,0:T(8,128)(2,1)S(1)}, bf16[128,640]{1,0:T(8,128)(2,1)S(1)}) custom-call(f32[408,128]{1,0:T(8,128)S(1)} %collective-permute-done.2.tail_in, ...), custom_call_target="tpu_custom_call", output_to_operand_aliasing={{1}: (5, {}), {2}: (6, {}), {3}: (7, {}), {4}: (8, {})} | custom-call | flops 1000000000 | bytes 1048576 | tf_op jit(solution)/shard_map/pallas_call | solution.py:197
  20.3 1.3 %collective-permute-start.1 = (f32[408,128]{1,0:T(8,128)S(1)}, f32[408,128]{1,0:T(8,128)S(1)}, u32[]{:S(2)}, u32[]{:S(2)}) collective-permute-start(f32[408,128]{1,0:T(8,128)S(1)} %get-tuple-element.117), channel_id=1, source_target_pairs={{2,4},{6,8},{10,12},{14,16},{18,20},{22,24},{26,28},{30,32},{34,36... | collective-permute-start | bytes 626696 | tf_op jit(solution)/shard_map/ppermute | solution.py:211
  21.6 0.1 collective-permute-done.3.tail_in
  21.8 3.6 %shard_map.127 = (f32[400,128]{1,0:T(8,128)S(1)}, f32[1,128]{1,0:T(1,128)S(1)}, bf16[400,640]{1,0:T(8,128)(2,1)S(1)}, bf16[400,640]{1,0:T(8,128)(2,1)S(1)}, f32[...) custom-call(s32[1,4]{1,0:T(1,128)S(1)} %bitcast.16, ...), custom_call_target="tpu_custom_call", output_to_operand_aliasing={{0}: (9, {}), {1}: (10, {}), {2}: (11, {}), {3}: (12, {}), ... | custom-call | flops 1000000000 | bytes 1048576 | tf_op jit(solution)/shard_map/pallas_call | solution.py:197
  25.4 7.7 %collective-permute-done.1.tail_in = f32[408,128]{1,0:T(8,128)S(1)} collective-permute-done((f32[408,128]{1,0:T(8,128)S(1)}, f32[408,128]{1,0:T(8,128)S(1)}, u32[]{:S(2)}, u32[]{:S(2)}) %collective-permute-start.1) | collective-permute-done | bytes 208928 | tf_op jit(solution)/shard_map/ppermute | solution.py:211
  33.1 1.2 %shard_map.128 = (f32[408,128]{1,0:T(8,128)S(1)}, bf16[400,128]{1,0:T(8,128)(2,1)S(1)}, bf16[400,128]{1,0:T(8,128)(2,1)S(1)}, bf16[128,640]{1,0:T(8,128)(2,1)S(1)}, bf16[128,640]{1,0:T(8,128)(2,1)S(1)}) custom-call(f32[408,128]{1,0:T(8,128)S(1)} %collective-permute-done.1.tail_in, ...), custom_call_target="tpu_custom_call", output_to_operand_aliasing={{1}: (5, {}), {2}: (6, {}), {3}: (7, {}), {4}: (8, {})} | custom-call | flops 1000000000 | bytes 1048576 | tf_op jit(solution)/shard_map/pallas_call | solution.py:197
  34.5 1.3 %collective-permute-start.5 = (f32[408,128]{1,0:T(8,128)S(1)}, f32[408,128]{1,0:T(8,128)S(1)}, u32[]{:S(2)}, u32[]{:S(2)}) collective-permute-start(f32[408,128]{1,0:T(8,128)S(1)} %get-tuple-element.161), channel_id=1, source_target_pairs={{2,4},{6,8},{10,12},{14,16},{18,20},{22,24},{26,28},{30,32},{34,36... | collective-permute-start | bytes 626696 | tf_op jit(solution)/shard_map/ppermute | solution.py:211
  35.8 0.1 collective-permute-done.4.tail_in
  35.9 3.6 %shard_map.130 = (f32[400,128]{1,0:T(8,128)S(1)}, f32[1,128]{1,0:T(1,128)S(1)}, bf16[400,640]{1,0:T(8,128)(2,1)S(1)}, bf16[400,640]{1,0:T(8,128)(2,1)S(1)}, f32[...) custom-call(s32[1,4]{1,0:T(1,128)S(1)} %bitcast.17, ...), custom_call_target="tpu_custom_call", output_to_operand_aliasing={{0}: (9, {}), {1}: (10, {}), {2}: (11, {}), {3}: (12, {}), ... | custom-call | flops 1000000000 | bytes 1048576 | tf_op jit(solution)/shard_map/pallas_call | solution.py:197
  39.5 7.8 %collective-permute-done.5.tail_in = f32[408,128]{1,0:T(8,128)S(1)} collective-permute-done((f32[408,128]{1,0:T(8,128)S(1)}, f32[408,128]{1,0:T(8,128)S(1)}, u32[]{:S(2)}, u32[]{:S(2)}) %collective-permute-start.5) | collective-permute-done | bytes 208928 | tf_op jit(solution)/shard_map/ppermute | solution.py:211
  47.3 1.2 %shard_map.131 = (f32[408,128]{1,0:T(8,128)S(1)}, bf16[400,128]{1,0:T(8,128)(2,1)S(1)}, bf16[400,128]{1,0:T(8,128)(2,1)S(1)}, bf16[128,640]{1,0:T(8,128)(2,1)S(1)}, bf16[128,640]{1,0:T(8,128)(2,1)S(1)}) custom-call(f32[408,128]{1,0:T(8,128)S(1)} %collective-permute-done.5.tail_in, ...), custom_call_target="tpu_custom_call", output_to_operand_aliasing={{1}: (5, {}), {2}: (6, {}), {3}: (7, {}), {4}: (8, {})} | custom-call | flops 1000000000 | bytes 1048576 | tf_op jit(solution)/shard_map/pallas_call | solution.py:197
  48.6 1.3 %collective-permute-start.7 = (f32[408,128]{1,0:T(8,128)S(1)}, f32[408,128]{1,0:T(8,128)S(1)}, u32[]{:S(2)}, u32[]{:S(2)}) collective-permute-start(f32[408,128]{1,0:T(8,128)S(1)} %get-tuple-element.172), channel_id=1, source_target_pairs={{0,250},{4,254},{8,2},{12,6},{16,10},{20,14},{24,18},{28,22},{32,2... | collective-permute-start | bytes 626696 | tf_op jit(solution)/shard_map/ppermute | solution.py:211
  49.9 1.3 %collective-permute-start.6 = (f32[408,128]{1,0:T(8,128)S(1)}, f32[408,128]{1,0:T(8,128)S(1)}, u32[]{:S(2)}, u32[]{:S(2)}) collective-permute-start(f32[408,128]{1,0:T(8,128)S(1)} %get-tuple-element.171), channel_id=1, source_target_pairs={{2,252},{6,0},{10,4},{14,8},{18,12},{22,16},{26,20},{30,24},{34,28... | collective-permute-start | bytes 626696 | tf_op jit(solution)/shard_map/ppermute | solution.py:211
  51.2 1.7 %shard_map.132 = (f32[400,128]{1,0:T(8,128)}, f32[1,128]{1,0:T(1,128)}) custom-call(f32[400,128]{1,0:T(8,128)S(1)} %get-tuple-element.158.head, f32[1,128]{1,0:T(1,128)S(1)} %get-tuple-element.159.hacc, bf16[400,640]{1,0:T(8,128)(2,1)S(1)} %get-tuple-element.160.rel_in, bf16[400,128]{1,0:T(8,128)(2,1)S(1)} %get-tuple-element.166.thi, ...), custom_call_target="tpu_custom_call" | custom-call | flops 1000000000 | bytes 1048576 | tf_op jit(solution)/shard_map/pallas_call | solution.py:197
  52.9 0.9 %collective-permute-done.7.from_even = f32[408,128]{1,0:T(8,128)S(1)} collective-permute-done((f32[408,128]{1,0:T(8,128)S(1)}, f32[408,128]{1,0:T(8,128)S(1)}, u32[]{:S(2)}, u32[]{:S(2)}) %collective-permute-start.7) | collective-permute-done | bytes 208928 | tf_op jit(solution)/shard_map/ppermute | solution.py:211
  53.7 4.8 %collective-permute-done.6.from_odd = f32[408,128]{1,0:T(8,128)S(1)} collective-permute-done((f32[408,128]{1,0:T(8,128)S(1)}, f32[408,128]{1,0:T(8,128)S(1)}, u32[]{:S(2)}, u32[]{:S(2)}) %collective-permute-start.6) | collective-permute-done | bytes 208928 | tf_op jit(solution)/shard_map/ppermute | solution.py:211
  58.5 0.7 %shard_map.133 = (f32[400,128]{1,0:T(8,128)}, f32[1,128]{1,0:T(1,128)}) custom-call(f32[408,128]{1,0:T(8,128)S(1)} %collective-permute-done.6.from_odd, f32[408,128]{1,0:T(8,128)S(1)} %collective-permute-done.7.from_even), custom_call_target="tpu_custom_call" | custom-call | flops 1000000000 | bytes 1048576 | tf_op jit(solution)/shard_map/pallas_call | solution.py:197
  (10 shorter events, 0.3 us)
Async XLA Ops:
  0.8 5.6 %copy-start = (s32[4,1,5]{2,1,0:T(1,128)S(1)}, s32[4,1,5]{2,1,0:T(1,128)}, u32[]{:S(2)}) copy-start(s32[4,1,5]{2,1,0:T(1,128)} %rel_ids.7) | copy-start | bytes 244
  0.8 5.6 %copy-start.1 = (s32[4,1]{0,1:T(1,128)S(1)}, s32[4,1]{0,1:T(1,128)}, u32[]{:S(2)}) copy-start(s32[4,1]{0,1:T(1,128)} %param.14) | copy-start | bytes 52
  5.0 2.1 %collective-permute-start = (f32[408,128]{1,0:T(8,128)S(1)}, f32[408,128]{1,0:T(8,128)S(1)}, u32[]{:S(2)}, u32[]{:S(2)}) collective-permute-start(f32[408,128]{1,0:T(8,128)S(1)} %get-tuple-element.101), channel_id=1, source_target_pairs={{0,2},{2,0},{4,6},{6,4},{8,10},{10,8},{12,14},{14,12},{16,18},{18,... | collective-permute-start | bytes 626696 | tf_op jit(solution)/shard_map/ppermute | solution.py:215
  5.1 13.9 %collective-permute-start.2 = (f32[408,128]{1,0:T(8,128)S(1)}, f32[408,128]{1,0:T(8,128)S(1)}, u32[]{:S(2)}, u32[]{:S(2)}) collective-permute-start(f32[408,128]{1,0:T(8,128)S(1)} %get-tuple-element.118), channel_id=1, source_target_pairs={{2,4},{6,8},{10,12},{14,16},{18,20},{22,24},{26,28},{30,32},{34,36... | collective-permute-start | bytes 626696 | tf_op jit(solution)/shard_map/ppermute | solution.py:211
  20.2 1.5 %collective-permute-start.3 = (f32[408,128]{1,0:T(8,128)S(1)}, f32[408,128]{1,0:T(8,128)S(1)}, u32[]{:S(2)}, u32[]{:S(2)}) collective-permute-start(f32[408,128]{1,0:T(8,128)S(1)} %get-tuple-element.130), channel_id=1, source_target_pairs={{0,2},{2,0},{4,6},{6,4},{8,10},{10,8},{12,14},{14,12},{16,18},{18,... | collective-permute-start | bytes 626696 | tf_op jit(solution)/shard_map/ppermute | solution.py:215
  20.3 12.8 %collective-permute-start.1 = (f32[408,128]{1,0:T(8,128)S(1)}, f32[408,128]{1,0:T(8,128)S(1)}, u32[]{:S(2)}, u32[]{:S(2)}) collective-permute-start(f32[408,128]{1,0:T(8,128)S(1)} %get-tuple-element.117), channel_id=1, source_target_pairs={{2,4},{6,8},{10,12},{14,16},{18,20},{22,24},{26,28},{30,32},{34,36... | collective-permute-start | bytes 626696 | tf_op jit(solution)/shard_map/ppermute | solution.py:211
  34.4 1.5 %collective-permute-start.4 = (f32[408,128]{1,0:T(8,128)S(1)}, f32[408,128]{1,0:T(8,128)S(1)}, u32[]{:S(2)}, u32[]{:S(2)}) collective-permute-start(f32[408,128]{1,0:T(8,128)S(1)} %get-tuple-element.146), channel_id=1, source_target_pairs={{0,2},{2,0},{4,6},{6,4},{8,10},{10,8},{12,14},{14,12},{16,18},{18,... | collective-permute-start | bytes 626696 | tf_op jit(solution)/shard_map/ppermute | solution.py:215
  34.5 12.8 %collective-permute-start.5 = (f32[408,128]{1,0:T(8,128)S(1)}, f32[408,128]{1,0:T(8,128)S(1)}, u32[]{:S(2)}, u32[]{:S(2)}) collective-permute-start(f32[408,128]{1,0:T(8,128)S(1)} %get-tuple-element.161), channel_id=1, source_target_pairs={{2,4},{6,8},{10,12},{14,16},{18,20},{22,24},{26,28},{30,32},{34,36... | collective-permute-start | bytes 626696 | tf_op jit(solution)/shard_map/ppermute | solution.py:211
  48.6 5.2 %collective-permute-start.7 = (f32[408,128]{1,0:T(8,128)S(1)}, f32[408,128]{1,0:T(8,128)S(1)}, u32[]{:S(2)}, u32[]{:S(2)}) collective-permute-start(f32[408,128]{1,0:T(8,128)S(1)} %get-tuple-element.172), channel_id=1, source_target_pairs={{0,250},{4,254},{8,2},{12,6},{16,10},{20,14},{24,18},{28,22},{32,2... | collective-permute-start | bytes 626696 | tf_op jit(solution)/shard_map/ppermute | solution.py:211
  49.9 8.6 %collective-permute-start.6 = (f32[408,128]{1,0:T(8,128)S(1)}, f32[408,128]{1,0:T(8,128)S(1)}, u32[]{:S(2)}, u32[]{:S(2)}) collective-permute-start(f32[408,128]{1,0:T(8,128)S(1)} %get-tuple-element.171), channel_id=1, source_target_pairs={{2,252},{6,0},{10,4},{14,8},{18,12},{22,16},{26,20},{30,24},{34,28... | collective-permute-start | bytes 626696 | tf_op jit(solution)/shard_map/ppermute | solution.py:211

commit v4 on v3

v4 whole, which is shorter than its diff:
```python
import jax
import jax.numpy as jnp
from jax import lax
from jax.experimental import pallas as pl
from jax.experimental.pallas import tpu as pltpu
from jax.sharding import PartitionSpec as P


NEG_WEIGHT = 0.0625
LEARN_RATE = 0.1
F32, BF16, I32 = jnp.float32, jnp.bfloat16, jnp.int32
LANES = 128
ODD, EVEN = 1, 0
VMEM = pl.BlockSpec(memory_space=pltpu.VMEM)
SMEM = pl.BlockSpec(memory_space=pltpu.SMEM)
HBM = pl.BlockSpec(memory_space=pltpu.HBM)
NN, NT, TN = ((1,), (0,)), ((1,), (1,)), ((0,), (0,))


def role():
    return lax.rem(lax.axis_index("blk"), 2)


def dot(a, b, dims):
    return lax.dot_general(a, b, (dims, ((), ())), preferred_element_type=F32)


def hi_lo(x):
    hi = x.astype(BF16)
    return hi, (x - hi.astype(F32)).astype(BF16)


def cols(s):
    return pl.ds(s * LANES, LANES)


def one_hot(rows):
    which = lax.broadcasted_iota(I32, (LANES, LANES), 0)
    parts = [jnp.where(rows[r : r + 1, :] == which, 1.0, 0.0).astype(BF16) for r in range(rows.shape[0])]
    return jnp.concatenate(parts, axis=1)


def make_labels(labels_ref, he, te, source, target, tasks):
    for s in range(tasks):
        labels_ref[target + s] = dot(one_hot(te[source + s]), one_hot(he[source + s]), NT)


def rel_copies(rel_ids, rel_ref, rel_buf, sem, k, tasks):
    copies = []
    for s in range(tasks):
        start = pl.multiple_of((rel_ids[k, 0, s] // LANES) * LANES, LANES)
        copies.append(pltpu.make_async_copy(rel_ref.at[:, pl.ds(start, LANES)], rel_buf.at[k * tasks + s], sem.at[k * tasks + s]))
    return copies


def scale_heads(head, lanes, rel_buf, k, shi, slo, rel_out, tasks):
    for s in range(tasks):
        pick = (lax.broadcasted_iota(I32, (LANES, LANES), 0) == lanes[k * tasks + s, 0:1, :]).astype(F32).astype(BF16)
        rel = dot(rel_buf[k * tasks + s], pick, NN)
        rel_out[:, cols(s)] = rel.astype(BF16)
        shi[:, cols(s)], slo[:, cols(s)] = hi_lo(head * rel)


def adagrad(block, state, grad):
    state = state + jnp.sum(grad * grad, axis=0, keepdims=True) * (1.0 / block.shape[0])
    return block - grad * (LEARN_RATE / jnp.sqrt(state)), state


def tail_step(tail, state, shi_ref, slo_ref, labels_ref, label_row, live_ref, live_row, kept, tail_out, tasks):
    thi_ref, tlo_ref, chi_ref, clo_ref = kept
    width = tail.shape[0]
    thi, tlo = hi_lo(tail)
    thi_ref[...], tlo_ref[...] = thi, tlo
    shi, slo = shi_ref[...], slo_ref[...]
    scores = dot(thi, shi, TN) + dot(tlo, shi, TN) + dot(thi, slo, TN)
    for s in range(tasks):
        score = scores[:, s * LANES : (s + 1) * LANES]
        coefficient = NEG_WEIGHT * (0.5 * jnp.tanh(0.5 * score) + 0.5) - labels_ref[label_row + s]
        chi_ref[:, cols(s)], clo_ref[:, cols(s)] = hi_lo(coefficient * live_ref[live_row + s, 0:1, :])
    chi, clo = chi_ref[...], clo_ref[...]
    grad = dot(shi, chi, NT) + dot(slo, chi, NT) + dot(shi, clo, NT)
    tail, state = adagrad(tail, state, grad)
    tail_out[pl.ds(0, width), :] = tail
    tail_out[pl.ds(width, 8), :] = jnp.broadcast_to(state, (8, LANES))


def head_step(head, state, kept, rel_ref, tasks):
    thi_ref, tlo_ref, chi_ref, clo_ref = kept
    thi, tlo = thi_ref[...], tlo_ref[...]
    grad = None
    for s in range(tasks):
        chi, clo = chi_ref[:, cols(s)], clo_ref[:, cols(s)]
        term = dot(thi, chi, NN) + dot(tlo, chi, NN) + dot(thi, clo, NN)
        term = term * rel_ref[:, cols(s)].astype(F32)
        grad = term if grad is None else grad + term
    return adagrad(head, state, grad)


def first_kernel(mine, tasks, rounds):
    n_out = 15

    def body(counts_hbm, ids_hbm, head_hbm, tail_hbm, hacc_hbm, tacc_hbm, rel_ref, he_hbm, te_hbm, *refs):
        outs, scratch = refs[-7 - n_out : -7], refs[-7:]
        tail_out, kept, (head, hacc, shi, slo, rel_out), (he, te, rel_buf, lanes, live) = outs[0], outs[1:5], outs[5:10], outs[10:]
        counts, rel_ids, tail, tacc, labels_ref, rel_sem, sem = scratch

        @pl.when(role() == mine)
        def _():
            pairs = ((ids_hbm, rel_ids), (counts_hbm, counts), (he_hbm, he), (te_hbm, te), (head_hbm, head), (tail_hbm, tail),
                     (hacc_hbm, hacc), (tacc_hbm, tacc))
            copies = [pltpu.make_async_copy(src, dst, sem.at[i]) for i, (src, dst) in enumerate(pairs)]
            for copy in copies:
                copy.start()
            copies[0].wait()
            rels = [rel_copies(rel_ids, rel_ref, rel_buf, rel_sem, k, tasks) for k in range(rounds)]
            for group in rels:
                for copy in group:
                    copy.start()
            for copy in copies[1:4]:
                copy.wait()
            make_labels(labels_ref, he, te, 0, 0, tasks)
            for k in range(rounds):
                for s in range(tasks):
                    lanes[k * tasks + s] = jnp.full(lanes.shape[1:], lax.rem(rel_ids[k, 0, s], LANES), I32)
                    live[k * tasks + s] = jnp.full(live.shape[1:], jnp.where(s < counts[0, k], 1.0, 0.0), F32)
            for copy in rels[0] + copies[4:]:
                copy.wait()
            scale_heads(head[...], lanes, rel_buf, 0, shi, slo, rel_out, tasks)
            tail_step(tail[...], tacc[...], shi, slo, labels_ref, 0, live, 0, kept, tail_out, tasks)
            for group in rels[1:]:
                for copy in group:
                    copy.wait()

    return body


def tail_kernel(mine, k, tasks, width):
    def body(tail_in, shi, slo, labels_ref, live, *refs):
        outs = refs[4:]

        @pl.when(role() == mine)
        def _():
            tail, state = tail_in[pl.ds(0, width), :], tail_in[pl.ds(width, 1), :]
            tail_step(tail, state, shi, slo, labels_ref, (k - 1) * tasks, live, k * tasks, outs[1:5], outs[0], tasks)

    return body


LABEL_ROUNDS = {(0, ODD): (1,), (1, ODD): (2, 3), (1, EVEN): (1, 2), (3, EVEN): (3,)}


def head_kernel(m, tasks, rounds):
    def body(he, te, rel_buf, lanes, thi, tlo, chi, clo, *refs):
        ins, (head_out, hacc_out, shi, slo, rel_out, labels_ref) = refs[:5], refs[-6:]
        head, hacc, rel_in = ins[0], ins[1], ins[4]
        for mine, done in ((ODD, m), (EVEN, m - 1)):
            if not 0 <= done < rounds - 1:
                continue

            @pl.when(role() == mine)
            def _():
                new, state = head_step(head[...], hacc[...], (thi, tlo, chi, clo), rel_in, tasks)
                head_out[...] = new
                hacc_out[...] = state
                scale_heads(new, lanes, rel_buf, done + 1, shi, slo, rel_out, tasks)
                for k in LABEL_ROUNDS.get((m, mine), ()):
                    make_labels(labels_ref, he, te, k * tasks, (k - 1) * tasks, tasks)

    return body


def last_heads(tasks):
    def body(head, hacc, rel_in, thi, tlo, chi, clo, head_out, hacc_out):
        head_out[...], hacc_out[...] = head_step(head[...], hacc[...], (thi, tlo, chi, clo), rel_in, tasks)

    return body


def pick_tails(width):
    def body(from_odd, from_even, tail_out, tacc_out):
        for mine, ref in ((EVEN, from_odd), (ODD, from_even)):
            @pl.when(role() == mine)
            def _():
                tail_out[...] = ref[pl.ds(0, width), :]
                tacc_out[...] = ref[pl.ds(width, 1), :]

    return body


def call(body, ins, outs, scratch, args, alias=None):
    args = [pltpu.with_memory_space_constraint(a, pltpu.HBM) if spec is HBM else a for spec, a in zip(ins, args)]
    return pl.pallas_call(
        body,
        in_specs=ins,
        out_specs=[VMEM] * len(outs),
        out_shape=[jax.ShapeDtypeStruct(*o) for o in outs],
        scratch_shapes=scratch,
        input_output_aliases=alias or {},
        compiler_params=pltpu.CompilerParams(vmem_limit_bytes=16 << 20),
        cost_estimate=pl.CostEstimate(flops=10**9, bytes_accessed=1 << 20, transcendentals=0),
    )(*args)


def send(block, distance, mine):
    n = lax.axis_size("blk")
    return lax.ppermute(block, "blk", [(i, (i + distance) % n) for i in range(mine, n, 2)])


def send_or_swap(block, distance, mine):
    n = lax.axis_size("blk")
    return lax.ppermute(block, "blk", [(i, (i + distance) % n if i % 2 == mine else i ^ 1) for i in range(n)])


def on_device(heads, tails, head_acc, tail_acc, relations, counts, rel_ids, head_edges, tail_edges):
    rounds, _, tasks, edges = head_edges.shape
    rows, width = heads.shape
    head, tail, rels = heads.T, tails.T, relations.T
    hacc, tacc, counts = head_acc.reshape(1, rows), tail_acc.reshape(1, rows), counts.T
    slots, groups, wide = rounds * tasks, edges // LANES, tasks * rows
    he, te = head_edges.reshape(slots, groups, LANES), tail_edges.reshape(slots, groups, LANES)
    block, packed, row = ((width, rows), F32), ((width + 8, rows), F32), ((1, rows), F32)
    coeff, scaled, half = ((rows, wide), BF16), ((width, wide), BF16), ((width, rows), BF16)
    table = ((slots - tasks, rows, rows), F32)
    kept_shapes = [half, half, coeff, coeff]
    state_shapes = [block, row, scaled, scaled, scaled]
    edge = ((slots, groups, LANES), I32)
    fixed_shapes = [edge, edge, ((slots, width, LANES), BF16), ((slots, 8, rows), I32), ((slots, 8, rows), F32)]

    def first(mine, carried):
        return call(
            first_kernel(mine, tasks, rounds), [HBM] * 9 + [VMEM] * len(carried),
            [packed] + kept_shapes + state_shapes + fixed_shapes,
            [pltpu.SMEM(counts.shape, I32), pltpu.SMEM(rel_ids.shape, I32), pltpu.VMEM(*block), pltpu.VMEM(*row),
             pltpu.VMEM((tasks, rows, rows), F32), pltpu.SemaphoreType.DMA((slots,)), pltpu.SemaphoreType.DMA((8,))],
            [counts, rel_ids, head, tail, hacc, tacc, rels, he, te] + carried,
            {9 + i: 1 + i for i in range(len(carried))})

    def tails_step(mine, k, tail_in, kept, state):
        out = call(
            tail_kernel(mine, k, tasks, width), [VMEM] * 9, [packed] + kept_shapes, [],
            [tail_in, state[2], state[3], state[5], fixed[4]] + kept, {5 + i: 1 + i for i in range(4)})
        return out[0], list(out[1:])

    def heads_step(m, kept, state):
        return list(call(
            head_kernel(m, tasks, rounds), [VMEM] * (8 + len(state)), state_shapes + [table], [],
            list(fixed[:4]) + kept + state, {8 + i: i for i in range(len(state))}))

    out = first(ODD, [])
    to_even = send(out[0], 1, ODD)
    out = first(EVEN, list(out[1:]))
    own, kept, state, fixed = out[0], list(out[1:5]), list(out[5:10]), list(out[10:])
    to_odd = send_or_swap(own, 1, EVEN)
    state = heads_step(0, kept, state)
    for k in range(1, rounds):
        distance = 1 if k < rounds - 1 else 1 - rounds
        own, kept = tails_step(ODD, k, to_odd, kept, state)
        arrived = to_even
        to_even = send_or_swap(own, distance, ODD)
        state = heads_step(k, kept, state)
        own, kept = tails_step(EVEN, k, arrived, kept, state)
        to_odd = send_or_swap(own, distance, EVEN)
    head, hacc = call(last_heads(tasks), [VMEM] * 7, [block, row], [], [state[0], state[1], state[4]] + kept)
    tail, tacc = call(pick_tails(width), [VMEM] * 2, [block, row], [], [to_even, to_odd])
    return head.T, tail.T, hacc.reshape(rows), tacc.reshape(rows)


def solution(mesh):
    split, edge = P(("blk", "help"), None), P(None, ("blk", "help"), None, None)
    flat = P(("blk", "help"))

    return jax.shard_map(
        on_device,
        mesh=mesh,
        in_specs=(split, split, flat, flat, P(), P(None, ("blk", "help")), P(None, ("blk", "help"), None), edge, edge),
        out_specs=(split, split, flat, flat),
        check_vma=False,
    )
```

time: 60.3 us -> 54.4 us (0.902)
  the two profiles are of different devices: /device:TPU:0 before, /device:TPU:126 now
where the time goes in v4:
time: 54.4 us; the launch traced here: 54.3 us
  waiting for transfers between devices  28.4 us (52%)
  Pallas kernels  16.2 us (30%)
  starting transfers between devices  8.88 us (16%)
  between operations  0.73 us (1%)
    ppermute x7, waiting for transfers between devices, send_or_swap(): lax.ppermute(block, 'blk', [(i, (i + distance) % n if i % 2 == mine else...  23.5 us
    pallas_call x14, Pallas kernels, call(): pl.pallas_call(body, in_specs=ins, out_specs=[VMEM] * len(outs), out_shap...  16.2 us
    ppermute x7, starting transfers between devices, send_or_swap(): lax.ppermute(block, 'blk', [(i, (i + distance) % n if i % 2 == mine else...  7.58 us
    ppermute x1, waiting for transfers between devices, send(): lax.ppermute(block, 'blk', [(i, (i + distance) % n) for i in range(mine,...  4.92 us
    ppermute x1, starting transfers between devices, send(): lax.ppermute(block, 'blk', [(i, (i + distance) % n) for i in range(mine,...  1.29 us
  transfers between devices with their start and end apart: 8, of which 7 were waited for; matrix products, arithmetic and copies ran while one was open for 0% of the time, Pallas kernels for 13%

profile of v4, /device:TPU:126, one launch (start us, length us, event | category | flops | bytes accessed | tf_op | source)
XLA Modules:
  0.0 54.3 jit_solution(13803721003247928202)
XLA Ops:
  0.6 0.3 shard_map.120
  0.9 4.3 %shard_map.121 = (f32[408,128]{1,0:T(8,128)S(1)}, bf16[400,128]{1,0:T(8,128)(2,1)S(1)}, bf16[400,128]{1,0:T(8,128)(2,1)S(1)}, bf16[128,640]{1,0:T(8,128)(2,1)S(1...) custom-call(s32[1,4]{1,0:T(1,128)} %bitcast.23, ...), custom_call_target="tpu_custom_call", output_to_operand_aliasing={{1}: (9, {}), {2}: (10, {}), {3}: (11, {}), {4}: (12, {}), ... | custom-call | flops 1000000000 | bytes 1048576 | tf_op jit(solution)/shard_map/pallas_call | solution.py:192
  5.2 0.1 collective-permute-start
  5.3 1.3 %collective-permute-start.2 = (f32[408,128]{1,0:T(8,128)S(1)}, f32[408,128]{1,0:T(8,128)S(1)}, u32[]{:S(2)}, u32[]{:S(2)}) collective-permute-start(f32[408,128]{1,0:T(8,128)S(1)} %get-tuple-element.125), channel_id=1, source_target_pairs={{2,4},{6,8},{10,12},{14,16},{18,20},{22,24},{26,28},{30,32},{34,36... | collective-permute-start | bytes 626696 | tf_op jit(solution)/shard_map/ppermute | solution.py:206
  6.6 0.1 collective-permute-done.tail_in
  6.8 2.2 %shard_map.124 = (f32[400,128]{1,0:T(8,128)S(1)}, f32[1,128]{1,0:T(1,128)S(1)}, bf16[400,640]{1,0:T(8,128)(2,1)S(1)}, bf16[400,640]{1,0:T(8,128)(2,1)S(1)}, bf16...) custom-call(s32[20,8,128]{2,1,0:T(8,128)S(1)} %get-tuple-element.106, ...), custom_call_target="tpu_custom_call", output_to_operand_aliasing={{0}: (8, {}), {1}: (9, {}), {2}: (10, {}), {3}: (11, {}), {... | custom-call | flops 1000000000 | bytes 1048576 | tf_op jit(solution)/shard_map/pallas_call | solution.py:192
  9.0 4.9 %collective-permute-done.2.tail_in = f32[408,128]{1,0:T(8,128)S(1)} collective-permute-done((f32[408,128]{1,0:T(8,128)S(1)}, f32[408,128]{1,0:T(8,128)S(1)}, u32[]{:S(2)}, u32[]{:S(2)}) %collective-permute-start.2) | collective-permute-done | bytes 208928 | tf_op jit(solution)/shard_map/ppermute | solution.py:206
  13.9 1.2 %shard_map.125 = (f32[408,128]{1,0:T(8,128)S(1)}, bf16[400,128]{1,0:T(8,128)(2,1)S(1)}, bf16[400,128]{1,0:T(8,128)(2,1)S(1)}, bf16[128,640]{1,0:T(8,128)(2,1)S(1)}, bf16[128,640]{1,0:T(8,128)(2,1)S(1)}) custom-call(f32[408,128]{1,0:T(8,128)S(1)} %collective-permute-done.2.tail_in, ...), custom_call_target="tpu_custom_call", output_to_operand_aliasing={{1}: (5, {}), {2}: (6, {}), {3}: (7, {}), {4}: (8, {})} | custom-call | flops 1000000000 | bytes 1048576 | tf_op jit(solution)/shard_map/pallas_call | solution.py:192
  15.2 1.6 %collective-permute-start.3 = (f32[408,128]{1,0:T(8,128)S(1)}, f32[408,128]{1,0:T(8,128)S(1)}, u32[]{:S(2)}, u32[]{:S(2)}) collective-permute-start(f32[408,128]{1,0:T(8,128)S(1)} %get-tuple-element.136), channel_id=1, source_target_pairs={{0,2},{2,0},{4,6},{6,4},{8,10},{10,8},{12,14},{14,12},{16,18},{18,... | collective-permute-start | bytes 626696 | tf_op jit(solution)/shard_map/ppermute | solution.py:211
  16.7 0.1 collective-permute-start.1
  16.8 1.0 %collective-permute-done.3.tail_in = f32[408,128]{1,0:T(8,128)S(1)} collective-permute-done((f32[408,128]{1,0:T(8,128)S(1)}, f32[408,128]{1,0:T(8,128)S(1)}, u32[]{:S(2)}, u32[]{:S(2)}) %collective-permute-start.3) | collective-permute-done | bytes 208928 | tf_op jit(solution)/shard_map/ppermute | solution.py:211
  17.8 1.5 %shard_map.127 = (f32[400,128]{1,0:T(8,128)S(1)}, f32[1,128]{1,0:T(1,128)S(1)}, bf16[400,640]{1,0:T(8,128)(2,1)S(1)}, bf16[400,640]{1,0:T(8,128)(2,1)S(1)}, bf16...) custom-call(s32[20,8,128]{2,1,0:T(8,128)S(1)} %get-tuple-element.106, ...), custom_call_target="tpu_custom_call", output_to_operand_aliasing={{0}: (8, {}), {1}: (9, {}), {2}: (10, {}), {3}: (11, {}), {... | custom-call | flops 1000000000 | bytes 1048576 | tf_op jit(solution)/shard_map/pallas_call | solution.py:192
  19.3 4.2 %collective-permute-done.1.tail_in = f32[408,128]{1,0:T(8,128)S(1)} collective-permute-done((f32[408,128]{1,0:T(8,128)S(1)}, f32[408,128]{1,0:T(8,128)S(1)}, u32[]{:S(2)}, u32[]{:S(2)}) %collective-permute-start.1) | collective-permute-done | bytes 208928 | tf_op jit(solution)/shard_map/ppermute | solution.py:211
  23.5 1.2 %shard_map.128 = (f32[408,128]{1,0:T(8,128)S(1)}, bf16[400,128]{1,0:T(8,128)(2,1)S(1)}, bf16[400,128]{1,0:T(8,128)(2,1)S(1)}, bf16[128,640]{1,0:T(8,128)(2,1)S(1)}, bf16[128,640]{1,0:T(8,128)(2,1)S(1)}) custom-call(f32[408,128]{1,0:T(8,128)S(1)} %collective-permute-done.1.tail_in, ...), custom_call_target="tpu_custom_call", output_to_operand_aliasing={{1}: (5, {}), {2}: (6, {}), {3}: (7, {}), {4}: (8, {})} | custom-call | flops 1000000000 | bytes 1048576 | tf_op jit(solution)/shard_map/pallas_call | solution.py:192
  24.7 1.5 %collective-permute-start.4 = (f32[408,128]{1,0:T(8,128)S(1)}, f32[408,128]{1,0:T(8,128)S(1)}, u32[]{:S(2)}, u32[]{:S(2)}) collective-permute-start(f32[408,128]{1,0:T(8,128)S(1)} %get-tuple-element.151), channel_id=1, source_target_pairs={{0,2},{2,0},{4,6},{6,4},{8,10},{10,8},{12,14},{14,12},{16,18},{18,... | collective-permute-start | bytes 626696 | tf_op jit(solution)/shard_map/ppermute | solution.py:211
  26.2 0.1 collective-permute-start.5
  26.3 1.0 %collective-permute-done.4.tail_in = f32[408,128]{1,0:T(8,128)S(1)} collective-permute-done((f32[408,128]{1,0:T(8,128)S(1)}, f32[408,128]{1,0:T(8,128)S(1)}, u32[]{:S(2)}, u32[]{:S(2)}) %collective-permute-start.4) | collective-permute-done | bytes 208928 | tf_op jit(solution)/shard_map/ppermute | solution.py:211
  27.3 1.9 %shard_map.130 = (f32[400,128]{1,0:T(8,128)S(1)}, f32[1,128]{1,0:T(1,128)S(1)}, bf16[400,640]{1,0:T(8,128)(2,1)S(1)}, bf16[400,640]{1,0:T(8,128)(2,1)S(1)}, bf16...) custom-call(s32[20,8,128]{2,1,0:T(8,128)S(1)} %get-tuple-element.106, ...), custom_call_target="tpu_custom_call", output_to_operand_aliasing={{0}: (8, {}), {1}: (9, {}), {2}: (10, {}), {3}: (11, {}), {... | custom-call | flops 1000000000 | bytes 1048576 | tf_op jit(solution)/shard_map/pallas_call | solution.py:192
  29.2 3.8 %collective-permute-done.5.tail_in = f32[408,128]{1,0:T(8,128)S(1)} collective-permute-done((f32[408,128]{1,0:T(8,128)S(1)}, f32[408,128]{1,0:T(8,128)S(1)}, u32[]{:S(2)}, u32[]{:S(2)}) %collective-permute-start.5) | collective-permute-done | bytes 208928 | tf_op jit(solution)/shard_map/ppermute | solution.py:211
  32.9 1.2 %shard_map.131 = (f32[408,128]{1,0:T(8,128)S(1)}, bf16[400,128]{1,0:T(8,128)(2,1)S(1)}, bf16[400,128]{1,0:T(8,128)(2,1)S(1)}, bf16[128,640]{1,0:T(8,128)(2,1)S(1)}, bf16[128,640]{1,0:T(8,128)(2,1)S(1)}) custom-call(f32[408,128]{1,0:T(8,128)S(1)} %collective-permute-done.5.tail_in, ...), custom_call_target="tpu_custom_call", output_to_operand_aliasing={{1}: (5, {}), {2}: (6, {}), {3}: (7, {}), {4}: (8, {})} | custom-call | flops 1000000000 | bytes 1048576 | tf_op jit(solution)/shard_map/pallas_call | solution.py:192
  34.2 4.2 %collective-permute-start.6 = (f32[408,128]{1,0:T(8,128)S(1)}, f32[408,128]{1,0:T(8,128)S(1)}, u32[]{:S(2)}, u32[]{:S(2)}) collective-permute-start(f32[408,128]{1,0:T(8,128)S(1)} %get-tuple-element.175), channel_id=1, source_target_pairs={{0,2},{2,252},{4,6},{6,0},{8,10},{10,4},{12,14},{14,8},{16,18},{18... | collective-permute-start | bytes 626696 | tf_op jit(solution)/shard_map/ppermute | solution.py:211
  38.4 1.7 %shard_map.132 = (f32[400,128]{1,0:T(8,128)}, f32[1,128]{1,0:T(1,128)}) custom-call(f32[400,128]{1,0:T(8,128)S(1)} %get-tuple-element.163.head, f32[1,128]{1,0:T(1,128)S(1)} %get-tuple-element.164.hacc, bf16[400,640]{1,0:T(8,128)(2,1)S(1)} %get-tuple-element.165.rel_in, bf16[400,128]{1,0:T(8,128)(2,1)S(1)} %get-tuple-element.170.thi, ...), custom_call_target="tpu_custom_call" | custom-call | flops 1000000000 | bytes 1048576 | tf_op jit(solution)/shard_map/pallas_call | solution.py:192
  40.1 13.5 %collective-permute-done.6.from_odd = f32[408,128]{1,0:T(8,128)S(1)} collective-permute-done((f32[408,128]{1,0:T(8,128)S(1)}, f32[408,128]{1,0:T(8,128)S(1)}, u32[]{:S(2)}, u32[]{:S(2)}) %collective-permute-start.6) | collective-permute-done | bytes 208928 | tf_op jit(solution)/shard_map/ppermute | solution.py:211
  53.6 0.7 %shard_map.133 = (f32[400,128]{1,0:T(8,128)}, f32[1,128]{1,0:T(1,128)}) custom-call(f32[408,128]{1,0:T(8,128)S(1)} %collective-permute-done.6.from_odd, f32[408,128]{1,0:T(8,128)S(1)} %collective-permute-done.7.from_even), custom_call_target="tpu_custom_call" | custom-call | flops 1000000000 | bytes 1048576 | tf_op jit(solution)/shard_map/pallas_call | solution.py:192
  (6 shorter events, 0.1 us)
Async XLA Ops:
  5.2 1.5 %collective-permute-start = (f32[408,128]{1,0:T(8,128)S(1)}, f32[408,128]{1,0:T(8,128)S(1)}, u32[]{:S(2)}, u32[]{:S(2)}) collective-permute-start(f32[408,128]{1,0:T(8,128)S(1)} %get-tuple-element.110), channel_id=1, source_target_pairs={{0,2},{2,0},{4,6},{6,4},{8,10},{10,8},{12,14},{14,12},{16,18},{18,... | collective-permute-start | bytes 626696 | tf_op jit(solution)/shard_map/ppermute | solution.py:211
  5.3 8.6 %collective-permute-start.2 = (f32[408,128]{1,0:T(8,128)S(1)}, f32[408,128]{1,0:T(8,128)S(1)}, u32[]{:S(2)}, u32[]{:S(2)}) collective-permute-start(f32[408,128]{1,0:T(8,128)S(1)} %get-tuple-element.125), channel_id=1, source_target_pairs={{2,4},{6,8},{10,12},{14,16},{18,20},{22,24},{26,28},{30,32},{34,36... | collective-permute-start | bytes 626696 | tf_op jit(solution)/shard_map/ppermute | solution.py:206
  15.2 2.6 %collective-permute-start.3 = (f32[408,128]{1,0:T(8,128)S(1)}, f32[408,128]{1,0:T(8,128)S(1)}, u32[]{:S(2)}, u32[]{:S(2)}) collective-permute-start(f32[408,128]{1,0:T(8,128)S(1)} %get-tuple-element.136), channel_id=1, source_target_pairs={{0,2},{2,0},{4,6},{6,4},{8,10},{10,8},{12,14},{14,12},{16,18},{18,... | collective-permute-start | bytes 626696 | tf_op jit(solution)/shard_map/ppermute | solution.py:211
  16.7 6.7 %collective-permute-start.1 = (f32[408,128]{1,0:T(8,128)S(1)}, f32[408,128]{1,0:T(8,128)S(1)}, u32[]{:S(2)}, u32[]{:S(2)}) collective-permute-start(f32[408,128]{1,0:T(8,128)S(1)} %get-tuple-element.124), channel_id=1, source_target_pairs={{0,2},{2,4},{4,6},{6,8},{8,10},{10,12},{12,14},{14,16},{16,18},{18... | collective-permute-start | bytes 626696 | tf_op jit(solution)/shard_map/ppermute | solution.py:211
  24.7 2.6 %collective-permute-start.4 = (f32[408,128]{1,0:T(8,128)S(1)}, f32[408,128]{1,0:T(8,128)S(1)}, u32[]{:S(2)}, u32[]{:S(2)}) collective-permute-start(f32[408,128]{1,0:T(8,128)S(1)} %get-tuple-element.151), channel_id=1, source_target_pairs={{0,2},{2,0},{4,6},{6,4},{8,10},{10,8},{12,14},{14,12},{16,18},{18,... | collective-permute-start | bytes 626696 | tf_op jit(solution)/shard_map/ppermute | solution.py:211
  26.2 6.7 %collective-permute-start.5 = (f32[408,128]{1,0:T(8,128)S(1)}, f32[408,128]{1,0:T(8,128)S(1)}, u32[]{:S(2)}, u32[]{:S(2)}) collective-permute-start(f32[408,128]{1,0:T(8,128)S(1)} %get-tuple-element.166), channel_id=1, source_target_pairs={{0,2},{2,4},{4,6},{6,8},{8,10},{10,12},{12,14},{14,16},{16,18},{18... | collective-permute-start | bytes 626696 | tf_op jit(solution)/shard_map/ppermute | solution.py:211
  34.2 6.0 %collective-permute-start.7 = (f32[408,128]{1,0:T(8,128)S(1)}, f32[408,128]{1,0:T(8,128)S(1)}, u32[]{:S(2)}, u32[]{:S(2)}) collective-permute-start(f32[408,128]{1,0:T(8,128)S(1)} %get-tuple-element.176), channel_id=1, source_target_pairs={{0,250},{2,0},{4,254},{6,4},{8,2},{10,8},{12,6},{14,12},{16,10},{1... | collective-permute-start | bytes 626696 | tf_op jit(solution)/shard_map/ppermute | solution.py:211
  34.2 19.3 %collective-permute-start.6 = (f32[408,128]{1,0:T(8,128)S(1)}, f32[408,128]{1,0:T(8,128)S(1)}, u32[]{:S(2)}, u32[]{:S(2)}) collective-permute-start(f32[408,128]{1,0:T(8,128)S(1)} %get-tuple-element.175), channel_id=1, source_target_pairs={{0,2},{2,252},{4,6},{6,0},{8,10},{10,4},{12,14},{14,8},{16,18},{18... | collective-permute-start | bytes 626696 | tf_op jit(solution)/shard_map/ppermute | solution.py:211

commit v5 on v4

--- a/solution.py
+++ b/solution.py
@@ -6,7 +6,7 @@
 from jax.sharding import PartitionSpec as P
 
 
-NEG_WEIGHT = 0.0625
+HALF_NEG = 0.0625 / 2
 LEARN_RATE = 0.1
 F32, BF16, I32 = jnp.float32, jnp.bfloat16, jnp.int32
 LANES = 128
@@ -40,9 +40,10 @@
     return jnp.concatenate(parts, axis=1)
 
 
-def make_labels(labels_ref, he, te, source, target, tasks):
-    for s in range(tasks):
-        labels_ref[target + s] = dot(one_hot(te[source + s]), one_hot(he[source + s]), NT)
+def make_labels(labels_ref, he, te, gain, source, target, tasks):
+    for s in range(tasks):
+        count = dot(one_hot(te[source + s]), one_hot(he[source + s]), NT)
+        labels_ref[target + s] = gain[source + s, 0:1, :] * (1.0 - count * (1.0 / HALF_NEG))
 
 
 def rel_copies(rel_ids, rel_ref, rel_buf, sem, k, tasks):
@@ -62,46 +63,59 @@
 
 
 def adagrad(block, state, grad):
-    state = state + jnp.sum(grad * grad, axis=0, keepdims=True) * (1.0 / block.shape[0])
+    width = block.shape[0]
+    square, part = grad * grad, width // 5
+    square = (square[:part] + square[part : 2 * part]) + (square[2 * part : 3 * part] + square[3 * part : 4 * part]) + square[4 * part :]
+    state = state + jnp.sum(square, axis=0, keepdims=True) * (1.0 / width)
     return block - grad * (LEARN_RATE / jnp.sqrt(state)), state
 
 
-def tail_step(tail, state, shi_ref, slo_ref, labels_ref, label_row, live_ref, live_row, kept, tail_out, tasks):
+def tail_step(tail, state, shi_ref, slo_ref, labels_ref, label_row, gain_ref, gain_row, kept, tail_outs, tasks):
     thi_ref, tlo_ref, chi_ref, clo_ref = kept
     width = tail.shape[0]
     thi, tlo = hi_lo(tail)
     thi_ref[...], tlo_ref[...] = thi, tlo
     shi, slo = shi_ref[...], slo_ref[...]
-    scores = dot(thi, shi, TN) + dot(tlo, shi, TN) + dot(thi, slo, TN)
+    both = dot(jnp.concatenate([thi, tlo], axis=1), shi, TN)
+    scores = both[:LANES] + both[LANES:] + dot(thi, slo, TN)
     for s in range(tasks):
         score = scores[:, s * LANES : (s + 1) * LANES]
-        coefficient = NEG_WEIGHT * (0.5 * jnp.tanh(0.5 * score) + 0.5) - labels_ref[label_row + s]
-        chi_ref[:, cols(s)], clo_ref[:, cols(s)] = hi_lo(coefficient * live_ref[live_row + s, 0:1, :])
+        coefficient = gain_ref[gain_row + s, 0:1, :] * jnp.tanh(0.5 * score) + labels_ref[label_row + s]
+        chi_ref[:, cols(s)], clo_ref[:, cols(s)] = hi_lo(coefficient)
     chi, clo = chi_ref[...], clo_ref[...]
-    grad = dot(shi, chi, NT) + dot(slo, chi, NT) + dot(shi, clo, NT)
+    both = dot(shi, jnp.concatenate([chi, clo], axis=0), NT)
+    grad = both[:, :LANES] + both[:, LANES:] + dot(slo, chi, NT)
     tail, state = adagrad(tail, state, grad)
-    tail_out[pl.ds(0, width), :] = tail
-    tail_out[pl.ds(width, 8), :] = jnp.broadcast_to(state, (8, LANES))
+    whole = ((0, width, tail), (width, 8, jnp.broadcast_to(state, (8, LANES))))
+    start = 0
+    for ref in tail_outs:
+        stop = start + ref.shape[0]
+        for first, size, value in whole:
+            lo, hi = max(start, first), min(stop, first + size)
+            if lo < hi:
+                ref[pl.ds(lo - start, hi - lo), :] = value[lo - first : hi - first]
+        start = stop
 
 
 def head_step(head, state, kept, rel_ref, tasks):
     thi_ref, tlo_ref, chi_ref, clo_ref = kept
-    thi, tlo = thi_ref[...], tlo_ref[...]
+    thi, tlo, chi = thi_ref[...], tlo_ref[...], chi_ref[...]
+    wide = dot(jnp.concatenate([thi, tlo], axis=1), jnp.concatenate([chi, chi], axis=0), NN) + dot(thi, clo_ref[...], NN)
     grad = None
     for s in range(tasks):
-        chi, clo = chi_ref[:, cols(s)], clo_ref[:, cols(s)]
-        term = dot(thi, chi, NN) + dot(tlo, chi, NN) + dot(thi, clo, NN)
-        term = term * rel_ref[:, cols(s)].astype(F32)
+        term = wide[:, s * LANES : (s + 1) * LANES] * rel_ref[:, cols(s)].astype(F32)
         grad = term if grad is None else grad + term
     return adagrad(head, state, grad)
 
 
 def first_kernel(mine, tasks, rounds):
-    n_out = 15
+    n_sent = 2 if mine == ODD else 1
+    n_out = 14 + n_sent
 
     def body(counts_hbm, ids_hbm, head_hbm, tail_hbm, hacc_hbm, tacc_hbm, rel_ref, he_hbm, te_hbm, *refs):
         outs, scratch = refs[-7 - n_out : -7], refs[-7:]
-        tail_out, kept, (head, hacc, shi, slo, rel_out), (he, te, rel_buf, lanes, live) = outs[0], outs[1:5], outs[5:10], outs[10:]
+        sent, outs = outs[:n_sent], outs[n_sent:]
+        kept, (head, hacc, shi, slo, rel_out), (he, te, rel_buf, lanes, gain) = outs[:4], outs[4:9], outs[9:]
         counts, rel_ids, tail, tacc, labels_ref, rel_sem, sem = scratch
 
         @pl.when(role() == mine)
@@ -113,20 +127,22 @@
                 copy.start()
             copies[0].wait()
             rels = [rel_copies(rel_ids, rel_ref, rel_buf, rel_sem, k, tasks) for k in range(rounds)]
-            for group in rels:
-                for copy in group:
-                    copy.start()
+            for copy in rels[0]:
+                copy.start()
             for copy in copies[1:4]:
                 copy.wait()
-            make_labels(labels_ref, he, te, 0, 0, tasks)
             for k in range(rounds):
                 for s in range(tasks):
                     lanes[k * tasks + s] = jnp.full(lanes.shape[1:], lax.rem(rel_ids[k, 0, s], LANES), I32)
-                    live[k * tasks + s] = jnp.full(live.shape[1:], jnp.where(s < counts[0, k], 1.0, 0.0), F32)
+                    gain[k * tasks + s] = jnp.full(gain.shape[1:], jnp.where(s < counts[0, k], HALF_NEG, 0.0), F32)
+            make_labels(labels_ref, he, te, gain, 0, 0, tasks)
+            for group in rels[1:]:
+                for copy in group:
+                    copy.start()
             for copy in rels[0] + copies[4:]:
                 copy.wait()
             scale_heads(head[...], lanes, rel_buf, 0, shi, slo, rel_out, tasks)
-            tail_step(tail[...], tacc[...], shi, slo, labels_ref, 0, live, 0, kept, tail_out, tasks)
+            tail_step(tail[...], tacc[...], shi, slo, labels_ref, 0, gain, 0, kept, sent, tasks)
             for group in rels[1:]:
                 for copy in group:
                     copy.wait()
@@ -134,14 +150,14 @@
     return body
 
 
-def tail_kernel(mine, k, tasks, width):
-    def body(tail_in, shi, slo, labels_ref, live, *refs):
-        outs = refs[4:]
+def tail_kernel(mine, k, tasks, width, n_in):
+    def body(*refs):
+        tail_in, (shi, slo, labels_ref, gain), outs = refs[:n_in], refs[n_in : n_in + 4], refs[n_in + 8 :]
 
         @pl.when(role() == mine)
         def _():
-            tail, state = tail_in[pl.ds(0, width), :], tail_in[pl.ds(width, 1), :]
-            tail_step(tail, state, shi, slo, labels_ref, (k - 1) * tasks, live, k * tasks, outs[1:5], outs[0], tasks)
+            tail = jnp.concatenate([ref[...] for ref in tail_in], axis=0) if n_in > 1 else tail_in[0][...]
+            tail_step(tail[:width], tail[width : width + 1], shi, slo, labels_ref, (k - 1) * tasks, gain, k * tasks, outs[1:5], outs[:1], tasks)
 
     return body
 
@@ -149,22 +165,21 @@
 LABEL_ROUNDS = {(0, ODD): (1,), (1, ODD): (2, 3), (1, EVEN): (1, 2), (3, EVEN): (3,)}
 
 
-def head_kernel(m, tasks, rounds):
-    def body(he, te, rel_buf, lanes, thi, tlo, chi, clo, *refs):
+def head_kernel(mine, m, tasks):
+    done = m if mine == ODD else m - 1
+
+    def body(he, te, rel_buf, lanes, gain, thi, tlo, chi, clo, *refs):
         ins, (head_out, hacc_out, shi, slo, rel_out, labels_ref) = refs[:5], refs[-6:]
         head, hacc, rel_in = ins[0], ins[1], ins[4]
-        for mine, done in ((ODD, m), (EVEN, m - 1)):
-            if not 0 <= done < rounds - 1:
-                continue
-
-            @pl.when(role() == mine)
-            def _():
-                new, state = head_step(head[...], hacc[...], (thi, tlo, chi, clo), rel_in, tasks)
-                head_out[...] = new
-                hacc_out[...] = state
-                scale_heads(new, lanes, rel_buf, done + 1, shi, slo, rel_out, tasks)
-                for k in LABEL_ROUNDS.get((m, mine), ()):
-                    make_labels(labels_ref, he, te, k * tasks, (k - 1) * tasks, tasks)
+
+        @pl.when(role() == mine)
+        def _():
+            new, state = head_step(head[...], hacc[...], (thi, tlo, chi, clo), rel_in, tasks)
+            head_out[...] = new
+            hacc_out[...] = state
+            scale_heads(new, lanes, rel_buf, done + 1, shi, slo, rel_out, tasks)
+            for k in LABEL_ROUNDS.get((m, mine), ()):
+                make_labels(labels_ref, he, te, gain, k * tasks, (k - 1) * tasks, tasks)
 
     return body
 
@@ -226,42 +241,50 @@
     edge = ((slots, groups, LANES), I32)
     fixed_shapes = [edge, edge, ((slots, width, LANES), BF16), ((slots, 8, rows), I32), ((slots, 8, rows), F32)]
 
+    halves = [((width // 2, rows), F32), ((width - width // 2 + 8, rows), F32)]
+
     def first(mine, carried):
+        sent = halves if mine == ODD else [packed]
         return call(
             first_kernel(mine, tasks, rounds), [HBM] * 9 + [VMEM] * len(carried),
-            [packed] + kept_shapes + state_shapes + fixed_shapes,
+            sent + kept_shapes + state_shapes + fixed_shapes,
             [pltpu.SMEM(counts.shape, I32), pltpu.SMEM(rel_ids.shape, I32), pltpu.VMEM(*block), pltpu.VMEM(*row),
              pltpu.VMEM((tasks, rows, rows), F32), pltpu.SemaphoreType.DMA((slots,)), pltpu.SemaphoreType.DMA((8,))],
             [counts, rel_ids, head, tail, hacc, tacc, rels, he, te] + carried,
-            {9 + i: 1 + i for i in range(len(carried))})
+            {9 + i: len(sent) + i for i in range(len(carried))})
 
     def tails_step(mine, k, tail_in, kept, state):
+        n = len(tail_in)
         out = call(
-            tail_kernel(mine, k, tasks, width), [VMEM] * 9, [packed] + kept_shapes, [],
-            [tail_in, state[2], state[3], state[5], fixed[4]] + kept, {5 + i: 1 + i for i in range(4)})
+            tail_kernel(mine, k, tasks, width, n), [VMEM] * (n + 8), [packed] + kept_shapes, [],
+            tail_in + [state[2], state[3], state[5], fixed[4]] + kept, {n + 4 + i: 1 + i for i in range(4)})
         return out[0], list(out[1:])
 
-    def heads_step(m, kept, state):
+    def heads_step(mine, m, kept, state):
         return list(call(
-            head_kernel(m, tasks, rounds), [VMEM] * (8 + len(state)), state_shapes + [table], [],
-            list(fixed[:4]) + kept + state, {8 + i: i for i in range(len(state))}))
-
-    out = first(ODD, [])
-    to_even = send(out[0], 1, ODD)
-    out = first(EVEN, list(out[1:]))
+            head_kernel(mine, m, tasks), [VMEM] * (9 + len(state)), state_shapes + [table], [],
+            list(fixed) + kept + state, {9 + i: i for i in range(len(state))}))
+
+    out = list(first(ODD, []))
+    to_even = []
+    for i in range(2):
+        to_even.append(send(out[i], 1, ODD))
+    out = first(EVEN, out[2:])
     own, kept, state, fixed = out[0], list(out[1:5]), list(out[5:10]), list(out[10:])
     to_odd = send_or_swap(own, 1, EVEN)
-    state = heads_step(0, kept, state)
+    state = heads_step(ODD, 0, kept, state)
     for k in range(1, rounds):
         distance = 1 if k < rounds - 1 else 1 - rounds
-        own, kept = tails_step(ODD, k, to_odd, kept, state)
+        own, kept = tails_step(ODD, k, [to_odd], kept, state)
         arrived = to_even
-        to_even = send_or_swap(own, distance, ODD)
-        state = heads_step(k, kept, state)
+        to_even = [send_or_swap(own, distance, ODD)]
+        if k < rounds - 1:
+            state = heads_step(ODD, k, kept, state)
+        state = heads_step(EVEN, k, kept, state)
         own, kept = tails_step(EVEN, k, arrived, kept, state)
         to_odd = send_or_swap(own, distance, EVEN)
     head, hacc = call(last_heads(tasks), [VMEM] * 7, [block, row], [], [state[0], state[1], state[4]] + kept)
-    tail, tacc = call(pick_tails(width), [VMEM] * 2, [block, row], [], [to_even, to_odd])
+    tail, tacc = call(pick_tails(width), [VMEM] * 2, [block, row], [], [to_even[0], to_odd])
     return head.T, tail.T, hacc.reshape(rows), tacc.reshape(rows)
 
 

time: 54.4 us -> 53.5 us (0.983)
  Pallas kernels: 16.2 us -> 13.2 us
  starting transfers between devices: 8.88 us -> 10.2 us
  waiting for transfers between devices: 28.4 us -> 29.1 us
    pallas_call x14 -> x16, Pallas kernels: 16.2 us -> 13.2 us  [call(): pl.pallas_call(body, in_specs=ins, out_specs=[VMEM] * len(outs), out_shap...]
    ppermute x1 -> x2, starting transfers between devices: 1.29 us -> 2.58 us  [send(): lax.ppermute(block, 'blk', [(i, (i + distance) % n) for i in range(mine,...]
    ppermute x7, waiting for transfers between devices: 23.5 us -> 24.7 us  [send_or_swap(): lax.ppermute(block, 'blk', [(i, (i + distance) % n if i % 2 == mine else...]
    ppermute x1 -> x2, waiting for transfers between devices: 4.92 us -> 4.34 us  [send(): lax.ppermute(block, 'blk', [(i, (i + distance) % n) for i in range(mine,...]
  transfers between devices with their start and end apart: 8 -> 9, of which waited for: 7 -> 7; matrix products, arithmetic and copies ran while one was open for 0% -> 0% of each run, Pallas kernels for 13% -> 10%
where the time goes in v5:
time: 53.5 us; the launch traced here: 53.3 us
  waiting for transfers between devices  29.1 us (54%)
  Pallas kernels  13.2 us (25%)
  starting transfers between devices  10.2 us (19%)
  between operations  0.76 us (1%)
    ppermute x7, waiting for transfers between devices, send_or_swap(): lax.ppermute(block, 'blk', [(i, (i + distance) % n if i % 2 == mine else...  24.7 us
    pallas_call x16, Pallas kernels, call(): pl.pallas_call(body, in_specs=ins, out_specs=[VMEM] * len(outs), out_shap...  13.2 us
    ppermute x7, starting transfers between devices, send_or_swap(): lax.ppermute(block, 'blk', [(i, (i + distance) % n if i % 2 == mine else...  7.66 us
    ppermute x2, waiting for transfers between devices, send(): lax.ppermute(block, 'blk', [(i, (i + distance) % n) for i in range(mine,...  4.34 us
    ppermute x2, starting transfers between devices, send(): lax.ppermute(block, 'blk', [(i, (i + distance) % n) for i in range(mine,...  2.58 us
  transfers between devices with their start and end apart: 9, of which 7 were waited for; matrix products, arithmetic and copies ran while one was open for 0% of the time, Pallas kernels for 10%

profile of v5, /device:TPU:126, one launch (start us, length us, event | category | flops | bytes accessed | tf_op | source)
XLA Modules:
  0.0 53.3 jit_solution(14267380850668874716)
XLA Ops:
  0.6 0.3 shard_map.120
  0.9 3.6 %shard_map.121 = (f32[408,128]{1,0:T(8,128)S(1)}, bf16[400,128]{1,0:T(8,128)(2,1)S(1)}, bf16[400,128]{1,0:T(8,128)(2,1)S(1)}, bf16[128,640]{1,0:T(8,128)(2,1)S(1...) custom-call(s32[1,4]{1,0:T(1,128)} %bitcast.23, ...), custom_call_target="tpu_custom_call", output_to_operand_aliasing={{1}: (9, {}), {2}: (10, {}), {3}: (11, {}), {4}: (12, {}), ... | custom-call | flops 1000000000 | bytes 1048576 | tf_op jit(solution)/shard_map/pallas_call | solution.py:207
  4.5 0.1 collective-permute-start
  4.6 1.3 %collective-permute-start.2 = (f32[200,128]{1,0:T(8,128)S(1)}, f32[200,128]{1,0:T(8,128)S(1)}, u32[]{:S(2)}, u32[]{:S(2)}) collective-permute-start(f32[200,128]{1,0:T(8,128)S(1)} %get-tuple-element.138), channel_id=1, source_target_pairs={{2,4},{6,8},{10,12},{14,16},{18,20},{22,24},{26,28},{30,32},{34,36... | collective-permute-start | bytes 307208 | tf_op jit(solution)/shard_map/ppermute | solution.py:221
  5.9 1.3 %collective-permute-start.3 = (f32[208,128]{1,0:T(8,128)S(1)}, f32[208,128]{1,0:T(8,128)S(1)}, u32[]{:S(2)}, u32[]{:S(2)}) collective-permute-start(f32[208,128]{1,0:T(8,128)S(1)} %get-tuple-element.139), channel_id=1, source_target_pairs={{2,4},{6,8},{10,12},{14,16},{18,20},{22,24},{26,28},{30,32},{34,36... | collective-permute-start | bytes 319496 | tf_op jit(solution)/shard_map/ppermute | solution.py:221
  7.3 1.8 %shard_map.125 = (f32[400,128]{1,0:T(8,128)S(1)}, f32[1,128]{1,0:T(1,128)S(1)}, bf16[400,640]{1,0:T(8,128)(2,1)S(1)}, bf16[400,640]{1,0:T(8,128)(2,1)S(1)}, bf16...) custom-call(s32[20,8,128]{2,1,0:T(8,128)S(1)} %get-tuple-element.119, ...), custom_call_target="tpu_custom_call", output_to_operand_aliasing={{0}: (9, {}), {1}: (10, {}), {2}: (11, {}), {3}: (12, {}), ... | custom-call | flops 1000000000 | bytes 1048576 | tf_op jit(solution)/shard_map/pallas_call | solution.py:207
  9.1 3.0 %collective-permute-done.2.refs_0_ = f32[200,128]{1,0:T(8,128)S(1)} collective-permute-done((f32[200,128]{1,0:T(8,128)S(1)}, f32[200,128]{1,0:T(8,128)S(1)}, u32[]{:S(2)}, u32[]{:S(2)}) %collective-permute-start.2) | collective-permute-done | bytes 102432 | tf_op jit(solution)/shard_map/ppermute | solution.py:221
  12.1 1.3 %collective-permute-done.3.refs_1_ = f32[208,128]{1,0:T(8,128)S(1)} collective-permute-done((f32[208,128]{1,0:T(8,128)S(1)}, f32[208,128]{1,0:T(8,128)S(1)}, u32[]{:S(2)}, u32[]{:S(2)}) %collective-permute-start.3) | collective-permute-done | bytes 106528 | tf_op jit(solution)/shard_map/ppermute | solution.py:221
  13.5 1.1 %shard_map.126 = (f32[408,128]{1,0:T(8,128)S(1)}, bf16[400,128]{1,0:T(8,128)(2,1)S(1)}, bf16[400,128]{1,0:T(8,128)(2,1)S(1)}, bf16[128,640]{1,0:T(8,128)(2,1)S(1)}, bf16[128,640]{1,0:T(8,128)(2,1)S(1)}) custom-call(f32[200,128]{1,0:T(8,128)S(1)} %collective-permute-done.2.refs_0_, ...), custom_call_target="tpu_custom_call", output_to_operand_aliasing={{1}: (6, {}), {2}: (7, {}), {3}: (8, {}), {4}: (9, {})} | custom-call | flops 1000000000 | bytes 1048576 | tf_op jit(solution)/shard_map/pallas_call | solution.py:207
  14.5 1.6 %collective-permute-start.4 = (f32[408,128]{1,0:T(8,128)S(1)}, f32[408,128]{1,0:T(8,128)S(1)}, u32[]{:S(2)}, u32[]{:S(2)}) collective-permute-start(f32[408,128]{1,0:T(8,128)S(1)} %get-tuple-element.156), channel_id=1, source_target_pairs={{0,2},{2,0},{4,6},{6,4},{8,10},{10,8},{12,14},{14,12},{16,18},{18,... | collective-permute-start | bytes 626696 | tf_op jit(solution)/shard_map/ppermute | solution.py:226
  16.1 0.1 collective-permute-start.1
  16.2 1.0 %collective-permute-done.4.refs_0_ = f32[408,128]{1,0:T(8,128)S(1)} collective-permute-done((f32[408,128]{1,0:T(8,128)S(1)}, f32[408,128]{1,0:T(8,128)S(1)}, u32[]{:S(2)}, u32[]{:S(2)}) %collective-permute-start.4) | collective-permute-done | bytes 208928 | tf_op jit(solution)/shard_map/ppermute | solution.py:226
  17.2 0.9 %shard_map.129 = (f32[400,128]{1,0:T(8,128)S(1)}, f32[1,128]{1,0:T(1,128)S(1)}, bf16[400,640]{1,0:T(8,128)(2,1)S(1)}, bf16[400,640]{1,0:T(8,128)(2,1)S(1)}, bf16...) custom-call(s32[20,8,128]{2,1,0:T(8,128)S(1)} %get-tuple-element.119, ...), custom_call_target="tpu_custom_call", output_to_operand_aliasing={{0}: (9, {}), {1}: (10, {}), {2}: (11, {}), {3}: (12, {}), ... | custom-call | flops 1000000000 | bytes 1048576 | tf_op jit(solution)/shard_map/pallas_call | solution.py:207
  18.1 4.7 %collective-permute-done.1.refs_0_ = f32[408,128]{1,0:T(8,128)S(1)} collective-permute-done((f32[408,128]{1,0:T(8,128)S(1)}, f32[408,128]{1,0:T(8,128)S(1)}, u32[]{:S(2)}, u32[]{:S(2)}) %collective-permute-start.1) | collective-permute-done | bytes 208928 | tf_op jit(solution)/shard_map/ppermute | solution.py:226
  22.9 1.1 %shard_map.130 = (f32[408,128]{1,0:T(8,128)S(1)}, bf16[400,128]{1,0:T(8,128)(2,1)S(1)}, bf16[400,128]{1,0:T(8,128)(2,1)S(1)}, bf16[128,640]{1,0:T(8,128)(2,1)S(1)}, bf16[128,640]{1,0:T(8,128)(2,1)S(1)}) custom-call(f32[408,128]{1,0:T(8,128)S(1)} %collective-permute-done.1.refs_0_, ...), custom_call_target="tpu_custom_call", output_to_operand_aliasing={{1}: (5, {}), {2}: (6, {}), {3}: (7, {}), {4}: (8, {})} | custom-call | flops 1000000000 | bytes 1048576 | tf_op jit(solution)/shard_map/pallas_call | solution.py:207
  24.0 1.5 %collective-permute-start.5 = (f32[408,128]{1,0:T(8,128)S(1)}, f32[408,128]{1,0:T(8,128)S(1)}, u32[]{:S(2)}, u32[]{:S(2)}) collective-permute-start(f32[408,128]{1,0:T(8,128)S(1)} %get-tuple-element.177), channel_id=1, source_target_pairs={{0,2},{2,0},{4,6},{6,4},{8,10},{10,8},{12,14},{14,12},{16,18},{18,... | collective-permute-start | bytes 626696 | tf_op jit(solution)/shard_map/ppermute | solution.py:226
  25.4 1.1 %collective-permute-done.5.refs_0_ = f32[408,128]{1,0:T(8,128)S(1)} collective-permute-done((f32[408,128]{1,0:T(8,128)S(1)}, f32[408,128]{1,0:T(8,128)S(1)}, u32[]{:S(2)}, u32[]{:S(2)}) %collective-permute-start.5) | collective-permute-done | bytes 208928 | tf_op jit(solution)/shard_map/ppermute | solution.py:226
  26.5 1.5 %shard_map.132 = (f32[400,128]{1,0:T(8,128)S(1)}, f32[1,128]{1,0:T(1,128)S(1)}, bf16[400,640]{1,0:T(8,128)(2,1)S(1)}, bf16[400,640]{1,0:T(8,128)(2,1)S(1)}, bf16...) custom-call(s32[20,8,128]{2,1,0:T(8,128)S(1)} %get-tuple-element.119, ...), custom_call_target="tpu_custom_call", output_to_operand_aliasing={{0}: (9, {}), {1}: (10, {}), {2}: (11, {}), {3}: (12, {}), ... | custom-call | flops 1000000000 | bytes 1048576 | tf_op jit(solution)/shard_map/pallas_call | solution.py:207
  28.0 4.2 %collective-permute-done.6.refs_0_ = f32[408,128]{1,0:T(8,128)S(1)} collective-permute-done((f32[408,128]{1,0:T(8,128)S(1)}, f32[408,128]{1,0:T(8,128)S(1)}, u32[]{:S(2)}, u32[]{:S(2)}) %collective-permute-start.6) | collective-permute-done | bytes 208928 | tf_op jit(solution)/shard_map/ppermute | solution.py:226
  32.2 1.1 %shard_map.133 = (f32[408,128]{1,0:T(8,128)S(1)}, bf16[400,128]{1,0:T(8,128)(2,1)S(1)}, bf16[400,128]{1,0:T(8,128)(2,1)S(1)}, bf16[128,640]{1,0:T(8,128)(2,1)S(1)}, bf16[128,640]{1,0:T(8,128)(2,1)S(1)}) custom-call(f32[408,128]{1,0:T(8,128)S(1)} %collective-permute-done.6.refs_0_, ...), custom_call_target="tpu_custom_call", output_to_operand_aliasing={{1}: (5, {}), {2}: (6, {}), {3}: (7, {}), {4}: (8, {})} | custom-call | flops 1000000000 | bytes 1048576 | tf_op jit(solution)/shard_map/pallas_call | solution.py:207
  33.3 4.3 %collective-permute-start.7 = (f32[408,128]{1,0:T(8,128)S(1)}, f32[408,128]{1,0:T(8,128)S(1)}, u32[]{:S(2)}, u32[]{:S(2)}) collective-permute-start(f32[408,128]{1,0:T(8,128)S(1)} %get-tuple-element.201), channel_id=1, source_target_pairs={{0,2},{2,252},{4,6},{6,0},{8,10},{10,4},{12,14},{14,8},{16,18},{18... | collective-permute-start | bytes 626696 | tf_op jit(solution)/shard_map/ppermute | solution.py:226
  37.6 1.2 %shard_map.134 = (f32[400,128]{1,0:T(8,128)}, f32[1,128]{1,0:T(1,128)}) custom-call(f32[400,128]{1,0:T(8,128)S(1)} %get-tuple-element.189.head, f32[1,128]{1,0:T(1,128)S(1)} %get-tuple-element.190.hacc, bf16[400,640]{1,0:T(8,128)(2,1)S(1)} %get-tuple-element.191.rel_in, bf16[400,128]{1,0:T(8,128)(2,1)S(1)} %get-tuple-element.196.thi, ...), custom_call_target="tpu_custom_call" | custom-call | flops 1000000000 | bytes 1048576 | tf_op jit(solution)/shard_map/pallas_call | solution.py:207
  38.9 13.7 %collective-permute-done.7.from_odd = f32[408,128]{1,0:T(8,128)S(1)} collective-permute-done((f32[408,128]{1,0:T(8,128)S(1)}, f32[408,128]{1,0:T(8,128)S(1)}, u32[]{:S(2)}, u32[]{:S(2)}) %collective-permute-start.7) | collective-permute-done | bytes 208928 | tf_op jit(solution)/shard_map/ppermute | solution.py:226
  52.6 0.7 %shard_map.135 = (f32[400,128]{1,0:T(8,128)}, f32[1,128]{1,0:T(1,128)}) custom-call(f32[408,128]{1,0:T(8,128)S(1)} %collective-permute-done.7.from_odd, f32[408,128]{1,0:T(8,128)S(1)} %collective-permute-done.8.from_even), custom_call_target="tpu_custom_call" | custom-call | flops 1000000000 | bytes 1048576 | tf_op jit(solution)/shard_map/pallas_call | solution.py:207
  (10 shorter events, 0.2 us)
Async XLA Ops:
  4.5 2.7 %collective-permute-start = (f32[408,128]{1,0:T(8,128)S(1)}, f32[408,128]{1,0:T(8,128)S(1)}, u32[]{:S(2)}, u32[]{:S(2)}) collective-permute-start(f32[408,128]{1,0:T(8,128)S(1)} %get-tuple-element.124), channel_id=1, source_target_pairs={{0,2},{2,0},{4,6},{6,4},{8,10},{10,8},{12,14},{14,12},{16,18},{18,... | collective-permute-start | bytes 626696 | tf_op jit(solution)/shard_map/ppermute | solution.py:226
  4.6 7.5 %collective-permute-start.2 = (f32[200,128]{1,0:T(8,128)S(1)}, f32[200,128]{1,0:T(8,128)S(1)}, u32[]{:S(2)}, u32[]{:S(2)}) collective-permute-start(f32[200,128]{1,0:T(8,128)S(1)} %get-tuple-element.138), channel_id=1, source_target_pairs={{2,4},{6,8},{10,12},{14,16},{18,20},{22,24},{26,28},{30,32},{34,36... | collective-permute-start | bytes 307208 | tf_op jit(solution)/shard_map/ppermute | solution.py:221
  5.9 7.5 %collective-permute-start.3 = (f32[208,128]{1,0:T(8,128)S(1)}, f32[208,128]{1,0:T(8,128)S(1)}, u32[]{:S(2)}, u32[]{:S(2)}) collective-permute-start(f32[208,128]{1,0:T(8,128)S(1)} %get-tuple-element.139), channel_id=1, source_target_pairs={{2,4},{6,8},{10,12},{14,16},{18,20},{22,24},{26,28},{30,32},{34,36... | collective-permute-start | bytes 319496 | tf_op jit(solution)/shard_map/ppermute | solution.py:221
  14.5 2.7 %collective-permute-start.4 = (f32[408,128]{1,0:T(8,128)S(1)}, f32[408,128]{1,0:T(8,128)S(1)}, u32[]{:S(2)}, u32[]{:S(2)}) collective-permute-start(f32[408,128]{1,0:T(8,128)S(1)} %get-tuple-element.156), channel_id=1, source_target_pairs={{0,2},{2,0},{4,6},{6,4},{8,10},{10,8},{12,14},{14,12},{16,18},{18,... | collective-permute-start | bytes 626696 | tf_op jit(solution)/shard_map/ppermute | solution.py:226
  16.1 6.7 %collective-permute-start.1 = (f32[408,128]{1,0:T(8,128)S(1)}, f32[408,128]{1,0:T(8,128)S(1)}, u32[]{:S(2)}, u32[]{:S(2)}) collective-permute-start(f32[408,128]{1,0:T(8,128)S(1)} %get-tuple-element.137), channel_id=1, source_target_pairs={{0,2},{2,4},{4,6},{6,8},{8,10},{10,12},{12,14},{14,16},{16,18},{18... | collective-permute-start | bytes 626696 | tf_op jit(solution)/shard_map/ppermute | solution.py:226
  24.0 2.6 %collective-permute-start.5 = (f32[408,128]{1,0:T(8,128)S(1)}, f32[408,128]{1,0:T(8,128)S(1)}, u32[]{:S(2)}, u32[]{:S(2)}) collective-permute-start(f32[408,128]{1,0:T(8,128)S(1)} %get-tuple-element.177), channel_id=1, source_target_pairs={{0,2},{2,0},{4,6},{6,4},{8,10},{10,8},{12,14},{14,12},{16,18},{18,... | collective-permute-start | bytes 626696 | tf_op jit(solution)/shard_map/ppermute | solution.py:226
  25.4 6.7 %collective-permute-start.6 = (f32[408,128]{1,0:T(8,128)S(1)}, f32[408,128]{1,0:T(8,128)S(1)}, u32[]{:S(2)}, u32[]{:S(2)}) collective-permute-start(f32[408,128]{1,0:T(8,128)S(1)} %get-tuple-element.192), channel_id=1, source_target_pairs={{0,2},{2,4},{4,6},{6,8},{8,10},{10,12},{12,14},{14,16},{16,18},{18... | collective-permute-start | bytes 626696 | tf_op jit(solution)/shard_map/ppermute | solution.py:226
  33.2 5.6 %collective-permute-start.8 = (f32[408,128]{1,0:T(8,128)S(1)}, f32[408,128]{1,0:T(8,128)S(1)}, u32[]{:S(2)}, u32[]{:S(2)}) collective-permute-start(f32[408,128]{1,0:T(8,128)S(1)} %get-tuple-element.202), channel_id=1, source_target_pairs={{0,250},{2,0},{4,254},{6,4},{8,2},{10,8},{12,6},{14,12},{16,10},{1... | collective-permute-start | bytes 626696 | tf_op jit(solution)/shard_map/ppermute | solution.py:226
  33.3 19.3 %collective-permute-start.7 = (f32[408,128]{1,0:T(8,128)S(1)}, f32[408,128]{1,0:T(8,128)S(1)}, u32[]{:S(2)}, u32[]{:S(2)}) collective-permute-start(f32[408,128]{1,0:T(8,128)S(1)} %get-tuple-element.201), channel_id=1, source_target_pairs={{0,2},{2,252},{4,6},{6,0},{8,10},{10,4},{12,14},{14,8},{16,18},{18... | collective-permute-start | bytes 626696 | tf_op jit(solution)/shard_map/ppermute | solution.py:226

commit v6 on v5

--- a/solution.py
+++ b/solution.py
@@ -35,8 +35,12 @@
 
 
 def one_hot(rows):
-    which = lax.broadcasted_iota(I32, (LANES, LANES), 0)
-    parts = [jnp.where(rows[r : r + 1, :] == which, 1.0, 0.0).astype(BF16) for r in range(rows.shape[0])]
+    which = lax.broadcasted_iota(I32, (LANES, LANES), 0).astype(F32).astype(BF16)
+    one, zero = jnp.ones((), BF16), jnp.zeros((), BF16)
+    parts = []
+    for r in range(rows.shape[0]):
+        row = jnp.broadcast_to(rows[r : r + 1, :].astype(F32), (16, LANES)).astype(BF16)
+        parts.append(jnp.where(which == jnp.concatenate([row] * (LANES // 16), axis=0), one, zero))
     return jnp.concatenate(parts, axis=1)
 
 
@@ -70,7 +74,7 @@
     return block - grad * (LEARN_RATE / jnp.sqrt(state)), state
 
 
-def tail_step(tail, state, shi_ref, slo_ref, labels_ref, label_row, gain_ref, gain_row, kept, tail_outs, tasks):
+def tail_step(tail, state, shi_ref, slo_ref, labels_ref, label_row, gain_ref, gain_row, kept, tail_out, tasks):
     thi_ref, tlo_ref, chi_ref, clo_ref = kept
     width = tail.shape[0]
     thi, tlo = hi_lo(tail)
@@ -86,15 +90,8 @@
     both = dot(shi, jnp.concatenate([chi, clo], axis=0), NT)
     grad = both[:, :LANES] + both[:, LANES:] + dot(slo, chi, NT)
     tail, state = adagrad(tail, state, grad)
-    whole = ((0, width, tail), (width, 8, jnp.broadcast_to(state, (8, LANES))))
-    start = 0
-    for ref in tail_outs:
-        stop = start + ref.shape[0]
-        for first, size, value in whole:
-            lo, hi = max(start, first), min(stop, first + size)
-            if lo < hi:
-                ref[pl.ds(lo - start, hi - lo), :] = value[lo - first : hi - first]
-        start = stop
+    tail_out[pl.ds(0, width), :] = tail
+    tail_out[pl.ds(width, 8), :] = jnp.broadcast_to(state, (8, LANES))
 
 
 def head_step(head, state, kept, rel_ref, tasks):
@@ -108,56 +105,48 @@
     return adagrad(head, state, grad)
 
 
-def first_kernel(mine, tasks, rounds):
-    n_sent = 2 if mine == ODD else 1
-    n_out = 14 + n_sent
-
+def first_kernel(tasks, rounds, width):
     def body(counts_hbm, ids_hbm, head_hbm, tail_hbm, hacc_hbm, tacc_hbm, rel_ref, he_hbm, te_hbm, *refs):
-        outs, scratch = refs[-7 - n_out : -7], refs[-7:]
-        sent, outs = outs[:n_sent], outs[n_sent:]
-        kept, (head, hacc, shi, slo, rel_out), (he, te, rel_buf, lanes, gain) = outs[:4], outs[4:9], outs[9:]
-        counts, rel_ids, tail, tacc, labels_ref, rel_sem, sem = scratch
+        outs, (counts, rel_ids, tacc, rel_sem, sem) = refs[:16], refs[16:]
+        tail_out, (head, hacc, shi, slo, rel_out, labels_ref), (he, te, rel_buf, lanes, gain) = outs[0], outs[5:11], outs[11:]
+        pairs = ((ids_hbm, rel_ids), (counts_hbm, counts), (he_hbm, he), (te_hbm, te), (head_hbm, head),
+                 (tail_hbm, tail_out.at[pl.ds(0, width)]), (hacc_hbm, hacc), (tacc_hbm, tacc))
+        copies = [pltpu.make_async_copy(src, dst, sem.at[i]) for i, (src, dst) in enumerate(pairs)]
+        for copy in copies:
+            copy.start()
+        copies[0].wait()
+        rels = [rel_copies(rel_ids, rel_ref, rel_buf, rel_sem, k, tasks) for k in range(rounds)]
+        for copy in rels[0]:
+            copy.start()
+        for copy in copies[1:4]:
+            copy.wait()
+        for k in range(rounds):
+            for s in range(tasks):
+                lanes[k * tasks + s] = jnp.full(lanes.shape[1:], lax.rem(rel_ids[k, 0, s], LANES), I32)
+                gain[k * tasks + s] = jnp.full(gain.shape[1:], jnp.where(s < counts[0, k], HALF_NEG, 0.0), F32)
+        make_labels(labels_ref, he, te, gain, 0, 0, tasks)
+        for group in rels[1:]:
+            for copy in group:
+                copy.start()
+        for copy in rels[0] + copies[4:]:
+            copy.wait()
+        tail_out[pl.ds(width, 8), :] = jnp.broadcast_to(tacc[...], (8, LANES))
+        scale_heads(head[...], lanes, rel_buf, 0, shi, slo, rel_out, tasks)
+        for group in rels[1:]:
+            for copy in group:
+                copy.wait()
+
+    return body
+
+
+def tail_kernel(mine, k, tasks, width):
+    def body(tail_in, shi, slo, labels_ref, gain, *refs):
+        outs = refs[4:]
 
         @pl.when(role() == mine)
         def _():
-            pairs = ((ids_hbm, rel_ids), (counts_hbm, counts), (he_hbm, he), (te_hbm, te), (head_hbm, head), (tail_hbm, tail),
-                     (hacc_hbm, hacc), (tacc_hbm, tacc))
-            copies = [pltpu.make_async_copy(src, dst, sem.at[i]) for i, (src, dst) in enumerate(pairs)]
-            for copy in copies:
-                copy.start()
-            copies[0].wait()
-            rels = [rel_copies(rel_ids, rel_ref, rel_buf, rel_sem, k, tasks) for k in range(rounds)]
-            for copy in rels[0]:
-                copy.start()
-            for copy in copies[1:4]:
-                copy.wait()
-            for k in range(rounds):
-                for s in range(tasks):
-                    lanes[k * tasks + s] = jnp.full(lanes.shape[1:], lax.rem(rel_ids[k, 0, s], LANES), I32)
-                    gain[k * tasks + s] = jnp.full(gain.shape[1:], jnp.where(s < counts[0, k], HALF_NEG, 0.0), F32)
-            make_labels(labels_ref, he, te, gain, 0, 0, tasks)
-            for group in rels[1:]:
-                for copy in group:
-                    copy.start()
-            for copy in rels[0] + copies[4:]:
-                copy.wait()
-            scale_heads(head[...], lanes, rel_buf, 0, shi, slo, rel_out, tasks)
-            tail_step(tail[...], tacc[...], shi, slo, labels_ref, 0, gain, 0, kept, sent, tasks)
-            for group in rels[1:]:
-                for copy in group:
-                    copy.wait()
-
-    return body
-
-
-def tail_kernel(mine, k, tasks, width, n_in):
-    def body(*refs):
-        tail_in, (shi, slo, labels_ref, gain), outs = refs[:n_in], refs[n_in : n_in + 4], refs[n_in + 8 :]
-
-        @pl.when(role() == mine)
-        def _():
-            tail = jnp.concatenate([ref[...] for ref in tail_in], axis=0) if n_in > 1 else tail_in[0][...]
-            tail_step(tail[:width], tail[width : width + 1], shi, slo, labels_ref, (k - 1) * tasks, gain, k * tasks, outs[1:5], outs[:1], tasks)
+            tail, state = tail_in[pl.ds(0, width), :], tail_in[pl.ds(width, 1), :]
+            tail_step(tail, state, shi, slo, labels_ref, k * tasks, gain, k * tasks, outs[1:5], outs[0], tasks)
 
     return body
 
@@ -179,7 +168,7 @@
             hacc_out[...] = state
             scale_heads(new, lanes, rel_buf, done + 1, shi, slo, rel_out, tasks)
             for k in LABEL_ROUNDS.get((m, mine), ()):
-                make_labels(labels_ref, he, te, gain, k * tasks, (k - 1) * tasks, tasks)
+                make_labels(labels_ref, he, te, gain, k * tasks, k * tasks, tasks)
 
     return body
 
@@ -216,11 +205,6 @@
     )(*args)
 
 
-def send(block, distance, mine):
-    n = lax.axis_size("blk")
-    return lax.ppermute(block, "blk", [(i, (i + distance) % n) for i in range(mine, n, 2)])
-
-
 def send_or_swap(block, distance, mine):
     n = lax.axis_size("blk")
     return lax.ppermute(block, "blk", [(i, (i + distance) % n if i % 2 == mine else i ^ 1) for i in range(n)])
@@ -235,56 +219,46 @@
     he, te = head_edges.reshape(slots, groups, LANES), tail_edges.reshape(slots, groups, LANES)
     block, packed, row = ((width, rows), F32), ((width + 8, rows), F32), ((1, rows), F32)
     coeff, scaled, half = ((rows, wide), BF16), ((width, wide), BF16), ((width, rows), BF16)
-    table = ((slots - tasks, rows, rows), F32)
+    table = ((slots, rows, rows), F32)
     kept_shapes = [half, half, coeff, coeff]
-    state_shapes = [block, row, scaled, scaled, scaled]
+    state_shapes = [block, row, scaled, scaled, scaled, table]
     edge = ((slots, groups, LANES), I32)
     fixed_shapes = [edge, edge, ((slots, width, LANES), BF16), ((slots, 8, rows), I32), ((slots, 8, rows), F32)]
 
-    halves = [((width // 2, rows), F32), ((width - width // 2 + 8, rows), F32)]
-
-    def first(mine, carried):
-        sent = halves if mine == ODD else [packed]
-        return call(
-            first_kernel(mine, tasks, rounds), [HBM] * 9 + [VMEM] * len(carried),
-            sent + kept_shapes + state_shapes + fixed_shapes,
-            [pltpu.SMEM(counts.shape, I32), pltpu.SMEM(rel_ids.shape, I32), pltpu.VMEM(*block), pltpu.VMEM(*row),
-             pltpu.VMEM((tasks, rows, rows), F32), pltpu.SemaphoreType.DMA((slots,)), pltpu.SemaphoreType.DMA((8,))],
-            [counts, rel_ids, head, tail, hacc, tacc, rels, he, te] + carried,
-            {9 + i: len(sent) + i for i in range(len(carried))})
-
     def tails_step(mine, k, tail_in, kept, state):
-        n = len(tail_in)
         out = call(
-            tail_kernel(mine, k, tasks, width, n), [VMEM] * (n + 8), [packed] + kept_shapes, [],
-            tail_in + [state[2], state[3], state[5], fixed[4]] + kept, {n + 4 + i: 1 + i for i in range(4)})
+            tail_kernel(mine, k, tasks, width), [VMEM] * 9, [packed] + kept_shapes, [],
+            [tail_in, state[2], state[3], state[5], fixed[4]] + kept, {5 + i: 1 + i for i in range(4)})
         return out[0], list(out[1:])
 
     def heads_step(mine, m, kept, state):
         return list(call(
-            head_kernel(mine, m, tasks), [VMEM] * (9 + len(state)), state_shapes + [table], [],
-            list(fixed) + kept + state, {9 + i: i for i in range(len(state))}))
-
-    out = list(first(ODD, []))
-    to_even = []
-    for i in range(2):
-        to_even.append(send(out[i], 1, ODD))
-    out = first(EVEN, out[2:])
-    own, kept, state, fixed = out[0], list(out[1:5]), list(out[5:10]), list(out[10:])
+            head_kernel(mine, m, tasks), [VMEM] * 15, state_shapes, [],
+            list(fixed) + kept + state, {9 + i: i for i in range(6)}))
+
+    out = call(
+        first_kernel(tasks, rounds, width), [HBM] * 9, [packed] + kept_shapes + state_shapes + fixed_shapes,
+        [pltpu.SMEM(counts.shape, I32), pltpu.SMEM(rel_ids.shape, I32), pltpu.VMEM(*row),
+         pltpu.SemaphoreType.DMA((slots,)), pltpu.SemaphoreType.DMA((8,))],
+        [counts, rel_ids, head, tail, hacc, tacc, rels, he, te])
+    start, kept, state, fixed = out[0], list(out[1:5]), list(out[5:11]), list(out[11:])
+    own, kept = tails_step(ODD, 0, start, kept, state)
+    to_even = send_or_swap(own, 1, ODD)
+    own, kept = tails_step(EVEN, 0, start, kept, state)
     to_odd = send_or_swap(own, 1, EVEN)
     state = heads_step(ODD, 0, kept, state)
     for k in range(1, rounds):
         distance = 1 if k < rounds - 1 else 1 - rounds
-        own, kept = tails_step(ODD, k, [to_odd], kept, state)
+        own, kept = tails_step(ODD, k, to_odd, kept, state)
         arrived = to_even
-        to_even = [send_or_swap(own, distance, ODD)]
+        to_even = send_or_swap(own, distance, ODD)
         if k < rounds - 1:
             state = heads_step(ODD, k, kept, state)
         state = heads_step(EVEN, k, kept, state)
         own, kept = tails_step(EVEN, k, arrived, kept, state)
         to_odd = send_or_swap(own, distance, EVEN)
     head, hacc = call(last_heads(tasks), [VMEM] * 7, [block, row], [], [state[0], state[1], state[4]] + kept)
-    tail, tacc = call(pick_tails(width), [VMEM] * 2, [block, row], [], [to_even[0], to_odd])
+    tail, tacc = call(pick_tails(width), [VMEM] * 2, [block, row], [], [to_even, to_odd])
     return head.T, tail.T, hacc.reshape(rows), tacc.reshape(rows)
 
 

time: 53.5 us -> 48.8 us (0.912)
  the two profiles are of different devices: /device:TPU:126 before, /device:TPU:123 now
where the time goes in v6:
time: 48.8 us; the launch traced here: 48.6 us
  starting transfers between devices  17.7 us (36%)
  waiting for transfers between devices  16.7 us (34%)
  Pallas kernels  13.5 us (28%)
  between operations  0.77 us (2%)
    ppermute x8, starting transfers between devices, send_or_swap(): lax.ppermute(block, 'blk', [(i, (i + distance) % n if i % 2 == mine else...  17.7 us
    ppermute x8, waiting for transfers between devices, send_or_swap(): lax.ppermute(block, 'blk', [(i, (i + distance) % n if i % 2 == mine else...  16.7 us
    pallas_call x17, Pallas kernels, call(): pl.pallas_call(body, in_specs=ins, out_specs=[VMEM] * len(outs), out_shap...  13.5 us
  transfers between devices with their start and end apart: 8, of which 3 were waited for; matrix products, arithmetic and copies ran while one was open for 0% of the time, Pallas kernels for 18%

profile of v6, /device:TPU:123, one launch (start us, length us, event | category | flops | bytes accessed | tf_op | source)
XLA Modules:
  0.0 48.6 jit_solution(888648866699183694)
XLA Ops:
  0.6 2.9 %shard_map.120 = (f32[408,128]{1,0:T(8,128)S(1)}, bf16[400,128]{1,0:T(8,128)(2,1)S(1)}, bf16[400,128]{1,0:T(8,128)(2,1)S(1)}, bf16[128,640]{1,0:T(8,128)(2,1)S(1...) custom-call(s32[1,4]{1,0:T(1,128)} %bitcast.17, ...), custom_call_target="tpu_custom_call" | custom-call | flops 1000000000 | bytes 1048576 | tf_op jit(solution)/shard_map/pallas_call | solution.py:196
  3.6 1.1 %shard_map.121 = (f32[408,128]{1,0:T(8,128)S(1)}, bf16[400,128]{1,0:T(8,128)(2,1)S(1)}, bf16[400,128]{1,0:T(8,128)(2,1)S(1)}, bf16[128,640]{1,0:T(8,128)(2,1)S(1)}, bf16[128,640]{1,0:T(8,128)(2,1)S(1)}) custom-call(f32[408,128]{1,0:T(8,128)S(1)} %get-tuple-element.105.tail_in, ...), custom_call_target="tpu_custom_call", output_to_operand_aliasing={{1}: (5, {}), {2}: (6, {}), {3}: (7, {}), {4}: (8, {})} | custom-call | flops 1000000000 | bytes 1048576 | tf_op jit(solution)/shard_map/pallas_call | solution.py:196
  4.7 0.8 %collective-permute-start = (f32[408,128]{1,0:T(8,128)S(1)}, f32[408,128]{1,0:T(8,128)S(1)}, u32[]{:S(2)}, u32[]{:S(2)}) collective-permute-start(f32[408,128]{1,0:T(8,128)S(1)} %get-tuple-element.117), channel_id=1, source_target_pairs={{0,2},{2,0},{4,6},{6,4},{8,10},{10,8},{12,14},{14,12},{16,18},{18,... | collective-permute-start | bytes 626696 | tf_op jit(solution)/shard_map/ppermute | solution.py:210
  5.5 1.8 %collective-permute-start.2 = (f32[408,128]{1,0:T(8,128)S(1)}, f32[408,128]{1,0:T(8,128)S(1)}, u32[]{:S(2)}, u32[]{:S(2)}) collective-permute-start(f32[408,128]{1,0:T(8,128)S(1)} %get-tuple-element.129), channel_id=1, source_target_pairs={{0,2},{2,4},{4,6},{6,8},{8,10},{10,12},{12,14},{14,16},{16,18},{18... | collective-permute-start | bytes 626696 | tf_op jit(solution)/shard_map/ppermute | solution.py:210
  7.3 1.4 %shard_map.123 = (f32[400,128]{1,0:T(8,128)S(1)}, f32[1,128]{1,0:T(1,128)S(1)}, bf16[400,640]{1,0:T(8,128)(2,1)S(1)}, bf16[400,640]{1,0:T(8,128)(2,1)S(1)}, bf16...) custom-call(s32[20,8,128]{2,1,0:T(8,128)S(1)} %get-tuple-element.100, ...), custom_call_target="tpu_custom_call", output_to_operand_aliasing={{0}: (9, {}), {1}: (10, {}), {2}: (11, {}), {3}: (12, {}), ... | custom-call | flops 1000000000 | bytes 1048576 | tf_op jit(solution)/shard_map/pallas_call | solution.py:196
  8.7 0.0 collective-permute-done.tail_in
  8.7 1.1 %shard_map.124 = (f32[408,128]{1,0:T(8,128)S(1)}, bf16[400,128]{1,0:T(8,128)(2,1)S(1)}, bf16[400,128]{1,0:T(8,128)(2,1)S(1)}, bf16[128,640]{1,0:T(8,128)(2,1)S(1)}, bf16[128,640]{1,0:T(8,128)(2,1)S(1)}) custom-call(f32[408,128]{1,0:T(8,128)S(1)} %collective-permute-done.tail_in, ...), custom_call_target="tpu_custom_call", output_to_operand_aliasing={{1}: (5, {}), {2}: (6, {}), {3}: (7, {}), {4}: (8, {})} | custom-call | flops 1000000000 | bytes 1048576 | tf_op jit(solution)/shard_map/pallas_call | solution.py:196
  9.8 1.7 %shard_map.125 = (f32[400,128]{1,0:T(8,128)S(1)}, f32[1,128]{1,0:T(1,128)S(1)}, bf16[400,640]{1,0:T(8,128)(2,1)S(1)}, bf16[400,640]{1,0:T(8,128)(2,1)S(1)}, bf16...) custom-call(s32[20,8,128]{2,1,0:T(8,128)S(1)} %get-tuple-element.100, ...), custom_call_target="tpu_custom_call", output_to_operand_aliasing={{0}: (9, {}), {1}: (10, {}), {2}: (11, {}), {3}: (12, {}), ... | custom-call | flops 1000000000 | bytes 1048576 | tf_op jit(solution)/shard_map/pallas_call | solution.py:196
  11.5 0.0 collective-permute-done.2.tail_in
  11.6 2.8 %collective-permute-start.3 = (f32[408,128]{1,0:T(8,128)S(1)}, f32[408,128]{1,0:T(8,128)S(1)}, u32[]{:S(2)}, u32[]{:S(2)}) collective-permute-start(f32[408,128]{1,0:T(8,128)S(1)} %get-tuple-element.146), channel_id=1, source_target_pairs={{0,2},{2,0},{4,6},{6,4},{8,10},{10,8},{12,14},{14,12},{16,18},{18,... | collective-permute-start | bytes 626696 | tf_op jit(solution)/shard_map/ppermute | solution.py:210
  14.3 1.1 %collective-permute-start.1 = (f32[408,128]{1,0:T(8,128)S(1)}, f32[408,128]{1,0:T(8,128)S(1)}, u32[]{:S(2)}, u32[]{:S(2)}) collective-permute-start(f32[408,128]{1,0:T(8,128)S(1)} %get-tuple-element.128), channel_id=1, source_target_pairs={{0,2},{2,4},{4,6},{6,8},{8,10},{10,12},{12,14},{14,16},{16,18},{18... | collective-permute-start | bytes 626696 | tf_op jit(solution)/shard_map/ppermute | solution.py:210
  15.4 0.0 collective-permute-done.3.tail_in
  15.4 1.1 %shard_map.128 = (f32[408,128]{1,0:T(8,128)S(1)}, bf16[400,128]{1,0:T(8,128)(2,1)S(1)}, bf16[400,128]{1,0:T(8,128)(2,1)S(1)}, bf16[128,640]{1,0:T(8,128)(2,1)S(1)}, bf16[128,640]{1,0:T(8,128)(2,1)S(1)}) custom-call(f32[408,128]{1,0:T(8,128)S(1)} %collective-permute-done.3.tail_in, ...), custom_call_target="tpu_custom_call", output_to_operand_aliasing={{1}: (5, {}), {2}: (6, {}), {3}: (7, {}), {4}: (8, {})} | custom-call | flops 1000000000 | bytes 1048576 | tf_op jit(solution)/shard_map/pallas_call | solution.py:196
  16.5 1.1 %shard_map.129 = (f32[400,128]{1,0:T(8,128)S(1)}, f32[1,128]{1,0:T(1,128)S(1)}, bf16[400,640]{1,0:T(8,128)(2,1)S(1)}, bf16[400,640]{1,0:T(8,128)(2,1)S(1)}, bf16...) custom-call(s32[20,8,128]{2,1,0:T(8,128)S(1)} %get-tuple-element.100, ...), custom_call_target="tpu_custom_call", output_to_operand_aliasing={{0}: (9, {}), {1}: (10, {}), {2}: (11, {}), {3}: (12, {}), ... | custom-call | flops 1000000000 | bytes 1048576 | tf_op jit(solution)/shard_map/pallas_call | solution.py:196
  17.6 0.5 %collective-permute-done.1.tail_in = f32[408,128]{1,0:T(8,128)S(1)} collective-permute-done((f32[408,128]{1,0:T(8,128)S(1)}, f32[408,128]{1,0:T(8,128)S(1)}, u32[]{:S(2)}, u32[]{:S(2)}) %collective-permute-start.1) | collective-permute-done | bytes 208928 | tf_op jit(solution)/shard_map/ppermute | solution.py:210
  18.2 5.0 %collective-permute-start.4 = (f32[408,128]{1,0:T(8,128)S(1)}, f32[408,128]{1,0:T(8,128)S(1)}, u32[]{:S(2)}, u32[]{:S(2)}) collective-permute-start(f32[408,128]{1,0:T(8,128)S(1)} %get-tuple-element.167), channel_id=1, source_target_pairs={{0,2},{2,0},{4,6},{6,4},{8,10},{10,8},{12,14},{14,12},{16,18},{18,... | collective-permute-start | bytes 626696 | tf_op jit(solution)/shard_map/ppermute | solution.py:210
  23.2 2.8 %collective-permute-start.5 = (f32[408,128]{1,0:T(8,128)S(1)}, f32[408,128]{1,0:T(8,128)S(1)}, u32[]{:S(2)}, u32[]{:S(2)}) collective-permute-start(f32[408,128]{1,0:T(8,128)S(1)} %get-tuple-element.182), channel_id=1, source_target_pairs={{0,2},{2,4},{4,6},{6,8},{8,10},{10,12},{12,14},{14,16},{16,18},{18... | collective-permute-start | bytes 626696 | tf_op jit(solution)/shard_map/ppermute | solution.py:210
  26.0 1.1 %shard_map.132 = (f32[408,128]{1,0:T(8,128)S(1)}, bf16[400,128]{1,0:T(8,128)(2,1)S(1)}, bf16[400,128]{1,0:T(8,128)(2,1)S(1)}, bf16[128,640]{1,0:T(8,128)(2,1)S(1)}, bf16[128,640]{1,0:T(8,128)(2,1)S(1)}) custom-call(f32[408,128]{1,0:T(8,128)S(1)} %collective-permute-done.4.tail_in, ...), custom_call_target="tpu_custom_call", output_to_operand_aliasing={{1}: (5, {}), {2}: (6, {}), {3}: (7, {}), {4}: (8, {})} | custom-call | flops 1000000000 | bytes 1048576 | tf_op jit(solution)/shard_map/pallas_call | solution.py:196
  27.0 0.1 collective-permute-start.6
  27.2 1.6 %collective-permute-done.5.tail_in = f32[408,128]{1,0:T(8,128)S(1)} collective-permute-done((f32[408,128]{1,0:T(8,128)S(1)}, f32[408,128]{1,0:T(8,128)S(1)}, u32[]{:S(2)}, u32[]{:S(2)}) %collective-permute-start.5) | collective-permute-done | bytes 208928 | tf_op jit(solution)/shard_map/ppermute | solution.py:210
  28.7 3.3 %collective-permute-start.7 = (f32[408,128]{1,0:T(8,128)S(1)}, f32[408,128]{1,0:T(8,128)S(1)}, u32[]{:S(2)}, u32[]{:S(2)}) collective-permute-start(f32[408,128]{1,0:T(8,128)S(1)} %get-tuple-element.192), channel_id=1, source_target_pairs={{0,250},{2,0},{4,254},{6,4},{8,2},{10,8},{12,6},{14,12},{16,10},{1... | collective-permute-start | bytes 626696 | tf_op jit(solution)/shard_map/ppermute | solution.py:210
  32.1 1.2 %shard_map.135 = (f32[400,128]{1,0:T(8,128)}, f32[1,128]{1,0:T(1,128)}) custom-call(f32[400,128]{1,0:T(8,128)S(1)} %get-tuple-element.179.head, f32[1,128]{1,0:T(1,128)S(1)} %get-tuple-element.180.hacc, bf16[400,640]{1,0:T(8,128)(2,1)S(1)} %get-tuple-element.181.rel_in, bf16[400,128]{1,0:T(8,128)(2,1)S(1)} %get-tuple-element.186.thi, ...), custom_call_target="tpu_custom_call" | custom-call | flops 1000000000 | bytes 1048576 | tf_op jit(solution)/shard_map/pallas_call | solution.py:196
  33.3 14.6 %collective-permute-done.7.from_even = f32[408,128]{1,0:T(8,128)S(1)} collective-permute-done((f32[408,128]{1,0:T(8,128)S(1)}, f32[408,128]{1,0:T(8,128)S(1)}, u32[]{:S(2)}, u32[]{:S(2)}) %collective-permute-start.7) | collective-permute-done | bytes 208928 | tf_op jit(solution)/shard_map/ppermute | solution.py:210
  47.9 0.7 %shard_map.136 = (f32[400,128]{1,0:T(8,128)}, f32[1,128]{1,0:T(1,128)}) custom-call(f32[408,128]{1,0:T(8,128)S(1)} %collective-permute-done.6.from_odd, f32[408,128]{1,0:T(8,128)S(1)} %collective-permute-done.7.from_even), custom_call_target="tpu_custom_call" | custom-call | flops 1000000000 | bytes 1048576 | tf_op jit(solution)/shard_map/pallas_call | solution.py:196
  (9 shorter events, 0.1 us)
Async XLA Ops:
  4.7 4.0 %collective-permute-start = (f32[408,128]{1,0:T(8,128)S(1)}, f32[408,128]{1,0:T(8,128)S(1)}, u32[]{:S(2)}, u32[]{:S(2)}) collective-permute-start(f32[408,128]{1,0:T(8,128)S(1)} %get-tuple-element.117), channel_id=1, source_target_pairs={{0,2},{2,0},{4,6},{6,4},{8,10},{10,8},{12,14},{14,12},{16,18},{18,... | collective-permute-start | bytes 626696 | tf_op jit(solution)/shard_map/ppermute | solution.py:210
  5.5 6.1 %collective-permute-start.2 = (f32[408,128]{1,0:T(8,128)S(1)}, f32[408,128]{1,0:T(8,128)S(1)}, u32[]{:S(2)}, u32[]{:S(2)}) collective-permute-start(f32[408,128]{1,0:T(8,128)S(1)} %get-tuple-element.129), channel_id=1, source_target_pairs={{0,2},{2,4},{4,6},{6,8},{8,10},{10,12},{12,14},{14,16},{16,18},{18... | collective-permute-start | bytes 626696 | tf_op jit(solution)/shard_map/ppermute | solution.py:210
  11.6 3.8 %collective-permute-start.3 = (f32[408,128]{1,0:T(8,128)S(1)}, f32[408,128]{1,0:T(8,128)S(1)}, u32[]{:S(2)}, u32[]{:S(2)}) collective-permute-start(f32[408,128]{1,0:T(8,128)S(1)} %get-tuple-element.146), channel_id=1, source_target_pairs={{0,2},{2,0},{4,6},{6,4},{8,10},{10,8},{12,14},{14,12},{16,18},{18,... | collective-permute-start | bytes 626696 | tf_op jit(solution)/shard_map/ppermute | solution.py:210
  14.3 3.8 %collective-permute-start.1 = (f32[408,128]{1,0:T(8,128)S(1)}, f32[408,128]{1,0:T(8,128)S(1)}, u32[]{:S(2)}, u32[]{:S(2)}) collective-permute-start(f32[408,128]{1,0:T(8,128)S(1)} %get-tuple-element.128), channel_id=1, source_target_pairs={{0,2},{2,4},{4,6},{6,8},{8,10},{10,12},{12,14},{14,16},{16,18},{18... | collective-permute-start | bytes 626696 | tf_op jit(solution)/shard_map/ppermute | solution.py:210
  18.2 7.8 %collective-permute-start.4 = (f32[408,128]{1,0:T(8,128)S(1)}, f32[408,128]{1,0:T(8,128)S(1)}, u32[]{:S(2)}, u32[]{:S(2)}) collective-permute-start(f32[408,128]{1,0:T(8,128)S(1)} %get-tuple-element.167), channel_id=1, source_target_pairs={{0,2},{2,0},{4,6},{6,4},{8,10},{10,8},{12,14},{14,12},{16,18},{18,... | collective-permute-start | bytes 626696 | tf_op jit(solution)/shard_map/ppermute | solution.py:210
  23.2 5.5 %collective-permute-start.5 = (f32[408,128]{1,0:T(8,128)S(1)}, f32[408,128]{1,0:T(8,128)S(1)}, u32[]{:S(2)}, u32[]{:S(2)}) collective-permute-start(f32[408,128]{1,0:T(8,128)S(1)} %get-tuple-element.182), channel_id=1, source_target_pairs={{0,2},{2,4},{4,6},{6,8},{8,10},{10,12},{12,14},{14,16},{16,18},{18... | collective-permute-start | bytes 626696 | tf_op jit(solution)/shard_map/ppermute | solution.py:210
  27.0 6.2 %collective-permute-start.6 = (f32[408,128]{1,0:T(8,128)S(1)}, f32[408,128]{1,0:T(8,128)S(1)}, u32[]{:S(2)}, u32[]{:S(2)}) collective-permute-start(f32[408,128]{1,0:T(8,128)S(1)} %get-tuple-element.191), channel_id=1, source_target_pairs={{0,2},{2,252},{4,6},{6,0},{8,10},{10,4},{12,14},{14,8},{16,18},{18... | collective-permute-start | bytes 626696 | tf_op jit(solution)/shard_map/ppermute | solution.py:210
  28.7 19.2 %collective-permute-start.7 = (f32[408,128]{1,0:T(8,128)S(1)}, f32[408,128]{1,0:T(8,128)S(1)}, u32[]{:S(2)}, u32[]{:S(2)}) collective-permute-start(f32[408,128]{1,0:T(8,128)S(1)} %get-tuple-element.192), channel_id=1, source_target_pairs={{0,250},{2,0},{4,254},{6,4},{8,2},{10,8},{12,6},{14,12},{16,10},{1... | collective-permute-start | bytes 626696 | tf_op jit(solution)/shard_map/ppermute | solution.py:210

commit v7 on v6

--- a/solution.py
+++ b/solution.py
@@ -116,8 +116,9 @@
             copy.start()
         copies[0].wait()
         rels = [rel_copies(rel_ids, rel_ref, rel_buf, rel_sem, k, tasks) for k in range(rounds)]
-        for copy in rels[0]:
-            copy.start()
+        for group in rels:
+            for copy in group:
+                copy.start()
         for copy in copies[1:4]:
             copy.wait()
         for k in range(rounds):
@@ -125,9 +126,6 @@
                 lanes[k * tasks + s] = jnp.full(lanes.shape[1:], lax.rem(rel_ids[k, 0, s], LANES), I32)
                 gain[k * tasks + s] = jnp.full(gain.shape[1:], jnp.where(s < counts[0, k], HALF_NEG, 0.0), F32)
         make_labels(labels_ref, he, te, gain, 0, 0, tasks)
-        for group in rels[1:]:
-            for copy in group:
-                copy.start()
         for copy in rels[0] + copies[4:]:
             copy.wait()
         tail_out[pl.ds(width, 8), :] = jnp.broadcast_to(tacc[...], (8, LANES))
@@ -180,13 +178,18 @@
     return body
 
 
-def pick_tails(width):
-    def body(from_odd, from_even, tail_out, tacc_out):
-        for mine, ref in ((EVEN, from_odd), (ODD, from_even)):
-            @pl.when(role() == mine)
-            def _():
-                tail_out[...] = ref[pl.ds(0, width), :]
-                tacc_out[...] = ref[pl.ds(width, 1), :]
+def pick_tails(mine, width):
+    def body(packed, *refs):
+        tail_out, tacc_out, row, sem = refs[-4:]
+
+        @pl.when(role() == mine)
+        def _():
+            row[...] = packed[pl.ds(width, 1), :]
+            copies = [pltpu.make_async_copy(packed.at[pl.ds(0, width)], tail_out, sem.at[0]), pltpu.make_async_copy(row, tacc_out, sem.at[1])]
+            for copy in copies:
+                copy.start()
+            for copy in copies:
+                copy.wait()
 
     return body
 
@@ -258,7 +261,18 @@
         own, kept = tails_step(EVEN, k, arrived, kept, state)
         to_odd = send_or_swap(own, distance, EVEN)
     head, hacc = call(last_heads(tasks), [VMEM] * 7, [block, row], [], [state[0], state[1], state[4]] + kept)
-    tail, tacc = call(pick_tails(width), [VMEM] * 2, [block, row], [], [to_even, to_odd])
+    results = []
+    for mine, packed_in in ((EVEN, to_even), (ODD, to_odd)):
+        results = pl.pallas_call(
+            pick_tails(mine, width),
+            in_specs=[VMEM] + [HBM] * len(results),
+            out_specs=[HBM] * 2,
+            out_shape=[pltpu.HBM(*block), pltpu.HBM(*row)],
+            scratch_shapes=[pltpu.VMEM(*row), pltpu.SemaphoreType.DMA((2,))],
+            input_output_aliases={1 + i: i for i in range(len(results))},
+            compiler_params=pltpu.CompilerParams(vmem_limit_bytes=16 << 20),
+        )(packed_in, *results)
+    tail, tacc = results
     return head.T, tail.T, hacc.reshape(rows), tacc.reshape(rows)
 
 

time: 48.8 us -> 48.6 us (level)
    pallas_call x17 -> x16, Pallas kernels: 13.5 us -> 12.4 us  [call(): pl.pallas_call(body, in_specs=ins, out_specs=[VMEM] * len(outs), out_shap...]
    pallas_call x0 -> x2, Pallas kernels: none -> 0.72 us  [on_device(): pl.pallas_call(pick_tails(mine, width), in_specs=[VMEM] + [HBM] * len(res...]
where the time goes in v7:
time: 48.6 us; the launch traced here: 48.4 us
  starting transfers between devices  17.7 us (36%)
  waiting for transfers between devices  16.7 us (34%)
  Pallas kernels  13.1 us (27%)
  between operations  0.94 us (2%)
    ppermute x8, starting transfers between devices, send_or_swap(): lax.ppermute(block, 'blk', [(i, (i + distance) % n if i % 2 == mine else...  17.7 us
    ppermute x8, waiting for transfers between devices, send_or_swap(): lax.ppermute(block, 'blk', [(i, (i + distance) % n if i % 2 == mine else...  16.7 us
    pallas_call x16, Pallas kernels, call(): pl.pallas_call(body, in_specs=ins, out_specs=[VMEM] * len(outs), out_shap...  12.4 us
  transfers between devices with their start and end apart: 8, of which 3 were waited for; matrix products, arithmetic and copies ran while one was open for 0% of the time, Pallas kernels for 18%

profile of v7, /device:TPU:123, one launch (start us, length us, event | category | flops | bytes accessed | tf_op | source)
XLA Modules:
  0.0 48.4 jit_solution(11949829085908757401)
XLA Ops:
  0.6 2.6 %shard_map.120 = (f32[408,128]{1,0:T(8,128)S(1)}, bf16[400,128]{1,0:T(8,128)(2,1)S(1)}, bf16[400,128]{1,0:T(8,128)(2,1)S(1)}, bf16[128,640]{1,0:T(8,128)(2,1)S(1...) custom-call(s32[1,4]{1,0:T(1,128)} %bitcast.19, ...), custom_call_target="tpu_custom_call" | custom-call | flops 1000000000 | bytes 1048576 | tf_op jit(solution)/shard_map/pallas_call | solution.py:199
  3.2 1.1 %shard_map.121 = (f32[408,128]{1,0:T(8,128)S(1)}, bf16[400,128]{1,0:T(8,128)(2,1)S(1)}, bf16[400,128]{1,0:T(8,128)(2,1)S(1)}, bf16[128,640]{1,0:T(8,128)(2,1)S(1)}, bf16[128,640]{1,0:T(8,128)(2,1)S(1)}) custom-call(f32[408,128]{1,0:T(8,128)S(1)} %get-tuple-element.107.tail_in, ...), custom_call_target="tpu_custom_call", output_to_operand_aliasing={{1}: (5, {}), {2}: (6, {}), {3}: (7, {}), {4}: (8, {})} | custom-call | flops 1000000000 | bytes 1048576 | tf_op jit(solution)/shard_map/pallas_call | solution.py:199
  4.3 0.8 %collective-permute-start = (f32[408,128]{1,0:T(8,128)S(1)}, f32[408,128]{1,0:T(8,128)S(1)}, u32[]{:S(2)}, u32[]{:S(2)}) collective-permute-start(f32[408,128]{1,0:T(8,128)S(1)} %get-tuple-element.119), channel_id=1, source_target_pairs={{0,2},{2,0},{4,6},{6,4},{8,10},{10,8},{12,14},{14,12},{16,18},{18,... | collective-permute-start | bytes 626696 | tf_op jit(solution)/shard_map/ppermute | solution.py:213
  5.1 1.8 %collective-permute-start.2 = (f32[408,128]{1,0:T(8,128)S(1)}, f32[408,128]{1,0:T(8,128)S(1)}, u32[]{:S(2)}, u32[]{:S(2)}) collective-permute-start(f32[408,128]{1,0:T(8,128)S(1)} %get-tuple-element.131), channel_id=1, source_target_pairs={{0,2},{2,4},{4,6},{6,8},{8,10},{10,12},{12,14},{14,16},{16,18},{18... | collective-permute-start | bytes 626696 | tf_op jit(solution)/shard_map/ppermute | solution.py:213
  6.9 1.4 %shard_map.123 = (f32[400,128]{1,0:T(8,128)S(1)}, f32[1,128]{1,0:T(1,128)S(1)}, bf16[400,640]{1,0:T(8,128)(2,1)S(1)}, bf16[400,640]{1,0:T(8,128)(2,1)S(1)}, bf16...) custom-call(s32[20,8,128]{2,1,0:T(8,128)S(1)} %get-tuple-element.102, ...), custom_call_target="tpu_custom_call", output_to_operand_aliasing={{0}: (9, {}), {1}: (10, {}), {2}: (11, {}), {3}: (12, {}), ... | custom-call | flops 1000000000 | bytes 1048576 | tf_op jit(solution)/shard_map/pallas_call | solution.py:199
  8.4 0.0 collective-permute-done.tail_in
  8.4 1.1 %shard_map.124 = (f32[408,128]{1,0:T(8,128)S(1)}, bf16[400,128]{1,0:T(8,128)(2,1)S(1)}, bf16[400,128]{1,0:T(8,128)(2,1)S(1)}, bf16[128,640]{1,0:T(8,128)(2,1)S(1)}, bf16[128,640]{1,0:T(8,128)(2,1)S(1)}) custom-call(f32[408,128]{1,0:T(8,128)S(1)} %collective-permute-done.tail_in, ...), custom_call_target="tpu_custom_call", output_to_operand_aliasing={{1}: (5, {}), {2}: (6, {}), {3}: (7, {}), {4}: (8, {})} | custom-call | flops 1000000000 | bytes 1048576 | tf_op jit(solution)/shard_map/pallas_call | solution.py:199
  9.4 1.7 %shard_map.125 = (f32[400,128]{1,0:T(8,128)S(1)}, f32[1,128]{1,0:T(1,128)S(1)}, bf16[400,640]{1,0:T(8,128)(2,1)S(1)}, bf16[400,640]{1,0:T(8,128)(2,1)S(1)}, bf16...) custom-call(s32[20,8,128]{2,1,0:T(8,128)S(1)} %get-tuple-element.102, ...), custom_call_target="tpu_custom_call", output_to_operand_aliasing={{0}: (9, {}), {1}: (10, {}), {2}: (11, {}), {3}: (12, {}), ... | custom-call | flops 1000000000 | bytes 1048576 | tf_op jit(solution)/shard_map/pallas_call | solution.py:199
  11.2 2.8 %collective-permute-start.3 = (f32[408,128]{1,0:T(8,128)S(1)}, f32[408,128]{1,0:T(8,128)S(1)}, u32[]{:S(2)}, u32[]{:S(2)}) collective-permute-start(f32[408,128]{1,0:T(8,128)S(1)} %get-tuple-element.148), channel_id=1, source_target_pairs={{0,2},{2,0},{4,6},{6,4},{8,10},{10,8},{12,14},{14,12},{16,18},{18,... | collective-permute-start | bytes 626696 | tf_op jit(solution)/shard_map/ppermute | solution.py:213
  14.0 1.1 %collective-permute-start.1 = (f32[408,128]{1,0:T(8,128)S(1)}, f32[408,128]{1,0:T(8,128)S(1)}, u32[]{:S(2)}, u32[]{:S(2)}) collective-permute-start(f32[408,128]{1,0:T(8,128)S(1)} %get-tuple-element.130), channel_id=1, source_target_pairs={{0,2},{2,4},{4,6},{6,8},{8,10},{10,12},{12,14},{14,16},{16,18},{18... | collective-permute-start | bytes 626696 | tf_op jit(solution)/shard_map/ppermute | solution.py:213
  15.1 0.0 collective-permute-done.3.tail_in
  15.1 1.1 %shard_map.128 = (f32[408,128]{1,0:T(8,128)S(1)}, bf16[400,128]{1,0:T(8,128)(2,1)S(1)}, bf16[400,128]{1,0:T(8,128)(2,1)S(1)}, bf16[128,640]{1,0:T(8,128)(2,1)S(1)}, bf16[128,640]{1,0:T(8,128)(2,1)S(1)}) custom-call(f32[408,128]{1,0:T(8,128)S(1)} %collective-permute-done.3.tail_in, ...), custom_call_target="tpu_custom_call", output_to_operand_aliasing={{1}: (5, {}), {2}: (6, {}), {3}: (7, {}), {4}: (8, {})} | custom-call | flops 1000000000 | bytes 1048576 | tf_op jit(solution)/shard_map/pallas_call | solution.py:199
  16.1 1.1 %shard_map.129 = (f32[400,128]{1,0:T(8,128)S(1)}, f32[1,128]{1,0:T(1,128)S(1)}, bf16[400,640]{1,0:T(8,128)(2,1)S(1)}, bf16[400,640]{1,0:T(8,128)(2,1)S(1)}, bf16...) custom-call(s32[20,8,128]{2,1,0:T(8,128)S(1)} %get-tuple-element.102, ...), custom_call_target="tpu_custom_call", output_to_operand_aliasing={{0}: (9, {}), {1}: (10, {}), {2}: (11, {}), {3}: (12, {}), ... | custom-call | flops 1000000000 | bytes 1048576 | tf_op jit(solution)/shard_map/pallas_call | solution.py:199
  17.3 0.5 %collective-permute-done.1.tail_in = f32[408,128]{1,0:T(8,128)S(1)} collective-permute-done((f32[408,128]{1,0:T(8,128)S(1)}, f32[408,128]{1,0:T(8,128)S(1)}, u32[]{:S(2)}, u32[]{:S(2)}) %collective-permute-start.1) | collective-permute-done | bytes 208928 | tf_op jit(solution)/shard_map/ppermute | solution.py:213
  17.8 5.0 %collective-permute-start.4 = (f32[408,128]{1,0:T(8,128)S(1)}, f32[408,128]{1,0:T(8,128)S(1)}, u32[]{:S(2)}, u32[]{:S(2)}) collective-permute-start(f32[408,128]{1,0:T(8,128)S(1)} %get-tuple-element.169), channel_id=1, source_target_pairs={{0,2},{2,0},{4,6},{6,4},{8,10},{10,8},{12,14},{14,12},{16,18},{18,... | collective-permute-start | bytes 626696 | tf_op jit(solution)/shard_map/ppermute | solution.py:213
  22.9 2.8 %collective-permute-start.5 = (f32[408,128]{1,0:T(8,128)S(1)}, f32[408,128]{1,0:T(8,128)S(1)}, u32[]{:S(2)}, u32[]{:S(2)}) collective-permute-start(f32[408,128]{1,0:T(8,128)S(1)} %get-tuple-element.184), channel_id=1, source_target_pairs={{0,2},{2,4},{4,6},{6,8},{8,10},{10,12},{12,14},{14,16},{16,18},{18... | collective-permute-start | bytes 626696 | tf_op jit(solution)/shard_map/ppermute | solution.py:213
  25.6 0.0 collective-permute-done.4.tail_in
  25.6 1.1 %shard_map.132 = (f32[408,128]{1,0:T(8,128)S(1)}, bf16[400,128]{1,0:T(8,128)(2,1)S(1)}, bf16[400,128]{1,0:T(8,128)(2,1)S(1)}, bf16[128,640]{1,0:T(8,128)(2,1)S(1)}, bf16[128,640]{1,0:T(8,128)(2,1)S(1)}) custom-call(f32[408,128]{1,0:T(8,128)S(1)} %collective-permute-done.4.tail_in, ...), custom_call_target="tpu_custom_call", output_to_operand_aliasing={{1}: (5, {}), {2}: (6, {}), {3}: (7, {}), {4}: (8, {})} | custom-call | flops 1000000000 | bytes 1048576 | tf_op jit(solution)/shard_map/pallas_call | solution.py:199
  26.7 0.1 collective-permute-start.7
  26.8 1.6 %collective-permute-done.5.tail_in = f32[408,128]{1,0:T(8,128)S(1)} collective-permute-done((f32[408,128]{1,0:T(8,128)S(1)}, f32[408,128]{1,0:T(8,128)S(1)}, u32[]{:S(2)}, u32[]{:S(2)}) %collective-permute-start.5) | collective-permute-done | bytes 208928 | tf_op jit(solution)/shard_map/ppermute | solution.py:213
  28.4 3.3 %collective-permute-start.6 = (f32[408,128]{1,0:T(8,128)S(1)}, f32[408,128]{1,0:T(8,128)S(1)}, u32[]{:S(2)}, u32[]{:S(2)}) collective-permute-start(f32[408,128]{1,0:T(8,128)S(1)} %get-tuple-element.193), channel_id=1, source_target_pairs={{0,250},{2,0},{4,254},{6,4},{8,2},{10,8},{12,6},{14,12},{16,10},{1... | collective-permute-start | bytes 626696 | tf_op jit(solution)/shard_map/ppermute | solution.py:213
  31.7 1.2 %shard_map.135 = (f32[400,128]{1,0:T(8,128)}, f32[1,128]{1,0:T(1,128)}) custom-call(f32[400,128]{1,0:T(8,128)S(1)} %get-tuple-element.181.head, f32[1,128]{1,0:T(1,128)S(1)} %get-tuple-element.182.hacc, bf16[400,640]{1,0:T(8,128)(2,1)S(1)} %get-tuple-element.183.rel_in, bf16[400,128]{1,0:T(8,128)(2,1)S(1)} %get-tuple-element.188.thi, ...), custom_call_target="tpu_custom_call" | custom-call | flops 1000000000 | bytes 1048576 | tf_op jit(solution)/shard_map/pallas_call | solution.py:199
  33.0 14.6 %collective-permute-done.6.packed = f32[408,128]{1,0:T(8,128)S(1)} collective-permute-done((f32[408,128]{1,0:T(8,128)S(1)}, f32[408,128]{1,0:T(8,128)S(1)}, u32[]{:S(2)}, u32[]{:S(2)}) %collective-permute-start.6) | collective-permute-done | bytes 208928 | tf_op jit(solution)/shard_map/ppermute | solution.py:213
  47.6 0.7 %shard_map.137 = (f32[400,128]{1,0:T(8,128)}, f32[1,128]{1,0:T(1,128)}) custom-call(f32[408,128]{1,0:T(8,128)S(1)} %collective-permute-done.6.packed, f32[400,128]{1,0:T(8,128)} %get-tuple-element.195.refs_0_, f32[1,128]{1,0:T(1,128)} %get-tuple-element.196.refs_1_), custom_call_target="tpu_custom_call", output_to_operand_aliasing={{0}: (1, {}), {1}: (2, {})} | custom-call | tf_op jit(solution)/shard_map/pallas_call | solution.py:266
  (10 shorter events, 0.1 us)
Async XLA Ops:
  4.3 4.0 %collective-permute-start = (f32[408,128]{1,0:T(8,128)S(1)}, f32[408,128]{1,0:T(8,128)S(1)}, u32[]{:S(2)}, u32[]{:S(2)}) collective-permute-start(f32[408,128]{1,0:T(8,128)S(1)} %get-tuple-element.119), channel_id=1, source_target_pairs={{0,2},{2,0},{4,6},{6,4},{8,10},{10,8},{12,14},{14,12},{16,18},{18,... | collective-permute-start | bytes 626696 | tf_op jit(solution)/shard_map/ppermute | solution.py:213
  5.1 6.1 %collective-permute-start.2 = (f32[408,128]{1,0:T(8,128)S(1)}, f32[408,128]{1,0:T(8,128)S(1)}, u32[]{:S(2)}, u32[]{:S(2)}) collective-permute-start(f32[408,128]{1,0:T(8,128)S(1)} %get-tuple-element.131), channel_id=1, source_target_pairs={{0,2},{2,4},{4,6},{6,8},{8,10},{10,12},{12,14},{14,16},{16,18},{18... | collective-permute-start | bytes 626696 | tf_op jit(solution)/shard_map/ppermute | solution.py:213
  11.2 3.9 %collective-permute-start.3 = (f32[408,128]{1,0:T(8,128)S(1)}, f32[408,128]{1,0:T(8,128)S(1)}, u32[]{:S(2)}, u32[]{:S(2)}) collective-permute-start(f32[408,128]{1,0:T(8,128)S(1)} %get-tuple-element.148), channel_id=1, source_target_pairs={{0,2},{2,0},{4,6},{6,4},{8,10},{10,8},{12,14},{14,12},{16,18},{18,... | collective-permute-start | bytes 626696 | tf_op jit(solution)/shard_map/ppermute | solution.py:213
  14.0 3.8 %collective-permute-start.1 = (f32[408,128]{1,0:T(8,128)S(1)}, f32[408,128]{1,0:T(8,128)S(1)}, u32[]{:S(2)}, u32[]{:S(2)}) collective-permute-start(f32[408,128]{1,0:T(8,128)S(1)} %get-tuple-element.130), channel_id=1, source_target_pairs={{0,2},{2,4},{4,6},{6,8},{8,10},{10,12},{12,14},{14,16},{16,18},{18... | collective-permute-start | bytes 626696 | tf_op jit(solution)/shard_map/ppermute | solution.py:213
  17.8 7.8 %collective-permute-start.4 = (f32[408,128]{1,0:T(8,128)S(1)}, f32[408,128]{1,0:T(8,128)S(1)}, u32[]{:S(2)}, u32[]{:S(2)}) collective-permute-start(f32[408,128]{1,0:T(8,128)S(1)} %get-tuple-element.169), channel_id=1, source_target_pairs={{0,2},{2,0},{4,6},{6,4},{8,10},{10,8},{12,14},{14,12},{16,18},{18,... | collective-permute-start | bytes 626696 | tf_op jit(solution)/shard_map/ppermute | solution.py:213
  22.9 5.5 %collective-permute-start.5 = (f32[408,128]{1,0:T(8,128)S(1)}, f32[408,128]{1,0:T(8,128)S(1)}, u32[]{:S(2)}, u32[]{:S(2)}) collective-permute-start(f32[408,128]{1,0:T(8,128)S(1)} %get-tuple-element.184), channel_id=1, source_target_pairs={{0,2},{2,4},{4,6},{6,8},{8,10},{10,12},{12,14},{14,16},{16,18},{18... | collective-permute-start | bytes 626696 | tf_op jit(solution)/shard_map/ppermute | solution.py:213
  26.7 6.2 %collective-permute-start.7 = (f32[408,128]{1,0:T(8,128)S(1)}, f32[408,128]{1,0:T(8,128)S(1)}, u32[]{:S(2)}, u32[]{:S(2)}) collective-permute-start(f32[408,128]{1,0:T(8,128)S(1)} %get-tuple-element.194), channel_id=1, source_target_pairs={{0,2},{2,252},{4,6},{6,0},{8,10},{10,4},{12,14},{14,8},{16,18},{18... | collective-permute-start | bytes 626696 | tf_op jit(solution)/shard_map/ppermute | solution.py:213
  28.4 19.2 %collective-permute-start.6 = (f32[408,128]{1,0:T(8,128)S(1)}, f32[408,128]{1,0:T(8,128)S(1)}, u32[]{:S(2)}, u32[]{:S(2)}) collective-permute-start(f32[408,128]{1,0:T(8,128)S(1)} %get-tuple-element.193), channel_id=1, source_target_pairs={{0,250},{2,0},{4,254},{6,4},{8,2},{10,8},{12,6},{14,12},{16,10},{1... | collective-permute-start | bytes 626696 | tf_op jit(solution)/shard_map/ppermute | solution.py:213

commit v8 on v7

--- a/solution.py
+++ b/solution.py
@@ -59,11 +59,20 @@
 
 
 def scale_heads(head, lanes, rel_buf, k, shi, slo, rel_out, tasks):
-    for s in range(tasks):
-        pick = (lax.broadcasted_iota(I32, (LANES, LANES), 0) == lanes[k * tasks + s, 0:1, :]).astype(F32).astype(BF16)
-        rel = dot(rel_buf[k * tasks + s], pick, NN)
-        rel_out[:, cols(s)] = rel.astype(BF16)
-        shi[:, cols(s)], slo[:, cols(s)] = hi_lo(head * rel)
+    which = lax.broadcasted_iota(I32, (LANES, LANES), 0)
+    for first in range(0, tasks, 2):
+        group = range(first, min(first + 2, tasks))
+        picks = [(which == lanes[k * tasks + s, 0:1, :]).astype(F32).astype(BF16) for s in group]
+        if len(group) == 2:
+            none = jnp.zeros_like(picks[0])
+            pick = jnp.concatenate([jnp.concatenate([picks[0], none], axis=1), jnp.concatenate([none, picks[1]], axis=1)], axis=0)
+        else:
+            pick = picks[0]
+        rel = dot(jnp.concatenate([rel_buf[k * tasks + s] for s in group], axis=1), pick, NN)
+        for i, s in enumerate(group):
+            part = rel[:, i * LANES : (i + 1) * LANES]
+            rel_out[:, cols(s)] = part.astype(BF16)
+            shi[:, cols(s)], slo[:, cols(s)] = hi_lo(head * part)
 
 
 def adagrad(block, state, grad):
@@ -71,7 +80,7 @@
     square, part = grad * grad, width // 5
     square = (square[:part] + square[part : 2 * part]) + (square[2 * part : 3 * part] + square[3 * part : 4 * part]) + square[4 * part :]
     state = state + jnp.sum(square, axis=0, keepdims=True) * (1.0 / width)
-    return block - grad * (LEARN_RATE / jnp.sqrt(state)), state
+    return block - grad * (LEARN_RATE * lax.rsqrt(state)), state
 
 
 def tail_step(tail, state, shi_ref, slo_ref, labels_ref, label_row, gain_ref, gain_row, kept, tail_out, tasks):

time: 48.6 us -> 48.5 us (level)
  the two profiles are of different devices: /device:TPU:123 before, /device:TPU:121 now
where the time goes in v8:
time: 48.5 us; the launch traced here: 48.4 us
  starting transfers between devices  17.6 us (36%)
  waiting for transfers between devices  16.8 us (35%)
  Pallas kernels  13.1 us (27%)
  between operations  0.94 us (2%)
    ppermute x8, starting transfers between devices, send_or_swap(): lax.ppermute(block, 'blk', [(i, (i + distance) % n if i % 2 == mine else...  17.6 us
    ppermute x8, waiting for transfers between devices, send_or_swap(): lax.ppermute(block, 'blk', [(i, (i + distance) % n if i % 2 == mine else...  16.8 us
    pallas_call x16, Pallas kernels, call(): pl.pallas_call(body, in_specs=ins, out_specs=[VMEM] * len(outs), out_shap...  12.3 us
  transfers between devices with their start and end apart: 8, of which 3 were waited for; matrix products, arithmetic and copies ran while one was open for 0% of the time, Pallas kernels for 18%

profile of v8, /device:TPU:121, one launch (start us, length us, event | category | flops | bytes accessed | tf_op | source)
XLA Modules:
  0.0 48.4 jit_solution(15515210980932875612)
XLA Ops:
  0.6 2.6 %shard_map.120 = (f32[408,128]{1,0:T(8,128)S(1)}, bf16[400,128]{1,0:T(8,128)(2,1)S(1)}, bf16[400,128]{1,0:T(8,128)(2,1)S(1)}, bf16[128,640]{1,0:T(8,128)(2,1)S(1...) custom-call(s32[1,4]{1,0:T(1,128)} %bitcast.19, ...), custom_call_target="tpu_custom_call" | custom-call | flops 1000000000 | bytes 1048576 | tf_op jit(solution)/shard_map/pallas_call | solution.py:208
  3.3 1.1 %shard_map.121 = (f32[408,128]{1,0:T(8,128)S(1)}, bf16[400,128]{1,0:T(8,128)(2,1)S(1)}, bf16[400,128]{1,0:T(8,128)(2,1)S(1)}, bf16[128,640]{1,0:T(8,128)(2,1)S(1)}, bf16[128,640]{1,0:T(8,128)(2,1)S(1)}) custom-call(f32[408,128]{1,0:T(8,128)S(1)} %get-tuple-element.107.tail_in, ...), custom_call_target="tpu_custom_call", output_to_operand_aliasing={{1}: (5, {}), {2}: (6, {}), {3}: (7, {}), {4}: (8, {})} | custom-call | flops 1000000000 | bytes 1048576 | tf_op jit(solution)/shard_map/pallas_call | solution.py:208
  4.4 0.7 %collective-permute-start = (f32[408,128]{1,0:T(8,128)S(1)}, f32[408,128]{1,0:T(8,128)S(1)}, u32[]{:S(2)}, u32[]{:S(2)}) collective-permute-start(f32[408,128]{1,0:T(8,128)S(1)} %get-tuple-element.119), channel_id=1, source_target_pairs={{0,2},{2,0},{4,6},{6,4},{8,10},{10,8},{12,14},{14,12},{16,18},{18,... | collective-permute-start | bytes 626696 | tf_op jit(solution)/shard_map/ppermute | solution.py:222
  5.1 2.7 %collective-permute-start.2 = (f32[408,128]{1,0:T(8,128)S(1)}, f32[408,128]{1,0:T(8,128)S(1)}, u32[]{:S(2)}, u32[]{:S(2)}) collective-permute-start(f32[408,128]{1,0:T(8,128)S(1)} %get-tuple-element.131), channel_id=1, source_target_pairs={{0,2},{2,4},{4,6},{6,8},{8,10},{10,12},{12,14},{14,16},{16,18},{18... | collective-permute-start | bytes 626696 | tf_op jit(solution)/shard_map/ppermute | solution.py:222
  7.8 1.5 %shard_map.123 = (f32[400,128]{1,0:T(8,128)S(1)}, f32[1,128]{1,0:T(1,128)S(1)}, bf16[400,640]{1,0:T(8,128)(2,1)S(1)}, bf16[400,640]{1,0:T(8,128)(2,1)S(1)}, bf16...) custom-call(s32[20,8,128]{2,1,0:T(8,128)S(1)} %get-tuple-element.102, ...), custom_call_target="tpu_custom_call", output_to_operand_aliasing={{0}: (9, {}), {1}: (10, {}), {2}: (11, {}), {3}: (12, {}), ... | custom-call | flops 1000000000 | bytes 1048576 | tf_op jit(solution)/shard_map/pallas_call | solution.py:208
  9.3 0.0 collective-permute-done.tail_in
  9.3 1.1 %shard_map.124 = (f32[408,128]{1,0:T(8,128)S(1)}, bf16[400,128]{1,0:T(8,128)(2,1)S(1)}, bf16[400,128]{1,0:T(8,128)(2,1)S(1)}, bf16[128,640]{1,0:T(8,128)(2,1)S(1)}, bf16[128,640]{1,0:T(8,128)(2,1)S(1)}) custom-call(f32[408,128]{1,0:T(8,128)S(1)} %collective-permute-done.tail_in, ...), custom_call_target="tpu_custom_call", output_to_operand_aliasing={{1}: (5, {}), {2}: (6, {}), {3}: (7, {}), {4}: (8, {})} | custom-call | flops 1000000000 | bytes 1048576 | tf_op jit(solution)/shard_map/pallas_call | solution.py:208
  10.4 1.6 %shard_map.125 = (f32[400,128]{1,0:T(8,128)S(1)}, f32[1,128]{1,0:T(1,128)S(1)}, bf16[400,640]{1,0:T(8,128)(2,1)S(1)}, bf16[400,640]{1,0:T(8,128)(2,1)S(1)}, bf16...) custom-call(s32[20,8,128]{2,1,0:T(8,128)S(1)} %get-tuple-element.102, ...), custom_call_target="tpu_custom_call", output_to_operand_aliasing={{0}: (9, {}), {1}: (10, {}), {2}: (11, {}), {3}: (12, {}), ... | custom-call | flops 1000000000 | bytes 1048576 | tf_op jit(solution)/shard_map/pallas_call | solution.py:208
  12.0 0.0 collective-permute-done.2.tail_in
  12.1 1.9 %collective-permute-start.3 = (f32[408,128]{1,0:T(8,128)S(1)}, f32[408,128]{1,0:T(8,128)S(1)}, u32[]{:S(2)}, u32[]{:S(2)}) collective-permute-start(f32[408,128]{1,0:T(8,128)S(1)} %get-tuple-element.148), channel_id=1, source_target_pairs={{0,2},{2,0},{4,6},{6,4},{8,10},{10,8},{12,14},{14,12},{16,18},{18,... | collective-permute-start | bytes 626696 | tf_op jit(solution)/shard_map/ppermute | solution.py:222
  14.0 1.8 %collective-permute-start.1 = (f32[408,128]{1,0:T(8,128)S(1)}, f32[408,128]{1,0:T(8,128)S(1)}, u32[]{:S(2)}, u32[]{:S(2)}) collective-permute-start(f32[408,128]{1,0:T(8,128)S(1)} %get-tuple-element.130), channel_id=1, source_target_pairs={{0,2},{2,4},{4,6},{6,8},{8,10},{10,12},{12,14},{14,16},{16,18},{18... | collective-permute-start | bytes 626696 | tf_op jit(solution)/shard_map/ppermute | solution.py:222
  15.8 0.0 collective-permute-done.3.tail_in
  15.8 1.0 %shard_map.128 = (f32[408,128]{1,0:T(8,128)S(1)}, bf16[400,128]{1,0:T(8,128)(2,1)S(1)}, bf16[400,128]{1,0:T(8,128)(2,1)S(1)}, bf16[128,640]{1,0:T(8,128)(2,1)S(1)}, bf16[128,640]{1,0:T(8,128)(2,1)S(1)}) custom-call(f32[408,128]{1,0:T(8,128)S(1)} %collective-permute-done.3.tail_in, ...), custom_call_target="tpu_custom_call", output_to_operand_aliasing={{1}: (5, {}), {2}: (6, {}), {3}: (7, {}), {4}: (8, {})} | custom-call | flops 1000000000 | bytes 1048576 | tf_op jit(solution)/shard_map/pallas_call | solution.py:208
  16.8 1.1 %shard_map.129 = (f32[400,128]{1,0:T(8,128)S(1)}, f32[1,128]{1,0:T(1,128)S(1)}, bf16[400,640]{1,0:T(8,128)(2,1)S(1)}, bf16[400,640]{1,0:T(8,128)(2,1)S(1)}, bf16...) custom-call(s32[20,8,128]{2,1,0:T(8,128)S(1)} %get-tuple-element.102, ...), custom_call_target="tpu_custom_call", output_to_operand_aliasing={{0}: (9, {}), {1}: (10, {}), {2}: (11, {}), {3}: (12, {}), ... | custom-call | flops 1000000000 | bytes 1048576 | tf_op jit(solution)/shard_map/pallas_call | solution.py:208
  18.0 0.6 %collective-permute-done.1.tail_in = f32[408,128]{1,0:T(8,128)S(1)} collective-permute-done((f32[408,128]{1,0:T(8,128)S(1)}, f32[408,128]{1,0:T(8,128)S(1)}, u32[]{:S(2)}, u32[]{:S(2)}) %collective-permute-start.1) | collective-permute-done | bytes 208928 | tf_op jit(solution)/shard_map/ppermute | solution.py:222
  18.5 4.3 %collective-permute-start.4 = (f32[408,128]{1,0:T(8,128)S(1)}, f32[408,128]{1,0:T(8,128)S(1)}, u32[]{:S(2)}, u32[]{:S(2)}) collective-permute-start(f32[408,128]{1,0:T(8,128)S(1)} %get-tuple-element.169), channel_id=1, source_target_pairs={{0,2},{2,0},{4,6},{6,4},{8,10},{10,8},{12,14},{14,12},{16,18},{18,... | collective-permute-start | bytes 626696 | tf_op jit(solution)/shard_map/ppermute | solution.py:222
  22.8 2.8 %collective-permute-start.5 = (f32[408,128]{1,0:T(8,128)S(1)}, f32[408,128]{1,0:T(8,128)S(1)}, u32[]{:S(2)}, u32[]{:S(2)}) collective-permute-start(f32[408,128]{1,0:T(8,128)S(1)} %get-tuple-element.184), channel_id=1, source_target_pairs={{0,2},{2,4},{4,6},{6,8},{8,10},{10,12},{12,14},{14,16},{16,18},{18... | collective-permute-start | bytes 626696 | tf_op jit(solution)/shard_map/ppermute | solution.py:222
  25.6 1.1 %shard_map.132 = (f32[408,128]{1,0:T(8,128)S(1)}, bf16[400,128]{1,0:T(8,128)(2,1)S(1)}, bf16[400,128]{1,0:T(8,128)(2,1)S(1)}, bf16[128,640]{1,0:T(8,128)(2,1)S(1)}, bf16[128,640]{1,0:T(8,128)(2,1)S(1)}) custom-call(f32[408,128]{1,0:T(8,128)S(1)} %collective-permute-done.4.tail_in, ...), custom_call_target="tpu_custom_call", output_to_operand_aliasing={{1}: (5, {}), {2}: (6, {}), {3}: (7, {}), {4}: (8, {})} | custom-call | flops 1000000000 | bytes 1048576 | tf_op jit(solution)/shard_map/pallas_call | solution.py:208
  26.7 0.1 collective-permute-start.7
  26.8 1.6 %collective-permute-done.5.tail_in = f32[408,128]{1,0:T(8,128)S(1)} collective-permute-done((f32[408,128]{1,0:T(8,128)S(1)}, f32[408,128]{1,0:T(8,128)S(1)}, u32[]{:S(2)}, u32[]{:S(2)}) %collective-permute-start.5) | collective-permute-done | bytes 208928 | tf_op jit(solution)/shard_map/ppermute | solution.py:222
  28.4 3.3 %collective-permute-start.6 = (f32[408,128]{1,0:T(8,128)S(1)}, f32[408,128]{1,0:T(8,128)S(1)}, u32[]{:S(2)}, u32[]{:S(2)}) collective-permute-start(f32[408,128]{1,0:T(8,128)S(1)} %get-tuple-element.193), channel_id=1, source_target_pairs={{0,250},{2,0},{4,254},{6,4},{8,2},{10,8},{12,6},{14,12},{16,10},{1... | collective-permute-start | bytes 626696 | tf_op jit(solution)/shard_map/ppermute | solution.py:222
  31.7 1.2 %shard_map.135 = (f32[400,128]{1,0:T(8,128)}, f32[1,128]{1,0:T(1,128)}) custom-call(f32[400,128]{1,0:T(8,128)S(1)} %get-tuple-element.181.head, f32[1,128]{1,0:T(1,128)S(1)} %get-tuple-element.182.hacc, bf16[400,640]{1,0:T(8,128)(2,1)S(1)} %get-tuple-element.183.rel_in, bf16[400,128]{1,0:T(8,128)(2,1)S(1)} %get-tuple-element.188.thi, ...), custom_call_target="tpu_custom_call" | custom-call | flops 1000000000 | bytes 1048576 | tf_op jit(solution)/shard_map/pallas_call | solution.py:208
  32.9 14.6 %collective-permute-done.6.packed = f32[408,128]{1,0:T(8,128)S(1)} collective-permute-done((f32[408,128]{1,0:T(8,128)S(1)}, f32[408,128]{1,0:T(8,128)S(1)}, u32[]{:S(2)}, u32[]{:S(2)}) %collective-permute-start.6) | collective-permute-done | bytes 208928 | tf_op jit(solution)/shard_map/ppermute | solution.py:222
  47.5 0.7 %shard_map.137 = (f32[400,128]{1,0:T(8,128)}, f32[1,128]{1,0:T(1,128)}) custom-call(f32[408,128]{1,0:T(8,128)S(1)} %collective-permute-done.6.packed, f32[400,128]{1,0:T(8,128)} %get-tuple-element.195.refs_0_, f32[1,128]{1,0:T(1,128)} %get-tuple-element.196.refs_1_), custom_call_target="tpu_custom_call", output_to_operand_aliasing={{0}: (1, {}), {1}: (2, {})} | custom-call | tf_op jit(solution)/shard_map/pallas_call | solution.py:275
  (10 shorter events, 0.1 us)
Async XLA Ops:
  4.4 4.9 %collective-permute-start = (f32[408,128]{1,0:T(8,128)S(1)}, f32[408,128]{1,0:T(8,128)S(1)}, u32[]{:S(2)}, u32[]{:S(2)}) collective-permute-start(f32[408,128]{1,0:T(8,128)S(1)} %get-tuple-element.119), channel_id=1, source_target_pairs={{0,2},{2,0},{4,6},{6,4},{8,10},{10,8},{12,14},{14,12},{16,18},{18,... | collective-permute-start | bytes 626696 | tf_op jit(solution)/shard_map/ppermute | solution.py:222
  5.1 6.9 %collective-permute-start.2 = (f32[408,128]{1,0:T(8,128)S(1)}, f32[408,128]{1,0:T(8,128)S(1)}, u32[]{:S(2)}, u32[]{:S(2)}) collective-permute-start(f32[408,128]{1,0:T(8,128)S(1)} %get-tuple-element.131), channel_id=1, source_target_pairs={{0,2},{2,4},{4,6},{6,8},{8,10},{10,12},{12,14},{14,16},{16,18},{18... | collective-permute-start | bytes 626696 | tf_op jit(solution)/shard_map/ppermute | solution.py:222
  12.1 3.7 %collective-permute-start.3 = (f32[408,128]{1,0:T(8,128)S(1)}, f32[408,128]{1,0:T(8,128)S(1)}, u32[]{:S(2)}, u32[]{:S(2)}) collective-permute-start(f32[408,128]{1,0:T(8,128)S(1)} %get-tuple-element.148), channel_id=1, source_target_pairs={{0,2},{2,0},{4,6},{6,4},{8,10},{10,8},{12,14},{14,12},{16,18},{18,... | collective-permute-start | bytes 626696 | tf_op jit(solution)/shard_map/ppermute | solution.py:222
  14.0 4.6 %collective-permute-start.1 = (f32[408,128]{1,0:T(8,128)S(1)}, f32[408,128]{1,0:T(8,128)S(1)}, u32[]{:S(2)}, u32[]{:S(2)}) collective-permute-start(f32[408,128]{1,0:T(8,128)S(1)} %get-tuple-element.130), channel_id=1, source_target_pairs={{0,2},{2,4},{4,6},{6,8},{8,10},{10,12},{12,14},{14,16},{16,18},{18... | collective-permute-start | bytes 626696 | tf_op jit(solution)/shard_map/ppermute | solution.py:222
  18.5 7.1 %collective-permute-start.4 = (f32[408,128]{1,0:T(8,128)S(1)}, f32[408,128]{1,0:T(8,128)S(1)}, u32[]{:S(2)}, u32[]{:S(2)}) collective-permute-start(f32[408,128]{1,0:T(8,128)S(1)} %get-tuple-element.169), channel_id=1, source_target_pairs={{0,2},{2,0},{4,6},{6,4},{8,10},{10,8},{12,14},{14,12},{16,18},{18,... | collective-permute-start | bytes 626696 | tf_op jit(solution)/shard_map/ppermute | solution.py:222
  22.8 5.5 %collective-permute-start.5 = (f32[408,128]{1,0:T(8,128)S(1)}, f32[408,128]{1,0:T(8,128)S(1)}, u32[]{:S(2)}, u32[]{:S(2)}) collective-permute-start(f32[408,128]{1,0:T(8,128)S(1)} %get-tuple-element.184), channel_id=1, source_target_pairs={{0,2},{2,4},{4,6},{6,8},{8,10},{10,12},{12,14},{14,16},{16,18},{18... | collective-permute-start | bytes 626696 | tf_op jit(solution)/shard_map/ppermute | solution.py:222
  26.7 6.2 %collective-permute-start.7 = (f32[408,128]{1,0:T(8,128)S(1)}, f32[408,128]{1,0:T(8,128)S(1)}, u32[]{:S(2)}, u32[]{:S(2)}) collective-permute-start(f32[408,128]{1,0:T(8,128)S(1)} %get-tuple-element.194), channel_id=1, source_target_pairs={{0,2},{2,252},{4,6},{6,0},{8,10},{10,4},{12,14},{14,8},{16,18},{18... | collective-permute-start | bytes 626696 | tf_op jit(solution)/shard_map/ppermute | solution.py:222
  28.4 19.2 %collective-permute-start.6 = (f32[408,128]{1,0:T(8,128)S(1)}, f32[408,128]{1,0:T(8,128)S(1)}, u32[]{:S(2)}, u32[]{:S(2)}) collective-permute-start(f32[408,128]{1,0:T(8,128)S(1)} %get-tuple-element.193), channel_id=1, source_target_pairs={{0,250},{2,0},{4,254},{6,4},{8,2},{10,8},{12,6},{14,12},{16,10},{1... | collective-permute-start | bytes 626696 | tf_op jit(solution)/shard_map/ppermute | solution.py:222

commit v9 on v8

--- a/solution.py
+++ b/solution.py
@@ -10,6 +10,7 @@
 LEARN_RATE = 0.1
 F32, BF16, I32 = jnp.float32, jnp.bfloat16, jnp.int32
 LANES = 128
+TAIL_GROUPS = ((0, 1), (1, 5))
 ODD, EVEN = 1, 0
 VMEM = pl.BlockSpec(memory_space=pltpu.VMEM)
 SMEM = pl.BlockSpec(memory_space=pltpu.SMEM)
@@ -91,13 +92,19 @@
     shi, slo = shi_ref[...], slo_ref[...]
     both = dot(jnp.concatenate([thi, tlo], axis=1), shi, TN)
     scores = both[:LANES] + both[LANES:] + dot(thi, slo, TN)
-    for s in range(tasks):
-        score = scores[:, s * LANES : (s + 1) * LANES]
-        coefficient = gain_ref[gain_row + s, 0:1, :] * jnp.tanh(0.5 * score) + labels_ref[label_row + s]
-        chi_ref[:, cols(s)], clo_ref[:, cols(s)] = hi_lo(coefficient)
-    chi, clo = chi_ref[...], clo_ref[...]
-    both = dot(shi, jnp.concatenate([chi, clo], axis=0), NT)
-    grad = both[:, :LANES] + both[:, LANES:] + dot(slo, chi, NT)
+    grad = None
+    for first, stop in TAIL_GROUPS:
+        stop = min(stop, tasks)
+        parts = []
+        for s in range(first, stop):
+            score = scores[:, s * LANES : (s + 1) * LANES]
+            parts.append(hi_lo(gain_ref[gain_row + s, 0:1, :] * jnp.tanh(0.5 * score) + labels_ref[label_row + s]))
+        span = pl.ds(first * LANES, (stop - first) * LANES)
+        chi, clo = (jnp.concatenate(part, axis=1) if len(part) > 1 else part[0] for part in zip(*parts))
+        chi_ref[:, span], clo_ref[:, span] = chi, clo
+        both = dot(shi_ref[:, span], jnp.concatenate([chi, clo], axis=0), NT)
+        term = both[:, :LANES] + both[:, LANES:] + dot(slo_ref[:, span], chi, NT)
+        grad = term if grad is None else grad + term
     tail, state = adagrad(tail, state, grad)
     tail_out[pl.ds(0, width), :] = tail
     tail_out[pl.ds(width, 8), :] = jnp.broadcast_to(state, (8, LANES))
@@ -194,7 +201,11 @@
         @pl.when(role() == mine)
         def _():
             row[...] = packed[pl.ds(width, 1), :]
-            copies = [pltpu.make_async_copy(packed.at[pl.ds(0, width)], tail_out, sem.at[0]), pltpu.make_async_copy(row, tacc_out, sem.at[1])]
+            part = width // 5
+            copies = [pltpu.make_async_copy(row, tacc_out, sem.at[5])]
+            for i in range(5):
+                rows = pl.ds(i * part, part)
+                copies.append(pltpu.make_async_copy(packed.at[rows], tail_out.at[rows], sem.at[i]))
             for copy in copies:
                 copy.start()
             for copy in copies:
@@ -277,7 +288,7 @@
             in_specs=[VMEM] + [HBM] * len(results),
             out_specs=[HBM] * 2,
             out_shape=[pltpu.HBM(*block), pltpu.HBM(*row)],
-            scratch_shapes=[pltpu.VMEM(*row), pltpu.SemaphoreType.DMA((2,))],
+            scratch_shapes=[pltpu.VMEM(*row), pltpu.SemaphoreType.DMA((6,))],
             input_output_aliases={1 + i: i for i in range(len(results))},
             compiler_params=pltpu.CompilerParams(vmem_limit_bytes=16 << 20),
         )(packed_in, *results)

time: 48.5 us -> 48.3 us (level)
  no operation moved by 1% of the time
where the time goes in v9:
time: 48.3 us; the launch traced here: 48.1 us
  starting transfers between devices  17.5 us (36%)
  waiting for transfers between devices  16.9 us (35%)
  Pallas kernels  12.8 us (27%)
  between operations  0.94 us (2%)
    ppermute x8, starting transfers between devices, send_or_swap(): lax.ppermute(block, 'blk', [(i, (i + distance) % n if i % 2 == mine else...  17.5 us
    ppermute x8, waiting for transfers between devices, send_or_swap(): lax.ppermute(block, 'blk', [(i, (i + distance) % n if i % 2 == mine else...  16.9 us
    pallas_call x16, Pallas kernels, call(): pl.pallas_call(body, in_specs=ins, out_specs=[VMEM] * len(outs), out_shap...  12.1 us
  transfers between devices with their start and end apart: 8, of which 3 were waited for; matrix products, arithmetic and copies ran while one was open for 0% of the time, Pallas kernels for 18%

profile of v9, /device:TPU:121, one launch (start us, length us, event | category | flops | bytes accessed | tf_op | source)
XLA Modules:
  0.0 48.1 jit_solution(17068487658253238852)
XLA Ops:
  0.6 2.6 %shard_map.120 = (f32[408,128]{1,0:T(8,128)S(1)}, bf16[400,128]{1,0:T(8,128)(2,1)S(1)}, bf16[400,128]{1,0:T(8,128)(2,1)S(1)}, bf16[128,640]{1,0:T(8,128)(2,1)S(1...) custom-call(s32[1,4]{1,0:T(1,128)} %bitcast.19, ...), custom_call_target="tpu_custom_call" | custom-call | flops 1000000000 | bytes 1048576 | tf_op jit(solution)/shard_map/pallas_call | solution.py:219
  3.3 1.0 %shard_map.121 = (f32[408,128]{1,0:T(8,128)S(1)}, bf16[400,128]{1,0:T(8,128)(2,1)S(1)}, bf16[400,128]{1,0:T(8,128)(2,1)S(1)}, bf16[128,640]{1,0:T(8,128)(2,1)S(1)}, bf16[128,640]{1,0:T(8,128)(2,1)S(1)}) custom-call(f32[408,128]{1,0:T(8,128)S(1)} %get-tuple-element.107.tail_in, ...), custom_call_target="tpu_custom_call", output_to_operand_aliasing={{1}: (5, {}), {2}: (6, {}), {3}: (7, {}), {4}: (8, {})} | custom-call | flops 1000000000 | bytes 1048576 | tf_op jit(solution)/shard_map/pallas_call | solution.py:219
  4.3 0.7 %collective-permute-start = (f32[408,128]{1,0:T(8,128)S(1)}, f32[408,128]{1,0:T(8,128)S(1)}, u32[]{:S(2)}, u32[]{:S(2)}) collective-permute-start(f32[408,128]{1,0:T(8,128)S(1)} %get-tuple-element.119), channel_id=1, source_target_pairs={{0,2},{2,0},{4,6},{6,4},{8,10},{10,8},{12,14},{14,12},{16,18},{18,... | collective-permute-start | bytes 626696 | tf_op jit(solution)/shard_map/ppermute | solution.py:233
  5.0 2.7 %collective-permute-start.2 = (f32[408,128]{1,0:T(8,128)S(1)}, f32[408,128]{1,0:T(8,128)S(1)}, u32[]{:S(2)}, u32[]{:S(2)}) collective-permute-start(f32[408,128]{1,0:T(8,128)S(1)} %get-tuple-element.131), channel_id=1, source_target_pairs={{0,2},{2,4},{4,6},{6,8},{8,10},{10,12},{12,14},{14,16},{16,18},{18... | collective-permute-start | bytes 626696 | tf_op jit(solution)/shard_map/ppermute | solution.py:233
  7.7 1.5 %shard_map.123 = (f32[400,128]{1,0:T(8,128)S(1)}, f32[1,128]{1,0:T(1,128)S(1)}, bf16[400,640]{1,0:T(8,128)(2,1)S(1)}, bf16[400,640]{1,0:T(8,128)(2,1)S(1)}, bf16...) custom-call(s32[20,8,128]{2,1,0:T(8,128)S(1)} %get-tuple-element.102, ...), custom_call_target="tpu_custom_call", output_to_operand_aliasing={{0}: (9, {}), {1}: (10, {}), {2}: (11, {}), {3}: (12, {}), ... | custom-call | flops 1000000000 | bytes 1048576 | tf_op jit(solution)/shard_map/pallas_call | solution.py:219
  9.2 0.0 collective-permute-done.tail_in
  9.2 1.0 %shard_map.124 = (f32[408,128]{1,0:T(8,128)S(1)}, bf16[400,128]{1,0:T(8,128)(2,1)S(1)}, bf16[400,128]{1,0:T(8,128)(2,1)S(1)}, bf16[128,640]{1,0:T(8,128)(2,1)S(1)}, bf16[128,640]{1,0:T(8,128)(2,1)S(1)}) custom-call(f32[408,128]{1,0:T(8,128)S(1)} %collective-permute-done.tail_in, ...), custom_call_target="tpu_custom_call", output_to_operand_aliasing={{1}: (5, {}), {2}: (6, {}), {3}: (7, {}), {4}: (8, {})} | custom-call | flops 1000000000 | bytes 1048576 | tf_op jit(solution)/shard_map/pallas_call | solution.py:219
  10.2 1.6 %shard_map.125 = (f32[400,128]{1,0:T(8,128)S(1)}, f32[1,128]{1,0:T(1,128)S(1)}, bf16[400,640]{1,0:T(8,128)(2,1)S(1)}, bf16[400,640]{1,0:T(8,128)(2,1)S(1)}, bf16...) custom-call(s32[20,8,128]{2,1,0:T(8,128)S(1)} %get-tuple-element.102, ...), custom_call_target="tpu_custom_call", output_to_operand_aliasing={{0}: (9, {}), {1}: (10, {}), {2}: (11, {}), {3}: (12, {}), ... | custom-call | flops 1000000000 | bytes 1048576 | tf_op jit(solution)/shard_map/pallas_call | solution.py:219
  11.9 0.0 collective-permute-done.2.tail_in
  11.9 1.9 %collective-permute-start.3 = (f32[408,128]{1,0:T(8,128)S(1)}, f32[408,128]{1,0:T(8,128)S(1)}, u32[]{:S(2)}, u32[]{:S(2)}) collective-permute-start(f32[408,128]{1,0:T(8,128)S(1)} %get-tuple-element.148), channel_id=1, source_target_pairs={{0,2},{2,0},{4,6},{6,4},{8,10},{10,8},{12,14},{14,12},{16,18},{18,... | collective-permute-start | bytes 626696 | tf_op jit(solution)/shard_map/ppermute | solution.py:233
  13.8 1.8 %collective-permute-start.1 = (f32[408,128]{1,0:T(8,128)S(1)}, f32[408,128]{1,0:T(8,128)S(1)}, u32[]{:S(2)}, u32[]{:S(2)}) collective-permute-start(f32[408,128]{1,0:T(8,128)S(1)} %get-tuple-element.130), channel_id=1, source_target_pairs={{0,2},{2,4},{4,6},{6,8},{8,10},{10,12},{12,14},{14,16},{16,18},{18... | collective-permute-start | bytes 626696 | tf_op jit(solution)/shard_map/ppermute | solution.py:233
  15.6 1.0 %shard_map.128 = (f32[408,128]{1,0:T(8,128)S(1)}, bf16[400,128]{1,0:T(8,128)(2,1)S(1)}, bf16[400,128]{1,0:T(8,128)(2,1)S(1)}, bf16[128,640]{1,0:T(8,128)(2,1)S(1)}, bf16[128,640]{1,0:T(8,128)(2,1)S(1)}) custom-call(f32[408,128]{1,0:T(8,128)S(1)} %collective-permute-done.3.tail_in, ...), custom_call_target="tpu_custom_call", output_to_operand_aliasing={{1}: (5, {}), {2}: (6, {}), {3}: (7, {}), {4}: (8, {})} | custom-call | flops 1000000000 | bytes 1048576 | tf_op jit(solution)/shard_map/pallas_call | solution.py:219
  16.6 1.1 %shard_map.129 = (f32[400,128]{1,0:T(8,128)S(1)}, f32[1,128]{1,0:T(1,128)S(1)}, bf16[400,640]{1,0:T(8,128)(2,1)S(1)}, bf16[400,640]{1,0:T(8,128)(2,1)S(1)}, bf16...) custom-call(s32[20,8,128]{2,1,0:T(8,128)S(1)} %get-tuple-element.102, ...), custom_call_target="tpu_custom_call", output_to_operand_aliasing={{0}: (9, {}), {1}: (10, {}), {2}: (11, {}), {3}: (12, {}), ... | custom-call | flops 1000000000 | bytes 1048576 | tf_op jit(solution)/shard_map/pallas_call | solution.py:219
  17.8 0.6 %collective-permute-done.1.tail_in = f32[408,128]{1,0:T(8,128)S(1)} collective-permute-done((f32[408,128]{1,0:T(8,128)S(1)}, f32[408,128]{1,0:T(8,128)S(1)}, u32[]{:S(2)}, u32[]{:S(2)}) %collective-permute-start.1) | collective-permute-done | bytes 208928 | tf_op jit(solution)/shard_map/ppermute | solution.py:233
  18.4 4.2 %collective-permute-start.4 = (f32[408,128]{1,0:T(8,128)S(1)}, f32[408,128]{1,0:T(8,128)S(1)}, u32[]{:S(2)}, u32[]{:S(2)}) collective-permute-start(f32[408,128]{1,0:T(8,128)S(1)} %get-tuple-element.169), channel_id=1, source_target_pairs={{0,2},{2,0},{4,6},{6,4},{8,10},{10,8},{12,14},{14,12},{16,18},{18,... | collective-permute-start | bytes 626696 | tf_op jit(solution)/shard_map/ppermute | solution.py:233
  22.6 2.9 %collective-permute-start.5 = (f32[408,128]{1,0:T(8,128)S(1)}, f32[408,128]{1,0:T(8,128)S(1)}, u32[]{:S(2)}, u32[]{:S(2)}) collective-permute-start(f32[408,128]{1,0:T(8,128)S(1)} %get-tuple-element.184), channel_id=1, source_target_pairs={{0,2},{2,4},{4,6},{6,8},{8,10},{10,12},{12,14},{14,16},{16,18},{18... | collective-permute-start | bytes 626696 | tf_op jit(solution)/shard_map/ppermute | solution.py:233
  25.5 1.0 %shard_map.132 = (f32[408,128]{1,0:T(8,128)S(1)}, bf16[400,128]{1,0:T(8,128)(2,1)S(1)}, bf16[400,128]{1,0:T(8,128)(2,1)S(1)}, bf16[128,640]{1,0:T(8,128)(2,1)S(1)}, bf16[128,640]{1,0:T(8,128)(2,1)S(1)}) custom-call(f32[408,128]{1,0:T(8,128)S(1)} %collective-permute-done.4.tail_in, ...), custom_call_target="tpu_custom_call", output_to_operand_aliasing={{1}: (5, {}), {2}: (6, {}), {3}: (7, {}), {4}: (8, {})} | custom-call | flops 1000000000 | bytes 1048576 | tf_op jit(solution)/shard_map/pallas_call | solution.py:219
  26.4 0.1 collective-permute-start.7
  26.6 1.6 %collective-permute-done.5.tail_in = f32[408,128]{1,0:T(8,128)S(1)} collective-permute-done((f32[408,128]{1,0:T(8,128)S(1)}, f32[408,128]{1,0:T(8,128)S(1)}, u32[]{:S(2)}, u32[]{:S(2)}) %collective-permute-start.5) | collective-permute-done | bytes 208928 | tf_op jit(solution)/shard_map/ppermute | solution.py:233
  28.2 3.2 %collective-permute-start.6 = (f32[408,128]{1,0:T(8,128)S(1)}, f32[408,128]{1,0:T(8,128)S(1)}, u32[]{:S(2)}, u32[]{:S(2)}) collective-permute-start(f32[408,128]{1,0:T(8,128)S(1)} %get-tuple-element.193), channel_id=1, source_target_pairs={{0,250},{2,0},{4,254},{6,4},{8,2},{10,8},{12,6},{14,12},{16,10},{1... | collective-permute-start | bytes 626696 | tf_op jit(solution)/shard_map/ppermute | solution.py:233
  31.4 1.2 %shard_map.135 = (f32[400,128]{1,0:T(8,128)}, f32[1,128]{1,0:T(1,128)}) custom-call(f32[400,128]{1,0:T(8,128)S(1)} %get-tuple-element.181.head, f32[1,128]{1,0:T(1,128)S(1)} %get-tuple-element.182.hacc, bf16[400,640]{1,0:T(8,128)(2,1)S(1)} %get-tuple-element.183.rel_in, bf16[400,128]{1,0:T(8,128)(2,1)S(1)} %get-tuple-element.188.thi, ...), custom_call_target="tpu_custom_call" | custom-call | flops 1000000000 | bytes 1048576 | tf_op jit(solution)/shard_map/pallas_call | solution.py:219
  32.6 0.1 shard_map.136
  32.7 14.6 %collective-permute-done.6.packed = f32[408,128]{1,0:T(8,128)S(1)} collective-permute-done((f32[408,128]{1,0:T(8,128)S(1)}, f32[408,128]{1,0:T(8,128)S(1)}, u32[]{:S(2)}, u32[]{:S(2)}) %collective-permute-start.6) | collective-permute-done | bytes 208928 | tf_op jit(solution)/shard_map/ppermute | solution.py:233
  47.2 0.7 %shard_map.137 = (f32[400,128]{1,0:T(8,128)}, f32[1,128]{1,0:T(1,128)}) custom-call(f32[408,128]{1,0:T(8,128)S(1)} %collective-permute-done.6.packed, f32[400,128]{1,0:T(8,128)} %get-tuple-element.195.refs_0_, f32[1,128]{1,0:T(1,128)} %get-tuple-element.196.refs_1_), custom_call_target="tpu_custom_call", output_to_operand_aliasing={{0}: (1, {}), {1}: (2, {})} | custom-call | tf_op jit(solution)/shard_map/pallas_call | solution.py:286
  (10 shorter events, 0.1 us)
Async XLA Ops:
  4.3 4.9 %collective-permute-start = (f32[408,128]{1,0:T(8,128)S(1)}, f32[408,128]{1,0:T(8,128)S(1)}, u32[]{:S(2)}, u32[]{:S(2)}) collective-permute-start(f32[408,128]{1,0:T(8,128)S(1)} %get-tuple-element.119), channel_id=1, source_target_pairs={{0,2},{2,0},{4,6},{6,4},{8,10},{10,8},{12,14},{14,12},{16,18},{18,... | collective-permute-start | bytes 626696 | tf_op jit(solution)/shard_map/ppermute | solution.py:233
  5.0 6.9 %collective-permute-start.2 = (f32[408,128]{1,0:T(8,128)S(1)}, f32[408,128]{1,0:T(8,128)S(1)}, u32[]{:S(2)}, u32[]{:S(2)}) collective-permute-start(f32[408,128]{1,0:T(8,128)S(1)} %get-tuple-element.131), channel_id=1, source_target_pairs={{0,2},{2,4},{4,6},{6,8},{8,10},{10,12},{12,14},{14,16},{16,18},{18... | collective-permute-start | bytes 626696 | tf_op jit(solution)/shard_map/ppermute | solution.py:233
  11.9 3.7 %collective-permute-start.3 = (f32[408,128]{1,0:T(8,128)S(1)}, f32[408,128]{1,0:T(8,128)S(1)}, u32[]{:S(2)}, u32[]{:S(2)}) collective-permute-start(f32[408,128]{1,0:T(8,128)S(1)} %get-tuple-element.148), channel_id=1, source_target_pairs={{0,2},{2,0},{4,6},{6,4},{8,10},{10,8},{12,14},{14,12},{16,18},{18,... | collective-permute-start | bytes 626696 | tf_op jit(solution)/shard_map/ppermute | solution.py:233
  13.8 4.6 %collective-permute-start.1 = (f32[408,128]{1,0:T(8,128)S(1)}, f32[408,128]{1,0:T(8,128)S(1)}, u32[]{:S(2)}, u32[]{:S(2)}) collective-permute-start(f32[408,128]{1,0:T(8,128)S(1)} %get-tuple-element.130), channel_id=1, source_target_pairs={{0,2},{2,4},{4,6},{6,8},{8,10},{10,12},{12,14},{14,16},{16,18},{18... | collective-permute-start | bytes 626696 | tf_op jit(solution)/shard_map/ppermute | solution.py:233
  18.4 7.1 %collective-permute-start.4 = (f32[408,128]{1,0:T(8,128)S(1)}, f32[408,128]{1,0:T(8,128)S(1)}, u32[]{:S(2)}, u32[]{:S(2)}) collective-permute-start(f32[408,128]{1,0:T(8,128)S(1)} %get-tuple-element.169), channel_id=1, source_target_pairs={{0,2},{2,0},{4,6},{6,4},{8,10},{10,8},{12,14},{14,12},{16,18},{18,... | collective-permute-start | bytes 626696 | tf_op jit(solution)/shard_map/ppermute | solution.py:233
  22.6 5.6 %collective-permute-start.5 = (f32[408,128]{1,0:T(8,128)S(1)}, f32[408,128]{1,0:T(8,128)S(1)}, u32[]{:S(2)}, u32[]{:S(2)}) collective-permute-start(f32[408,128]{1,0:T(8,128)S(1)} %get-tuple-element.184), channel_id=1, source_target_pairs={{0,2},{2,4},{4,6},{6,8},{8,10},{10,12},{12,14},{14,16},{16,18},{18... | collective-permute-start | bytes 626696 | tf_op jit(solution)/shard_map/ppermute | solution.py:233
  26.4 6.2 %collective-permute-start.7 = (f32[408,128]{1,0:T(8,128)S(1)}, f32[408,128]{1,0:T(8,128)S(1)}, u32[]{:S(2)}, u32[]{:S(2)}) collective-permute-start(f32[408,128]{1,0:T(8,128)S(1)} %get-tuple-element.194), channel_id=1, source_target_pairs={{0,2},{2,252},{4,6},{6,0},{8,10},{10,4},{12,14},{14,8},{16,18},{18... | collective-permute-start | bytes 626696 | tf_op jit(solution)/shard_map/ppermute | solution.py:233
  28.2 19.0 %collective-permute-start.6 = (f32[408,128]{1,0:T(8,128)S(1)}, f32[408,128]{1,0:T(8,128)S(1)}, u32[]{:S(2)}, u32[]{:S(2)}) collective-permute-start(f32[408,128]{1,0:T(8,128)S(1)} %get-tuple-element.193), channel_id=1, source_target_pairs={{0,250},{2,0},{4,254},{6,4},{8,2},{10,8},{12,6},{14,12},{16,10},{1... | collective-permute-start | bytes 626696 | tf_op jit(solution)/shard_map/ppermute | solution.py:233
